TPU v7x, 256 devices: a whole 4x4x8 slice. The times are simulated.
256 devices in a mesh: dp: 32 (over x, y, core), ctx: 8 (over z).
Axes of the slice: x: 4, y: 4, z: 8, core: 2. Of those that a mesh axis runs over, the one named last changes fastest.
Arguments:
- cotangent: bfloat16 [32, 4096, 8192], P('dp', 'ctx'), may hold values from -6 to 6
- out_weight: bfloat16 [256, 8192], P(None, 'ctx'), may hold values from -0.0625 to 0.0625
- head_input: bfloat16 [32, 4096, 256], P('dp', 'ctx'), may hold values from -6 to 6
- injector: bfloat16 [32, 4096, 128], P('dp', 'ctx'), may hold values from -0.59765625 to 0.59765625
- readout: bfloat16 [32, 4096, 128], P('dp', 'ctx'), may hold values from -0.59765625 to 0.59765625
- decay_code: int32 [32, 4096, 2], P('dp', 'ctx'), may hold values from 1 to 40960
- decay_rate: float32 [2], replicated, may hold values from 4.8828125e-06 to 0.0061035156
- start_state: float32 [32, 8, 2, 128, 128], P('dp', 'ctx'), may hold values from -6 to 6
Outputs:
- gradient_input: bfloat16 [32, 4096, 256], P('dp', 'ctx')
- gradient_injector: float32 [32, 4096, 128], P('dp', 'ctx')
- gradient_readout: float32 [32, 4096, 128], P('dp', 'ctx')
- gradient_weight: float32 [256, 8192], P('ctx', 'dp')
- gradient_rate: float32 [2], replicated
All inputs are finite; a program needn't handle non-finite values.
Results may differ from a plain program's by a relative error of at most 0.0049.
Values may be sent and summed in bfloat16 or wider, within the bound.
No kernel may reach another device: no remote copies, remote signals or barrier semaphores. Data moves between devices by JAX's collectives and lax.ppermute only.
A program may use at most 128 MiB of HBM per device.

v0:
```python
import jax
import jax.numpy as jnp
from jax import lax
from jax.sharding import PartitionSpec as P

precise = lax.Precision.HIGHEST


def carried_in(value, axis, join, neutral):
    count, mine = (lax.axis_size(axis), lax.axis_index(axis))
    pieces = jax.tree.map(lambda part: lax.all_gather(part, axis), value)
    pieces = jax.tree.map(lambda part: part[::-1], pieces)
    mine = count - 1 - mine
    total = jax.tree.map(
        lambda part, zero: jnp.full_like(part, 0) + jnp.asarray(zero, part.dtype), value, neutral
    )

    def lap(position, total):
        longer = join(total, jax.tree.map(lambda part: part[position], pieces))
        return jax.tree.map(lambda new, old: jnp.where(position < mine, new, old), longer, total)

    return lax.fori_loop(0, count - 1, lap, total)


def decay_table(log_decay):
    cumulative = jnp.cumsum(log_decay, axis=0)
    length = log_decay.shape[0]
    row_index = lax.broadcasted_iota(jnp.int32, (length, length), 0)
    col_index = lax.broadcasted_iota(jnp.int32, (length, length), 1)
    causal = (row_index >= col_index)[None]
    spread = cumulative.T[:, :, None] - cumulative.T[:, None, :]
    weights = jnp.where(causal, jnp.exp(jnp.where(causal, spread, 0.0)), 0.0)
    return (cumulative, weights)


def forward_shard(head_input, injector, readout, log_decay, start_state):
    length, heads_count = log_decay.shape
    cumulative, weights = decay_table(log_decay)
    intersection = jnp.dot(readout, injector.T, preferred_element_type=jnp.float32)
    mixing = intersection[None] * weights
    inputs_heads = head_input.reshape(length, heads_count, -1).astype(jnp.float32)
    within = jnp.einsum("hts,shp->thp", mixing, inputs_heads, precision=precise)
    carried = jnp.einsum("tn,hpn->thp", readout.astype(jnp.float32), start_state, precision=precise)
    outputs = within + jnp.exp(cumulative)[:, :, None] * carried
    return outputs.reshape(length, -1).astype(jnp.bfloat16)


def chain_piece(readout, output_grad, log_decay):
    length, heads_count = log_decay.shape
    cumulative = jnp.cumsum(log_decay, axis=0)
    grad_heads = output_grad.reshape(length, heads_count, -1).astype(jnp.float32)
    scaled = jnp.exp(cumulative)[:, :, None] * readout.astype(jnp.float32)[:, None, :]
    adjoint = jnp.einsum("thp,thn->hpn", grad_heads, scaled, precision=precise)
    return (jnp.exp(cumulative[-1]), adjoint)


def backward_shard(head_input, injector, readout, output_grad, log_decay, start_state, incoming):
    length, heads_count = log_decay.shape
    cumulative, weights = decay_table(log_decay)
    inputs_narrow = head_input.reshape(length, heads_count, -1)
    grad_narrow = output_grad.reshape(length, heads_count, -1)
    inputs_heads = inputs_narrow.astype(jnp.float32)
    grad_heads = grad_narrow.astype(jnp.float32)
    inject_float = injector.astype(jnp.float32)
    read_float = readout.astype(jnp.float32)
    intersection = jnp.dot(readout, injector.T, preferred_element_type=jnp.float32)
    mixing = intersection[None] * weights
    to_end = jnp.exp(cumulative[-1][None, :] - cumulative)
    from_start = jnp.exp(cumulative)
    entering = jnp.einsum("sn,hpn->shp", inject_float, incoming, precision=precise)
    grad_input = (
        jnp.einsum("hts,thp->shp", mixing, grad_heads, precision=precise)
        + to_end[:, :, None] * entering
    )
    pairing = (
        jnp.einsum("thp,shp->hts", grad_narrow, inputs_narrow, preferred_element_type=jnp.float32)
        * weights
    )
    through_start = jnp.einsum("thp,hpn->thn", grad_heads, start_state, precision=precise)
    grad_read = jnp.einsum("hts,sn->tn", pairing, inject_float, precision=precise)
    grad_read = grad_read + jnp.einsum("th,thn->tn", from_start, through_start, precision=precise)
    input_state = jnp.einsum("shp,hpn->shn", inputs_heads, incoming, precision=precise)
    grad_inject = jnp.einsum("hts,tn->sn", pairing, read_float, precision=precise)
    grad_inject = grad_inject + jnp.einsum("sh,shn->sn", to_end, input_state, precision=precise)
    products = intersection[None] * pairing
    carried = (
        jnp.einsum("tn,hpn->thp", read_float, start_state, precision=precise)
        * from_start[:, :, None]
    )
    reaching = to_end * jnp.einsum("shn,sn->sh", input_state, inject_float, precision=precise)
    end_term = from_start[-1] * jnp.einsum(
        "hpn,hpn->h", incoming, start_state, precision=precise
    ) + jnp.sum(reaching, axis=0)
    cumul_grad = jnp.sum(products, axis=2).T - jnp.sum(products, axis=1).T
    cumul_grad = cumul_grad + jnp.sum(grad_heads * carried, axis=2) - reaching
    is_last = lax.broadcasted_iota(jnp.int32, (length, 1), 0) == length - 1
    cumul_grad = cumul_grad + jnp.where(is_last, end_term[None, :], 0.0)
    decay_grad = jnp.flip(jnp.cumsum(jnp.flip(cumul_grad, 0), axis=0), 0)
    rate_terms = jnp.sum(decay_grad * log_decay, axis=0)
    return (grad_input.reshape(length, -1).astype(jnp.bfloat16), grad_inject, grad_read, rate_terms)


def combine(earlier, later):
    return (later[0] * earlier[0], later[1] + later[0][:, None, None] * earlier[1])


def local(
    cotangent, out_weight, head_input, injector, readout, decay_code, decay_rate, start_state
):
    grad_out = cotangent[0]
    inputs_local = head_input[0]
    inject_local = injector[0]
    read_local = readout[0]
    state_local = start_state[0, 0]
    length = grad_out.shape[0]
    output_grad = lax.dot_general(
        grad_out,
        lax.all_gather(out_weight, "ctx", axis=1, tiled=True),
        (((1,), (1,)), ((), ())),
        preferred_element_type=jnp.float32,
    ).astype(jnp.bfloat16)
    log_decay = -decay_rate[None, :] * decay_code[0].astype(jnp.float32)
    decay_total, adjoint = chain_piece(read_local, output_grad, log_decay)
    identity = (jnp.ones_like(decay_total), jnp.zeros_like(adjoint))
    incoming = carried_in((decay_total, adjoint), "ctx", combine, identity)[1]
    outputs = forward_shard(inputs_local, inject_local, read_local, log_decay, state_local)
    local_weight = lax.dot_general(
        outputs, grad_out, (((0,), (0,)), ((), ())), preferred_element_type=jnp.float32
    )
    data_part = lax.psum_scatter(local_weight, "dp", scatter_dimension=1, tiled=True)
    weight_part = lax.psum_scatter(data_part, "ctx", scatter_dimension=0, tiled=True)
    grad_input, grad_inject, grad_read, rate_terms = backward_shard(
        inputs_local, inject_local, read_local, output_grad, log_decay, state_local, incoming
    )
    tokens_all = length * lax.axis_size("dp") * lax.axis_size("ctx")
    rate_sum = lax.psum(rate_terms, ("dp", "ctx"))
    return (
        grad_input[None],
        grad_inject[None],
        grad_read[None],
        weight_part,
        rate_sum / tokens_all,
    )


def solution(mesh):
    in_specs = (
        P("dp", "ctx", None),
        P(None, "ctx"),
        P("dp", "ctx", None),
        P("dp", "ctx", None),
        P("dp", "ctx", None),
        P("dp", "ctx", None),
        P(),
        P("dp", "ctx", None, None, None),
    )
    out_specs = (
        P("dp", "ctx", None),
        P("dp", "ctx", None),
        P("dp", "ctx", None),
        P("ctx", "dp"),
        P(),
    )
    return jax.shard_map(local, mesh=mesh, in_specs=in_specs, out_specs=out_specs, check_vma=False)
```

profile of v0, /device:TPU:2, one launch (start us, length us, event | category | flops | bytes accessed | tf_op | source)
XLA Modules:
  0.0 262.4 jit_solution(3269358175071123547)
XLA Ops:
  7.2 0.7 all-gather.5.cloned.1.call-update
  7.9 0.0 all-gather.7.cloned.1.call-start
  7.9 0.7 neg.4
  8.6 0.8 fusion.61
  9.4 0.6 reduce-window.14
  10.0 0.2 slice_reduce_fusion.1
  10.1 0.2 reduce-window.15
  10.3 0.9 bitcast_convert_fusion.1
  11.3 0.1 copy.52
  11.4 0.1 add_bitcast_fusion.1
  11.5 56.1 %all-gather.5.cloned.1.call-done = bf16[256,8192]{1,0:T(8,128)(2,1)} async-done(((bf16[256,1024]{1,0:T(8,128)(2,1)}), bf16[256,8192]{1,0:T(8,128)(2,1)}) %all-gather.5.cloned.1.call-update) | async-done | bytes 4194320 | tf_op jit(solution)/shard_map/all_gather | solution.py:118
  67.6 6.9 %fusion.26 = bf16[512,256]{0,1:T(8,128)(2,1)S(1)} fusion(bf16[256,8192]{1,0:T(8,128)(2,1)} %all-gather.5.cloned.1.call-done, bf16[1,512,8192]{2,1,0:T(8,128)(2,1)} %param.10), kind=kOutput, calls=%fused_computation.24 | convolution fusion | flops 2147614720 | bytes 12845056 | tf_op jit(solution)/shard_map/dot_general | solution.py:116
  74.6 1.1 fusion.43
  75.7 0.0 reduce-scatter.3.cloned.1.call-start
  75.7 0.1 copy.91
  75.9 0.1 iota_compare_fusion
  76.0 0.3 fusion.55
  76.3 0.4 multiply_reduce_fusion.2
  76.8 2.0 fusion.22
  78.7 9.1 %fusion.1 = f32[256,8192]{1,0:T(8,128)} fusion(bf16[512,256]{0,1:T(8,128)(2,1)S(1)} %bitcast.164, bf16[1,512,8192]{2,1,0:T(8,128)(2,1)} %param.10), kind=kOutput, calls=%fused_computation.3 | convolution fusion | flops 2147483648 | bytes 17039360 | tf_op jit(solution)/shard_map/dot_general | solution.py:127
  87.8 0.0 reduce-scatter.5.cloned.1.call-start
  87.9 0.2 slice_reduce_fusion.3
  88.0 14.7 %all-gather.1 = f32[8,1,2]{2,1,0:T(1,128)S(1)} all-gather(f32[1,1,2]{2,1,0:T(1,128)S(1)} %bitcast.175), channel_id=1, replica_groups=mesh['dp'=32,'ctx'=8] {'ctx'}, dimensions={0}, use_global_device_ids=true | all-gather | bytes 72 | tf_op jit(solution)/shard_map/all_gather | solution.py:11
  102.8 0.1 copy.54
  102.9 0.1 rev.14
  103.0 0.1 copy.55
  103.0 0.1 copy.72
  103.2 0.1 copy.89
  103.4 0.2 slice_reduce_fusion.2
  103.6 0.4 convolution_bitcast_fusion
  104.0 4.4 %fusion.45 = f32[512,1,128]{2,1,0:T(1,128)} fusion(f32[512,2,1]{1,2,0:T(1,128)S(1)} %copy.72, f32[512,2,128]{2,0,1:T(8,128)S(1)} %convolution_bitcast_fusion), kind=kOutput, calls=%fused_computation.47 | convolution fusion | flops 1572864 | bytes 790528 | tf_op jit(solution)/shard_map/th,thn->tn/dot_general | solution.py:81
  108.4 2.4 fusion.11
  110.8 2.2 multiply_reduce_fusion
  113.0 0.1 all-gather.7.cloned.1.call-done
  113.1 1.3 rev.13
  114.5 0.9 while.14
  114.5 0.1 fusion.81
  114.6 0.1 fusion.81
  114.8 0.1 fusion.81
  114.9 0.1 fusion.81
  115.0 0.1 fusion.81
  115.2 0.1 fusion.81
  115.3 0.1 fusion.81
  115.4 0.1 fusion.49
  115.5 0.4 fusion.41
  115.9 0.2 multiply_reduce_fusion.4
  116.1 0.1 fusion.60
  116.2 0.4 rev.15
  116.6 0.6 reduce-window.16
  117.2 0.2 slice_reduce_fusion
  117.4 0.2 reduce-window.19
  117.5 0.1 add_bitcast_fusion
  117.6 0.4 rev.16
  118.0 0.2 multiply_reduce_fusion.3
  118.2 1.3 fusion.29
  119.5 75.2 %psum.7 = f32[2]{0:T(128)S(1)} all-reduce(f32[2]{0:T(128)S(1)} %multiply_reduce_fusion.3), channel_id=1, replica_groups=mesh['dp'=32,'ctx'=8] {'dp','ctx'}, use_global_device_ids=true, to_apply=%region_14.15 | all-reduce | flops 2 | bytes 16 | tf_op jit(solution)/shard_map/psum | solution.py:136
  194.7 0.1 fusion.42
  194.8 0.1 copy.70
  194.9 21.4 %reduce-scatter.3.cloned.1.call-done = f32[256,256]{1,0:T(8,128)} async-done(((f32[256,8192]{1,0:T(8,128)}), f32[256,256]{1,0:T(8,128)}) %reduce-scatter.3.cloned.1.call-update) | async-done | bytes 262160 | tf_op jit(solution)/shard_map/reduce_scatter | solution.py:130
  216.3 0.4 fusion.25
  216.7 0.8 copy.62
  217.6 1.7 fusion.30
  219.3 0.5 broadcast_multiply_fusion
  219.8 36.1 %reduce-scatter.5.cloned.1.call-done = f32[32,256]{1,0:T(8,128)} async-done(((f32[256,256]{1,0:T(8,128)}), f32[32,256]{1,0:T(8,128)}) %reduce-scatter.5.cloned.1.call-update) | async-done | bytes 32784 | tf_op jit(solution)/shard_map/reduce_scatter | solution.py:131
  (36 shorter events, 0.3 us)
Async XLA Ops:
  7.2 60.4 %all-gather.5.cloned.1.call-start = ((), (), s32[]{:S(2)}) async-start(), calls=%async_computation.2 | async-start | bytes 4718592 | tf_op jit(solution)/shard_map/all_gather | solution.py:118
  7.9 105.2 %all-gather.7.cloned.1.call-start = ((), (), s32[]{:S(2)}) async-start(), calls=%async_computation.5 | async-start | bytes 1179648 | tf_op jit(solution)/shard_map/all_gather | solution.py:11
  11.5 64.2 %copy-start.4 = (bf16[1,512,256]{2,1,0:T(8,128)(2,1)S(1)}, bf16[1,512,256]{2,1,0:T(8,128)(2,1)}, u32[]{:S(2)}) copy-start(bf16[1,512,256]{2,1,0:T(8,128)(2,1)} %param.12) | copy-start | bytes 786436
  11.5 64.5 %copy-start = (bf16[1,512,128]{2,1,0:T(8,128)(2,1)S(1)}, bf16[1,512,128]{2,1,0:T(8,128)(2,1)}, u32[]{:S(2)}) copy-start(bf16[1,512,128]{2,1,0:T(8,128)(2,1)} %param.13) | copy-start | bytes 393220
  11.5 64.5 %copy-start.1 = (bf16[1,512,128]{2,1,0:T(8,128)(2,1)S(1)}, bf16[1,512,128]{2,1,0:T(8,128)(2,1)}, u32[]{:S(2)}) copy-start(bf16[1,512,128]{2,1,0:T(8,128)(2,1)} %param.14) | copy-start | bytes 393220
  74.5 1.8 copy-start.2
  75.7 140.6 %reduce-scatter.3.cloned.1.call-start = ((), (), s32[]{:S(2)}) async-start(), calls=%async_computation.3 | async-start | bytes 8650752 | tf_op jit(solution)/shard_map/reduce_scatter | solution.py:130
  76.0 32.4 %copy-start.5 = (pred[512,512]{1,0:T(8,128)(4,1)}, pred[512,512]{1,0:T(8,128)(4,1)S(1)}, u32[]{:S(2)}) copy-start(pred[512,512]{1,0:T(8,128)(4,1)S(1)} %iota_compare_fusion) | copy-start | bytes 786436
  87.8 168.0 %reduce-scatter.5.cloned.1.call-start = ((), (), s32[]{:S(2)}) async-start(), calls=%async_computation.4 | async-start | bytes 294912 | tf_op jit(solution)/shard_map/reduce_scatter | solution.py:131
  114.4 3.5 %copy-start.7 = (s32[1,512,2]{1,2,0:T(2,128)S(1)}, s32[1,512,2]{1,2,0:T(2,128)}, u32[]{:S(2)}) copy-start(s32[1,512,2]{1,2,0:T(2,128)} %param.15) | copy-start | bytes 12292
  114.5 3.7 %copy-start.6 = (f32[512,1,128]{2,1,0:T(1,128)S(1)}, f32[512,1,128]{2,1,0:T(1,128)}, u32[]{:S(2)}) copy-start(f32[512,1,128]{2,1,0:T(1,128)} %fusion.45) | copy-start | bytes 786436
  115.5 100.8 %copy-start.3 = (f32[512,2,128]{0,2,1:T(8,128)S(1)}, f32[512,2,128]{0,2,1:T(8,128)}, u32[]{:S(2)}) copy-start(f32[512,2,128]{0,2,1:T(8,128)} %fusion.11) | copy-start | bytes 1572868
Sparse Core Ops, SparseCore 0:
  9.8 57.7 all-gather.4
  75.8 37.3 all-gather.6
  117.2 99.0 reduce-scatter.2
  219.4 36.4 reduce-scatter.4
where the time goes:
time: 263 us; the launch traced here: 262 us
  waiting for transfers between devices  114 us (43%)
  blocking collectives  89.9 us (34%)
  matrix products  33.1 us (13%)
  between operations  14 us (5%)
  other arithmetic  5.93 us (2%)
  local copies, waits for them, and re-layouts  4.61 us (2%)
    psum x1, blocking collectives, local(): rate_sum = lax.psum(rate_terms, ('dp', 'ctx'))  75.2 us
    all_gather x1, waiting for transfers between devices, local(): lax.all_gather(out_weight, 'ctx', axis=1, tiled=True)  56.1 us
    reduce_scatter x1, waiting for transfers between devices, local(): lax.psum_scatter(data_part, 'ctx', scatter_dimension=0, tiled=True)  36.1 us
    reduce_scatter x1, waiting for transfers between devices, local(): lax.psum_scatter(local_weight, 'dp', scatter_dimension=1, tiled=True)  21.4 us
    all_gather x1, blocking collectives, carried_in(): pieces = jax.tree.map(lambda part: lax.all_gather(part, axis), value)  14.7 us
    dot_general x1, matrix products, local(): lax.dot_general(outputs, grad_out, (((0,), (0,)), ((), ())), preferred_el...  9.06 us
    dot_general x1, matrix products, local(): lax.dot_general(grad_out, lax.all_gather(out_weight, 'ctx', axis=1, tiled...  6.93 us
  transfers between devices with their start and end apart: 4, of which 4 were waited for; matrix products, arithmetic and copies ran while one was open for 14% of the time, Pallas kernels for 0%

commit v1 on v0

v1 whole, which is shorter than its diff:
```python
import jax
import jax.numpy as jnp
from jax import lax
from jax.experimental import pallas as pl
from jax.experimental.pallas import tpu as pltpu
from jax.sharding import PartitionSpec as P

F32 = jnp.float32
BF16 = jnp.bfloat16
T = 512
D = 8192
HP = 256
N = 128
ROWS = 128
SIDE = 4
DEPTH = 8
VMEM_LIMIT = 48 << 20


def dot(a, b, contract):
    return lax.dot_general(a, b, (contract, ((), ())), preferred_element_type=F32)


def nn(a, b):
    return dot(a, b, ((1,), (0,)))


def nt(a, b):
    return dot(a, b, ((1,), (1,)))


def tn(a, b):
    return dot(a, b, ((0,), (0,)))


def split(a):
    high = a.astype(BF16)
    return high, (a - high.astype(F32)).astype(BF16)


def call(kernel, outs, args, smem=(), flops=0, bytes_accessed=0):
    specs = [
        pl.BlockSpec(memory_space=pltpu.SMEM if i in smem else pltpu.VMEM)
        for i in range(len(args))
    ]
    return pl.pallas_call(
        kernel,
        out_shape=outs,
        in_specs=specs,
        out_specs=jax.tree.map(lambda _: pl.BlockSpec(memory_space=pltpu.VMEM), outs),
        compiler_params=pltpu.CompilerParams(vmem_limit_bytes=VMEM_LIMIT),
        cost_estimate=pl.CostEstimate(
            flops=flops, bytes_accessed=bytes_accessed, transcendentals=0
        ),
    )(*args)


def shape(dims, kind=F32):
    return jax.ShapeDtypeStruct(dims, kind)


def forward_kernel(
    rate_ref, x_ref, inj_ref, rd_ref, code_ref, code_t_ref, state_ref,
    out_t_ref, mix_ref, wts_ref, rate_w_ref, carr_ref, fr_hi_ref, fr_lo_ref, aux_ref,
    chain_ref, decay_ref,
):
    rows = lax.broadcasted_iota(jnp.int32, (T, T), 0)
    cols = lax.broadcasted_iota(jnp.int32, (T, T), 1)
    lower = jnp.where(rows >= cols, 1.0, 0.0).astype(BF16)
    upper = jnp.where(rows <= cols, 1.0, 0.0).astype(BF16)

    def parts(code):
        return (code >> 8).astype(F32).astype(BF16), (code & 255).astype(F32).astype(BF16)

    high, low = parts(code_ref[...])
    count = 256.0 * nn(lower, high) + nn(lower, low)
    high, low = parts(code_t_ref[...])
    count_t = 256.0 * nn(high, upper) + nn(low, upper)
    inject = inj_ref[...]
    read = rd_ref[...]
    inject_f = inject.astype(F32)
    read_f = read.astype(F32)
    lane = lax.broadcasted_iota(jnp.int32, (T, 128), 1)
    aux = jnp.zeros((T, 128), F32)
    decay_rows = []
    for h in range(2):
        rate = rate_ref[h]
        hs = slice(h * 128, h * 128 + 128)
        x = x_ref[:, hs]
        state = state_ref[h]
        s_hi, s_lo = split(state)
        cum = -rate * count[:, h : h + 1]
        cum_end = cum[T - 1 :, :]
        start_w = jnp.exp(cum)
        to_end = jnp.exp(-rate * (count[T - 1 :, h : h + 1] - count[:, h : h + 1]))
        aux = jnp.where(lane == h, to_end, aux)
        aux = jnp.where(lane == 2 + h, start_w, aux)
        fr_hi, fr_lo = split(start_w * read_f)
        fr_hi_ref[h] = fr_hi
        fr_lo_ref[h] = fr_lo
        carried = (nt(read, s_hi) + nt(read, s_lo)) * start_w
        carr_ref[:, hs] = carried * cum
        scaled = (cum_end - cum) * to_end * inject_f
        b_hi, b_lo = split(scaled)
        end_w = jnp.exp(cum_end)
        chain = tn(x, b_hi) + tn(x, b_lo) + (cum_end * end_w) * state
        for z in range(DEPTH):
            chain_ref[z, h * 16 : h * 16 + 16, :] = chain[z * 16 : z * 16 + 16, :]
        decay_rows.append(jnp.broadcast_to(end_w, (1, 128)))
        for i in range(T // ROWS):
            rs = slice(i * ROWS, i * ROWS + ROWS)
            width = (i + 1) * ROWS
            inter = nt(read[rs], inject[:width])
            spread = -rate * (count[rs, h : h + 1] - count_t[h : h + 1, :width])
            keep = rows[rs, :width] >= cols[rs, :width]
            spread = jnp.where(keep, spread, 0.0)
            wts = jnp.where(keep, jnp.exp(spread), 0.0)
            mixed = inter * wts
            narrow = mixed.astype(BF16)
            wts_ref[h, rs, :width] = wts
            rate_w_ref[h, rs, :width] = mixed * spread
            mix_ref[h, rs, :width] = narrow
            within = nn(narrow, x[:width])
            out = within + carried[rs]
            out_t_ref[hs, rs] = out.T.astype(BF16)
    aux_ref[...] = aux
    decay_ref[...] = jnp.concatenate(decay_rows + [jnp.zeros((6, 128), F32)], axis=0)


def weight_send_kernel(pos_ref, out_t_ref, c0, c1, c2, c3, o_ref):
    for dy, c_ref in enumerate((c0, c1, c2, c3)):
        o_ref[0, dy] = nn(out_t_ref[...], c_ref[...]).astype(BF16)


def weight_keep_kernel(pos_ref, out_t_ref, c0, c1, c2, c3, recv_ref, *outs):
    first, second = outs[:SIDE], outs[SIDE:]
    dx = pl.program_id(0)
    for dy, c_ref in enumerate((c0, c1, c2, c3)):
        total = nn(out_t_ref[...], c_ref[...]) + recv_ref[0, dy].astype(F32)
        total = total.astype(BF16)
        second[dy][dx] = total[128:]
        for k in range(SIDE):

            @pl.when(dx == k)
            def _(k=k, dy=dy, total=total):
                first[k][dy] = total[:128]


def weight_terms(pos, out_t, cotangent, recv=None):
    def column(dy):
        def index(dx, pos):
            block = lax.rem(pos[0] + dx, SIDE) * 8 + lax.rem(pos[1] + dy, SIDE) * 2
            return (0, block + (pos[2] if recv is not None else 1 - pos[2]))

        return pl.BlockSpec((T, 256), index)

    in_specs = [pl.BlockSpec((HP, T), lambda dx, pos: (0, 0))]
    in_specs += [column(dy) for dy in range(SIDE)]
    args = [out_t] + [cotangent] * SIDE
    if recv is None:
        kernel = weight_send_kernel
        outs = shape((SIDE, SIDE, 256, 256), BF16)
        out_specs = pl.BlockSpec((1, SIDE, 256, 256), lambda dx, pos: (dx, 0, 0, 0))
    else:
        kernel = weight_keep_kernel
        in_specs.append(pl.BlockSpec((1, SIDE, 256, 256), lambda dx, pos: (dx, 0, 0, 0)))
        args.append(recv)
        outs = [shape((SIDE, 128, 256), BF16)] * (2 * SIDE)
        out_specs = [pl.BlockSpec((SIDE, 128, 256), lambda dx, pos: (0, 0, 0))] * (2 * SIDE)
    return pl.pallas_call(
        kernel,
        out_shape=outs,
        grid_spec=pltpu.PrefetchScalarGridSpec(
            num_scalar_prefetch=1, grid=(SIDE,), in_specs=in_specs, out_specs=out_specs
        ),
        compiler_params=pltpu.CompilerParams(vmem_limit_bytes=VMEM_LIMIT),
        cost_estimate=pl.CostEstimate(
            flops=T * D * HP, bytes_accessed=7 << 20, transcendentals=0
        ),
    )(pos, *args)


def plane_sum_kernel(*refs):
    ins, outs = refs[:8], refs[8:]
    for part in range(2):
        for k in range(SIDE):
            total = ins[part * 4][k].astype(F32)
            for j in range(1, SIDE):
                total = total + ins[part * 4 + j][k].astype(F32)
            outs[part * 4 + k][...] = total


def line_sum_kernel(*refs):
    ins, out_ref = refs[:8], refs[8]
    for part in range(2):
        total = ins[part * 4][...] + ins[part * 4 + 1][...]
        total = total + ins[part * 4 + 2][...] + ins[part * 4 + 3][...]
        for k in range(4):
            out_ref[part * 4 + k] = total[k * 32 : k * 32 + 32, :]


def depth_sum_kernel(in_ref, out_ref):
    total = in_ref[0]
    for k in range(1, DEPTH):
        total = total + in_ref[k]
    out_ref[...] = total


def grad_first_kernel(pos_ref, cot_ref, w_ref, o_ref):
    part = nt(cot_ref[...], w_ref[0])

    @pl.when(pl.program_id(0) == 0)
    def _():
        o_ref[...] = part

    @pl.when(pl.program_id(0) > 0)
    def _():
        o_ref[...] += part


def grad_second_kernel(
    pos_ref, cot_ref, w_ref, first_ref, fr_hi_ref, fr_lo_ref, chain_ref, decay_ref,
    og_ref, pay_ref, acc_ref,
):
    part = nt(cot_ref[...], w_ref[0])
    step = pl.program_id(0)

    @pl.when(step == 0)
    def _():
        acc_ref[...] = part + first_ref[...]

    @pl.when(step > 0)
    def _():
        acc_ref[...] += part

    @pl.when(step == pl.num_programs(0) - 1)
    def _():
        grad = acc_ref[...].astype(BF16)
        og_ref[...] = grad
        for h in range(2):
            g = grad[:, h * 128 : h * 128 + 128]
            adjoint = tn(g, fr_hi_ref[h]) + tn(g, fr_lo_ref[h])
            for z in range(DEPTH):
                pay_ref[z, h * 16 : h * 16 + 16, :] = adjoint[z * 16 : z * 16 + 16, :]
        for z in range(DEPTH):
            pay_ref[z, 32:64, :] = chain_ref[z]
            pay_ref[z, 64:72, :] = decay_ref[...]


def output_grad_part(pos, cotangent, weights, mine, more=None):
    def fixed(dims):
        return pl.BlockSpec(dims, lambda z, pos: (0,) * len(dims))

    in_specs = [
        pl.BlockSpec((T, 512), lambda z, pos: (0, 2 * z + (pos[2] if mine else 1 - pos[2]))),
        pl.BlockSpec((1, HP, 512), lambda z, pos: (z, 0, 0)),
    ]
    scratch = []
    if more is None:
        kernel, outs, out_specs, more = grad_first_kernel, shape((T, HP)), fixed((T, HP)), ()
    else:
        kernel = grad_second_kernel
        in_specs += [fixed(a.shape) for a in more]
        outs = [shape((T, HP), BF16), shape((DEPTH, 72, 128))]
        out_specs = [fixed((T, HP)), fixed((DEPTH, 72, 128))]
        scratch = [pltpu.VMEM((T, HP), F32)]
    return pl.pallas_call(
        kernel,
        out_shape=outs,
        grid_spec=pltpu.PrefetchScalarGridSpec(
            num_scalar_prefetch=1,
            grid=(DEPTH,),
            in_specs=in_specs,
            out_specs=out_specs,
            scratch_shapes=scratch,
        ),
        compiler_params=pltpu.CompilerParams(vmem_limit_bytes=VMEM_LIMIT),
        cost_estimate=pl.CostEstimate(
            flops=T * D * HP, bytes_accessed=7 << 20, transcendentals=0
        ),
    )(pos, cotangent, weights, *more)


def backward_kernel(
    g_ref, x_ref, inj_ref, rd_ref, state_ref, mix_ref, wts_ref, rate_w_ref, carr_ref, aux_ref,
    gi_ref, ginj_ref, gread_ref, rate_ref,
):
    inject = inj_ref[...]
    read = rd_ref[...]
    gi_ref[...] = jnp.zeros((T, HP), F32)
    ginj_ref[...] = jnp.zeros((T, N), F32)
    rate_rows = []
    for h in range(2):
        hs = slice(h * 128, h * 128 + 128)
        x = x_ref[:, hs]
        g = g_ref[:, hs]
        state = state_ref[h].astype(BF16)
        rate = jnp.sum(g.astype(F32) * carr_ref[:, hs], axis=0, keepdims=True)
        for i in range(T // ROWS):
            rs = slice(i * ROWS, i * ROWS + ROWS)
            width = (i + 1) * ROWS
            pairing = nt(g[rs], x[:width])
            rated = jnp.sum(pairing * rate_w_ref[h, rs, :width], axis=0, keepdims=True)
            for j in range(i + 1):
                rate = rate + rated[:, j * ROWS : j * ROWS + ROWS]
            pairing = (pairing * wts_ref[h, rs, :width]).astype(BF16)
            through = nn(g[rs], state) * aux_ref[rs, 2 + h : 3 + h]
            read_part = nn(pairing, inject[:width]) + through
            if h == 0:
                gread_ref[rs, :] = read_part
            else:
                gread_ref[rs, :] += read_part
            ginj_ref[:width, :] += tn(pairing, read[rs])
            gi_ref[:width, hs] += tn(mix_ref[h, rs, :width], g[rs])
        rate_rows.append(rate)
    rate_ref[...] = jnp.concatenate(rate_rows + [jnp.zeros((6, 128), F32)], axis=0)


def scan_kernel(pay_ref, local_ref, inc_ref, rate_ref):
    rates = [local_ref[h : h + 1, :] for h in range(2)]
    for h in range(2):
        hs = slice(h * 16, h * 16 + 16)
        running = jnp.zeros((16, 128), F32)
        for c in range(DEPTH - 1, -1, -1):
            inc_ref[c, hs, :] = running
            rates[h] = rates[h] + jnp.sum(
                running * pay_ref[c, 32 + h * 16 : 48 + h * 16, :], axis=0, keepdims=True
            )
            running = pay_ref[c, hs, :] + pay_ref[c, 64 + h : 65 + h, :] * running
    sums = [jnp.broadcast_to(jnp.sum(r, axis=1, keepdims=True), (1, 128)) for r in rates]
    rate_ref[...] = jnp.concatenate(sums + [jnp.zeros((6, 128), F32)], axis=0)


def finish_kernel(gi_ref, ginj_ref, x_ref, inj_ref, aux_ref, inc_ref, o_gi_ref, o_ginj_ref):
    total = ginj_ref[...]
    inject = inj_ref[...]
    for h in range(2):
        hs = slice(h * 128, h * 128 + 128)
        pieces = [inc_ref[z, h * 16 : h * 16 + 16, :] for z in range(DEPTH)]
        incoming = jnp.concatenate(pieces, axis=0).astype(BF16)
        to_end = aux_ref[:, h : h + 1]
        o_gi_ref[:, hs] = (gi_ref[:, hs] + to_end * nt(inject, incoming)).astype(BF16)
        total = total + to_end * nn(x_ref[:, hs], incoming)
    o_ginj_ref[...] = total


def dp_index(x, y, core):
    return ((x % SIDE) * SIDE + y % SIDE) * 2 + core


def shifts(dx, dy):
    places = [(x, y, c) for x in range(SIDE) for y in range(SIDE) for c in range(2)]
    return [(dp_index(x, y, c), dp_index(x + dx, y + dy, c)) for x, y, c in places]


def flips(bits):
    return [(i, i ^ bits) for i in range(2 * SIDE * SIDE)]


def local(
    cotangent, out_weight, head_input, injector, readout, decay_code, decay_rate, start_state
):
    cot = cotangent[0]
    x = head_input[0]
    inject = injector[0]
    read = readout[0]
    state = start_state[0, 0]
    code = decay_code[0]
    me = lax.axis_index("dp")
    core = me % 2
    pos = jnp.stack([me // 8, (me // 2) % SIDE, core]).astype(jnp.int32)

    half = lax.dynamic_slice_in_dim(out_weight, core * 512, 512, 1)
    mine = lax.all_gather(half, "ctx", axis=0)
    other = lax.ppermute(mine, "dp", flips(1))

    code_cols = jnp.pad(code, ((0, 0), (0, 126)))
    code_rows = jnp.pad(code.T, ((0, 6), (0, 0)))
    out_t, mix, wts, rate_w, carr, fr_hi, fr_lo, aux, chain, decay = call(
        forward_kernel,
        [
            shape((HP, T), BF16), shape((2, T, T), BF16), shape((2, T, T)), shape((2, T, T)),
            shape((T, HP)), shape((2, T, N), BF16), shape((2, T, N), BF16), shape((T, 128)),
            shape((DEPTH, 32, 128)), shape((8, 128)),
        ],
        (decay_rate, x, inject, read, code_cols, code_rows, state),
        smem=(0,), flops=1 << 30, bytes_accessed=8 << 20,
    )

    sent = lax.ppermute(weight_terms(pos, out_t, cot), "dp", flips(1))
    parts = weight_terms(pos, out_t, cot, sent)
    first, second = parts[:SIDE], parts[SIDE:]
    first = [first[0]] + [lax.ppermute(first[d], "dp", shifts(d, 0)) for d in range(1, SIDE)]
    second = [second[0]] + [lax.ppermute(second[d], "dp", shifts(0, d)) for d in range(1, SIDE)]
    parts = call(plane_sum_kernel, [shape((128, 256))] * 8, (*first, *second),
                 flops=4 << 20, bytes_accessed=3 << 20)
    first, second = parts[:SIDE], parts[SIDE:]
    first = [first[0]] + [lax.ppermute(first[d], "dp", shifts(0, d)) for d in range(1, SIDE)]
    second = [second[0]] + [lax.ppermute(second[d], "dp", shifts(d, 0)) for d in range(1, SIDE)]
    blocks = call(line_sum_kernel, shape((DEPTH, 32, 256)), (*first, *second),
                  flops=1 << 20, bytes_accessed=1 << 20)
    blocks = lax.all_to_all(blocks, "ctx", 0, 0, tiled=True)
    grad_weight = call(depth_sum_kernel, shape((32, 256)), (blocks,),
                       flops=1 << 18, bytes_accessed=1 << 18)

    part = output_grad_part(pos, cot, mine, True)
    grad, pay = output_grad_part(pos, cot, other, False, (part, fr_hi, fr_lo, chain, decay))
    pay = lax.all_to_all(pay, "ctx", 0, 0, tiled=True)
    gi, ginj, grad_read, rate_local = call(
        backward_kernel,
        [shape((T, HP)), shape((T, N)), shape((T, N)), shape((8, 128))],
        (grad, x, inject, read, state, mix, wts, rate_w, carr, aux),
        flops=1 << 30, bytes_accessed=8 << 20,
    )
    incoming, rate = call(
        scan_kernel, [shape((DEPTH, 32, 128)), shape((8, 128))], (pay, rate_local),
        flops=1 << 18, bytes_accessed=1 << 19,
    )
    incoming = lax.all_to_all(incoming, "ctx", 0, 0, tiled=True)
    grad_input, grad_inject = call(
        finish_kernel, [shape((T, HP), BF16), shape((T, N))],
        (gi, ginj, x, inject, aux, incoming), flops=1 << 26, bytes_accessed=2 << 20,
    )

    rate = rate + lax.ppermute(rate, "dp", flips(1))
    for unit in (2, 8):
        one, two, three = (lax.ppermute(rate, "dp", flips(unit * k)) for k in (1, 2, 3))
        rate = (rate + two) + (one + three)
    rate = lax.all_to_all(jnp.broadcast_to(rate, (DEPTH, 8, 128)), "ctx", 0, 0, tiled=True)
    rate = jnp.sum(rate[:, :2, 0], axis=0)
    tokens = T * lax.axis_size("dp") * lax.axis_size("ctx")
    return grad_input[None], grad_inject[None], grad_read[None], grad_weight, rate / tokens


def solution(mesh):
    in_specs = (
        P("dp", "ctx", None),
        P(None, "ctx"),
        P("dp", "ctx", None),
        P("dp", "ctx", None),
        P("dp", "ctx", None),
        P("dp", "ctx", None),
        P(),
        P("dp", "ctx", None, None, None),
    )
    out_specs = (
        P("dp", "ctx", None),
        P("dp", "ctx", None),
        P("dp", "ctx", None),
        P("ctx", "dp"),
        P(),
    )
    return jax.shard_map(local, mesh=mesh, in_specs=in_specs, out_specs=out_specs, check_vma=False)
```

time: 263 us -> 185 us (0.70)
  blocking collectives: 89.9 us -> 0 us
  waiting for transfers between devices: 114 us -> 50.8 us
  starting transfers between devices: 0.16 us -> 50.3 us
  Pallas kernels: 0 us -> 41.5 us
  matrix products: 33.1 us -> 0 us
  local copies, waits for them, and re-layouts: 4.61 us -> 25.8 us
  other arithmetic: 5.93 us -> 0.73 us
    psum x1 -> x0, blocking collectives: 75.2 us -> none  [local(): rate_sum = lax.psum(rate_terms, ('dp', 'ctx'))]
    reduce_scatter x2 -> x0, waiting for transfers between devices: 57.5 us -> none  [the longest x1 36.1 us: local(): lax.psum_scatter(data_part, 'ctx', scatter_dimension=0, tiled=True)]
    pallas_call x0 -> x11, Pallas kernels: none -> 41.5 us  [the longest x7 14.2 us: call(): pl.pallas_call(kernel, out_shape=outs, in_specs=specs, out_specs=jax.tree...]
    dot_general x14 -> x0, matrix products: 33.1 us -> none  [the longest x1 9.06 us: local(): lax.dot_general(outputs, grad_out, (((0,), (0,)), ((), ())), preferred_el...]
    all_gather x2 -> x1, waiting for transfers between devices: 56.2 us -> 27.8 us  [local(): mine = lax.all_gather(half, 'ctx', axis=0)]
    ppermute x0 -> x21, starting transfers between devices: none -> 28.2 us  [the longest x6 9.47 us: local(): lax.ppermute(rate, 'dp', flips(unit * k))]
    unnamed x21 -> x79, local copies, waits for them, and re-layouts: 1.11 us -> 23.7 us
    all_to_all x0 -> x4, starting transfers between devices: none -> 22 us  [the longest x1 7.2 us: local(): lax.all_to_all(jnp.broadcast_to(rate, (DEPTH, 8, 128)), 'ctx', 0, 0, tile...]
  transfers between devices with their start and end apart: 4 -> 26, of which waited for: 4 -> 8; matrix products, arithmetic and copies ran while one was open for 14% -> 1% of each run, Pallas kernels for 0% -> 22%
where the time goes in v1:
time: 185 us; the launch traced here: 183 us
  waiting for transfers between devices  50.8 us (27%)
  starting transfers between devices  50.3 us (27%)
  Pallas kernels  41.5 us (22%)
  local copies, waits for them, and re-layouts  25.8 us (14%)
  between operations  14.4 us (8%)
    all_gather x1, waiting for transfers between devices, local(): mine = lax.all_gather(half, 'ctx', axis=0)  27.8 us
    unnamed x79, local copies, waits for them, and re-layouts  23.7 us
    pallas_call x7, Pallas kernels, call(): pl.pallas_call(kernel, out_shape=outs, in_specs=specs, out_specs=jax.tree...  14.2 us
    pallas_call x2, Pallas kernels, output_grad_part(): pl.pallas_call(kernel, out_shape=outs, grid_spec=pltpu.PrefetchScalarGrid...  13.9 us
    pallas_call x2, Pallas kernels, weight_terms(): pl.pallas_call(kernel, out_shape=outs, grid_spec=pltpu.PrefetchScalarGrid...  13.5 us
    ppermute x6, starting transfers between devices, local(): lax.ppermute(rate, 'dp', flips(unit * k))  9.47 us
    all_to_all x1, waiting for transfers between devices, local(): incoming = lax.all_to_all(incoming, 'ctx', 0, 0, tiled=True)  8.36 us
    all_to_all x1, waiting for transfers between devices, local(): lax.all_to_all(jnp.broadcast_to(rate, (DEPTH, 8, 128)), 'ctx', 0, 0, tile...  7.39 us
  transfers between devices with their start and end apart: 26, of which 8 were waited for; matrix products, arithmetic and copies ran while one was open for 1% of the time, Pallas kernels for 22%

profile of v1, /device:TPU:2, one launch (start us, length us, event | category | flops | bytes accessed | tf_op | source)
XLA Modules:
  0.0 183.4 jit_solution(11824112781232721752)
XLA Ops:
  7.2 1.0 copy-done
  8.2 0.7 constant_dynamic-slice_fusion
  9.0 0.7 pad.9.code_t_ref
  9.7 0.8 copy.19
  10.6 0.9 copy-done.6
  11.5 0.9 copy-done.10
  12.4 0.9 copy-done.28
  13.3 0.9 copy-done.30
  14.2 0.7 copy-done.38
  14.9 3.6 %shard_map.120 = (bf16[256,512]{1,0:T(8,128)(2,1)S(1)}, bf16[2,512,512]{2,1,0:T(8,128)(2,1)S(1)}, f32[2,512,512]{2,1,0:T(8,128)S(1)}, f32[2,512,512]{2,1,0:T(8,1...) custom-call(f32[2]{0:T(128)S(1)} %copy-done.38, ...), custom_call_target="tpu_custom_call" | custom-call | flops 1073741824 | bytes 8388608 | tf_op jit(solution)/shard_map/pallas_call | solution.py:46
  18.5 1.3 copy-done.1
  19.9 0.9 copy-done.4
  20.9 5.6 %shard_map.125 = bf16[4,4,256,256]{3,2,1,0:T(8,128)(2,1)} custom-call(s32[3]{0:T(128)S(1)} %pad_add_fusion.pos_ref, bf16[256,512]{1,0:T(8,128)(2,1)S(1)} %get-tuple-element.59.out_t_ref, bf16[512,8192]{1,0:T(8,128)(2,1)} %bitcast.27, bf16[512,8192]{1,0:T(8,128)(2,1)} %bitcast.28, bf16[512,8192]{1,0:T(8,128)(2,1)} %bitcast.29, bf16[512,8192]{1,0:T(8,128)(2,1)} %bitcast.30), custom_call_target="tpu_custom_call" | custom-call | flops 1073741824 | bytes 7340032 | tf_op jit(solution)/shard_map/pallas_call | solution.py:170
  26.7 27.8 %all-gather.3.cloned.1.call-done = bf16[2048,512]{1,0:T(8,128)(2,1)} async-done(((bf16[256,512]{1,0:T(8,128)(2,1)}), bf16[2048,512]{1,0:T(8,128)(2,1)}) %all-gather.3.cloned.1.call-update) | async-done | bytes 2097168 | tf_op jit(solution)/shard_map/all_gather | solution.py:374
  54.5 7.8 %shard_map.126 = (bf16[4,128,256]{2,1,0:T(8,128)(2,1)S(1)}, bf16[4,128,256]{2,1,0:T(8,128)(2,1)S(1)}, bf16[4,128,256]{2,1,0:T(8,128)(2,1)}, bf16[4,128,256]{2,1,...) custom-call(s32[3]{0:T(128)S(1)} %pad_add_fusion.pos_ref, ...), custom_call_target="tpu_custom_call" | custom-call | flops 1073741824 | bytes 7340032 | tf_op jit(solution)/shard_map/pallas_call | solution.py:170
  62.3 0.7 copy-done.20
  63.0 1.5 collective-permute-start.2
  64.5 1.2 collective-permute-start.3
  65.6 2.1 %collective-permute-start.4 = (bf16[4,128,256]{2,1,0:T(8,128)(2,1)}, bf16[4,128,256]{2,1,0:T(8,128)(2,1)}, u32[]{:S(2)}, u32[]{:S(2)}) collective-permute-start(bf16[4,128,256]{2,1,0:T(8,128)(2,1)} %get-tuple-element.63), channel_id=1, source_target_pairs={{0,192},{8,200},{16,208},{24,216},{32,224},{40,232},{48,240},{56,2... | collective-permute-start | bytes 786440 | tf_op jit(solution)/shard_map/ppermute | solution.py:393
  67.7 1.8 collective-permute-start.5
  69.5 6.7 %shard_map.119.first_ref = f32[512,256]{1,0:T(8,128)S(1)} custom-call(s32[3]{0:T(128)S(1)} %pad_add_fusion.pos_ref, bf16[512,8192]{1,0:T(8,128)(2,1)} %bitcast.35, bf16[8,256,512]{2,1,0:T(8,128)(2,1)S(1)} %bitcast.16), custom_call_target="tpu_custom_call" | custom-call | flops 1073741824 | bytes 7340032 | tf_op jit(solution)/shard_map/pallas_call | solution.py:267
  76.3 3.3 %collective-permute-start.6 = (bf16[4,128,256]{2,1,0:T(8,128)(2,1)}, bf16[4,128,256]{2,1,0:T(8,128)(2,1)}, u32[]{:S(2)}, u32[]{:S(2)}) collective-permute-start(bf16[4,128,256]{2,1,0:T(8,128)(2,1)} %get-tuple-element.66), channel_id=1, source_target_pairs={{0,32},{8,40},{16,48},{24,56},{32,0},{40,8},{48,16},{56,24},{64,96... | collective-permute-start | bytes 786440 | tf_op jit(solution)/shard_map/ppermute | solution.py:394
  80.2 7.1 %shard_map.121 = (bf16[512,256]{1,0:T(8,128)(2,1)S(1)}, f32[8,72,128]{2,1,0:T(8,128)S(1)}) custom-call(s32[3]{0:T(128)S(1)} %pad_add_fusion.pos_ref, bf16[512,8192]{1,0:T(8,128)(2,1)} %bitcast.36, bf16[8,256,512]{2,1,0:T(8,128)(2,1)S(1)} %collective-permute-done.w_ref, f32[512,256]{1,0:T(8,128)S(1)} %shard_map.119.first_ref, ...), custom_call_target="tpu_custom_call" | custom-call | flops 1073741824 | bytes 7340032 | tf_op jit(solution)/shard_map/pallas_call | solution.py:267
  87.3 0.7 copy-done.15
  88.1 0.7 copy-done.26
  88.8 4.5 %all-to-all-start = ((f32[8,72,128]{2,1,0:T(8,128)}), f32[8,72,128]{2,1,0:T(8,128)S(1)}, u32[]{:S(2)}, u32[]{:S(2)}) async-start(f32[8,72,128]{2,1,0:T(8,128)} %copy-done.15), calls=%async_computation | async-start | bytes 589824 | tf_op jit(solution)/shard_map/all_to_all | solution.py:408
  93.3 1.0 copy-done.21
  94.2 0.9 copy-done.23
  95.2 0.9 copy-done.25
  96.2 2.2 %shard_map.127 = (f32[128,256]{1,0:T(8,128)S(1)}, f32[128,256]{1,0:T(8,128)S(1)}, f32[128,256]{1,0:T(8,128)}, f32[128,256]{1,0:T(8,128)}, f32[128,256]{1,0:T(8,1...) custom-call(bf16[4,128,256]{2,1,0:T(8,128)(2,1)S(1)} %copy-done.21, ...), custom_call_target="tpu_custom_call" | custom-call | flops 4194304 | bytes 3145728 | tf_op jit(solution)/shard_map/pallas_call | solution.py:46
  98.3 0.6 copy-done.32
  99.0 0.7 copy-done.34
  100.2 1.1 collective-permute-start.9
  101.3 1.6 collective-permute-start.10
  102.9 3.0 %collective-permute-start.11 = (f32[128,256]{1,0:T(8,128)}, f32[128,256]{1,0:T(8,128)}, u32[]{:S(2)}, u32[]{:S(2)}) collective-permute-start(f32[128,256]{1,0:T(8,128)} %get-tuple-element.73), channel_id=1, source_target_pairs={{0,64},{8,72},{16,80},{24,88},{32,96},{40,104},{48,112},{56,120},{... | collective-permute-start | bytes 393224 | tf_op jit(solution)/shard_map/ppermute | solution.py:399
  106.4 1.3 collective-permute-done.8.refs_1_
  107.7 0.6 copy-done.36
  108.3 1.5 collective-permute-start.13
  109.8 1.2 copy-done.5
  111.1 1.0 copy-done.14
  112.1 0.9 copy-done.27
  113.0 0.9 copy-done.31
  113.9 4.1 %shard_map.122 = (f32[512,256]{1,0:T(8,128)S(1)}, f32[512,128]{1,0:T(8,128)S(1)}, f32[512,128]{1,0:T(8,128)}, f32[8,128]{1,0:T(8,128)S(1)}) custom-call(bf16[512,256]{1,0:T(8,128)(2,1)S(1)} %copy-done.27, bf16[512,256]{1,0:T(8,128)(2,1)S(1)} %bitcast.18, bf16[512,128]{1,0:T(8,128)(2,1)S(1)} %bitcast.21, bf16[512,128]{1,0:T(8,128)(2,1)S(1)} %bitcast.24, ...), custom_call_target="tpu_custom_call" | custom-call | flops 1073741824 | bytes 8388608 | tf_op jit(solution)/shard_map/pallas_call | solution.py:46
  118.0 0.8 copy-done.8
  118.8 0.7 copy-done.18
  119.5 0.7 shard_map.123
  120.3 0.9 copy-done.33
  121.2 0.9 copy-done.35
  122.1 0.9 copy-done.37
  123.0 1.9 %shard_map.128 = f32[8,32,256]{2,1,0:T(8,128)} custom-call(f32[128,256]{1,0:T(8,128)S(1)} %copy-done.33, f32[128,256]{1,0:T(8,128)S(1)} %copy-done.37, f32[128,256]{1,0:T(8,128)} %collective-permute-done.9.refs_2_, f32[128,256]{1,0:T(8,128)} %collective-permute-done.10.refs_3_, f32[128,256]{1,0:T(8,128)S(1)} %copy-done.35, ...), custom_call_target="tpu_custom_call" | custom-call | flops 1048576 | bytes 1048576 | tf_op jit(solution)/shard_map/pallas_call | solution.py:46
  124.9 7.0 %all-to-all-start.2 = ((f32[8,32,256]{2,1,0:T(8,128)}), f32[8,32,256]{2,1,0:T(8,128)S(1)}, u32[]{:S(2)}, u32[]{:S(2)}) async-start(f32[8,32,256]{2,1,0:T(8,128)} %shard_map.128), calls=%async_computation.2 | async-start | bytes 524288 | tf_op jit(solution)/shard_map/all_to_all | solution.py:402
  132.0 1.8 collective-permute-start.16
  133.8 2.9 %collective-permute-start.15 = (f32[8,128]{1,0:T(8,128)S(1)}, f32[8,128]{1,0:T(8,128)S(1)}, u32[]{:S(2)}, u32[]{:S(2)}) collective-permute-start(f32[8,128]{1,0:T(8,128)S(1)} %add.40), channel_id=1, source_target_pairs={{0,32},{8,40},{16,48},{24,56},{32,0},{40,8},{48,16},{56,24},{64,96... | collective-permute-start | bytes 12296 | tf_op jit(solution)/shard_map/ppermute | solution.py:427
  136.8 2.1 %collective-permute-done.15 = f32[8,128]{1,0:T(8,128)S(1)} collective-permute-done((f32[8,128]{1,0:T(8,128)S(1)}, f32[8,128]{1,0:T(8,128)S(1)}, u32[]{:S(2)}, u32[]{:S(2)}) %collective-permute-start.15) | collective-permute-done | bytes 4128 | tf_op jit(solution)/shard_map/ppermute | solution.py:427
  139.5 2.6 %collective-permute-start.19 = (f32[8,128]{1,0:T(8,128)S(1)}, f32[8,128]{1,0:T(8,128)S(1)}, u32[]{:S(2)}, u32[]{:S(2)}) collective-permute-start(f32[8,128]{1,0:T(8,128)S(1)} %add_add_fusion.1), channel_id=1, source_target_pairs={{0,64},{8,72},{16,80},{24,88},{32,96},{40,104},{48,112},{56,120},{... | collective-permute-start | bytes 12296 | tf_op jit(solution)/shard_map/ppermute | solution.py:427
  142.2 1.5 collective-permute-start.18
  143.7 3.5 %collective-permute-done.18 = f32[8,128]{1,0:T(8,128)S(1)} collective-permute-done((f32[8,128]{1,0:T(8,128)S(1)}, f32[8,128]{1,0:T(8,128)S(1)}, u32[]{:S(2)}, u32[]{:S(2)}) %collective-permute-start.18) | collective-permute-done | bytes 4128 | tf_op jit(solution)/shard_map/ppermute | solution.py:427
  147.3 0.6 broadcast_in_dim.15
  147.9 7.2 %all-to-all-start.3 = ((f32[8,8,128]{2,1,0:T(8,128)}), f32[8,8,128]{2,1,0:T(8,128)S(1)}, u32[]{:S(2)}, u32[]{:S(2)}) async-start(f32[8,8,128]{2,1,0:T(8,128)} %broadcast_in_dim.15), calls=%async_computation.3 | async-start | bytes 65536 | tf_op jit(solution)/shard_map/all_to_all | solution.py:429
  155.1 0.6 shard_map.129
  155.7 7.4 %all-to-all-done.3 = f32[8,8,128]{2,1,0:T(8,128)S(1)} async-done(((f32[8,8,128]{2,1,0:T(8,128)}), f32[8,8,128]{2,1,0:T(8,128)S(1)}, u32[]{:S(2)}, u32[]{:S(2)}) %all-to-all-start.3) | async-done | bytes 32800 | tf_op jit(solution)/shard_map/all_to_all | solution.py:429
  163.1 3.4 %all-to-all-start.1 = ((f32[8,32,128]{2,1,0:T(8,128)}), f32[8,32,128]{2,1,0:T(8,128)S(1)}, u32[]{:S(2)}, u32[]{:S(2)}) async-start(f32[8,32,128]{2,1,0:T(8,128)} %get-tuple-element.55), calls=%async_computation.1 | async-start | bytes 262144 | tf_op jit(solution)/shard_map/all_to_all | solution.py:419
  167.1 8.4 %all-to-all-done.1.inc_ref = f32[8,32,128]{2,1,0:T(8,128)S(1)} async-done(((f32[8,32,128]{2,1,0:T(8,128)}), f32[8,32,128]{2,1,0:T(8,128)S(1)}, u32[]{:S(2)}, u32[]{:S(2)}) %all-to-all-start.1) | async-done | bytes 131104 | tf_op jit(solution)/shard_map/all_to_all | solution.py:419
  175.5 1.1 shard_map.124
  (89 shorter events, 3.7 us)
Async XLA Ops:
  7.2 1.0 copy-start
  7.2 47.3 %all-gather.3.cloned.1.call-start = ((), (), s32[]{:S(2)}) async-start(), calls=%async_computation.4 | async-start | bytes 2359296 | tf_op jit(solution)/shard_map/all_gather | solution.py:374
  10.6 1.0 copy-start.6
  11.5 0.9 copy-start.10
  12.4 0.9 copy-start.28
  13.3 0.9 copy-start.30
  14.2 0.7 copy-start.38
  18.5 1.3 copy-start.1
  19.9 0.9 copy-start.4
  20.8 5.7 %copy-start.13 = (f32[512,256]{1,0:T(8,128)}, f32[512,256]{1,0:T(8,128)S(1)}, u32[]{:S(2)}) copy-start(f32[512,256]{1,0:T(8,128)S(1)} %get-tuple-element.49.carr_ref) | copy-start | bytes 1572868
  20.8 5.7 %copy-start.16 = (bf16[2,512,128]{2,1,0:T(8,128)(2,1)}, bf16[2,512,128]{2,1,0:T(8,128)(2,1)S(1)}, u32[]{:S(2)}) copy-start(bf16[2,512,128]{2,1,0:T(8,128)(2,1)S(1)} %get-tuple-element.42.fr_lo_ref) | copy-start | bytes 786436
  26.6 27.9 %collective-permute-start.1 = (bf16[4,4,256,256]{3,2,1,0:T(8,128)(2,1)}, bf16[4,4,256,256]{3,2,1,0:T(8,128)(2,1)S(1)}, u32[]{:S(2)}, u32[]{:S(2)}) collective-permute-start(bf16[4,4,256,256]{3,2,1,0:T(8,128)(2,1)} %shard_map.125), channel_id=1, source_target_pairs={{0,8},{8,0},{16,24},{24,16},{32,40},{40,32},{48,56},{56,48},{64,72... | collective-permute-start | bytes 6291464 | tf_op jit(solution)/shard_map/ppermute | solution.py:390
  54.5 15.1 %copy-start.3 = (bf16[2048,512]{1,0:T(8,128)(2,1)S(1)}, bf16[2048,512]{1,0:T(8,128)(2,1)}, u32[]{:S(2)}) copy-start(bf16[2048,512]{1,0:T(8,128)(2,1)} %all-gather.3.cloned.1.call-done) | copy-start | bytes 6291460
  54.5 25.1 %collective-permute-start = (bf16[8,256,512]{2,1,0:T(8,128)(2,1)}, bf16[8,256,512]{2,1,0:T(8,128)(2,1)S(1)}, u32[]{:S(2)}, u32[]{:S(2)}) collective-permute-start(bf16[8,256,512]{2,1,0:T(8,128)(2,1)} %bitcast.15), channel_id=1, source_target_pairs={{0,8},{8,0},{16,24},{24,16},{32,40},{40,32},{48,56},{56,48},{64,72... | collective-permute-start | bytes 6291464 | tf_op jit(solution)/shard_map/ppermute | solution.py:375
  62.3 0.7 copy-start.20
  63.0 13.2 %copy-start.22 = (bf16[4,128,256]{2,1,0:T(8,128)(2,1)}, bf16[4,128,256]{2,1,0:T(8,128)(2,1)S(1)}, u32[]{:S(2)}) copy-start(bf16[4,128,256]{2,1,0:T(8,128)(2,1)S(1)} %get-tuple-element.64.refs_4_) | copy-start | bytes 786436
  63.0 13.3 %collective-permute-start.2 = (bf16[4,128,256]{2,1,0:T(8,128)(2,1)S(1)}, bf16[4,128,256]{2,1,0:T(8,128)(2,1)S(1)}, u32[]{:S(2)}, u32[]{:S(2)}) collective-permute-start(bf16[4,128,256]{2,1,0:T(8,128)(2,1)S(1)} %get-tuple-element.61), channel_id=1, source_target_pairs={{0,64},{8,72},{16,80},{24,88},{32,96},{40,104},{48,112},{56,120},{... | collective-permute-start | bytes 786440 | tf_op jit(solution)/shard_map/ppermute | solution.py:393
  64.5 28.7 %collective-permute-start.3 = (bf16[4,128,256]{2,1,0:T(8,128)(2,1)}, bf16[4,128,256]{2,1,0:T(8,128)(2,1)}, u32[]{:S(2)}, u32[]{:S(2)}) collective-permute-start(bf16[4,128,256]{2,1,0:T(8,128)(2,1)} %get-tuple-element.62), channel_id=1, source_target_pairs={{0,128},{8,136},{16,144},{24,152},{32,160},{40,168},{48,176},{56,1... | collective-permute-start | bytes 786440 | tf_op jit(solution)/shard_map/ppermute | solution.py:393
  65.6 27.6 %collective-permute-start.4 = (bf16[4,128,256]{2,1,0:T(8,128)(2,1)}, bf16[4,128,256]{2,1,0:T(8,128)(2,1)}, u32[]{:S(2)}, u32[]{:S(2)}) collective-permute-start(bf16[4,128,256]{2,1,0:T(8,128)(2,1)} %get-tuple-element.63), channel_id=1, source_target_pairs={{0,192},{8,200},{16,208},{24,216},{32,224},{40,232},{48,240},{56,2... | collective-permute-start | bytes 786440 | tf_op jit(solution)/shard_map/ppermute | solution.py:393
  67.7 12.4 %copy-start.17 = (bf16[2,512,128]{2,1,0:T(8,128)(2,1)S(1)}, bf16[2,512,128]{2,1,0:T(8,128)(2,1)}, u32[]{:S(2)}) copy-start(bf16[2,512,128]{2,1,0:T(8,128)(2,1)} %copy-done.16) | copy-start | bytes 786436
  67.7 25.5 %collective-permute-start.5 = (bf16[4,128,256]{2,1,0:T(8,128)(2,1)}, bf16[4,128,256]{2,1,0:T(8,128)(2,1)}, u32[]{:S(2)}, u32[]{:S(2)}) collective-permute-start(bf16[4,128,256]{2,1,0:T(8,128)(2,1)} %get-tuple-element.65), channel_id=1, source_target_pairs={{0,16},{8,24},{16,32},{24,40},{32,48},{40,56},{48,0},{56,8},{64,80... | collective-permute-start | bytes 786440 | tf_op jit(solution)/shard_map/ppermute | solution.py:394
  76.3 11.1 %copy-start.24 = (bf16[4,128,256]{2,1,0:T(8,128)(2,1)}, bf16[4,128,256]{2,1,0:T(8,128)(2,1)S(1)}, u32[]{:S(2)}) copy-start(bf16[4,128,256]{2,1,0:T(8,128)(2,1)S(1)} %collective-permute-done.2.refs_1_) | copy-start | bytes 786436
  76.3 17.0 %collective-permute-start.6 = (bf16[4,128,256]{2,1,0:T(8,128)(2,1)}, bf16[4,128,256]{2,1,0:T(8,128)(2,1)}, u32[]{:S(2)}, u32[]{:S(2)}) collective-permute-start(bf16[4,128,256]{2,1,0:T(8,128)(2,1)} %get-tuple-element.66), channel_id=1, source_target_pairs={{0,32},{8,40},{16,48},{24,56},{32,0},{40,8},{48,16},{56,24},{64,96... | collective-permute-start | bytes 786440 | tf_op jit(solution)/shard_map/ppermute | solution.py:394
  79.6 13.6 %collective-permute-start.7 = (bf16[4,128,256]{2,1,0:T(8,128)(2,1)}, bf16[4,128,256]{2,1,0:T(8,128)(2,1)}, u32[]{:S(2)}, u32[]{:S(2)}) collective-permute-start(bf16[4,128,256]{2,1,0:T(8,128)(2,1)} %get-tuple-element.67), channel_id=1, source_target_pairs={{0,48},{8,56},{16,0},{24,8},{32,16},{40,24},{48,32},{56,40},{64,11... | collective-permute-start | bytes 786440 | tf_op jit(solution)/shard_map/ppermute | solution.py:394
  87.3 0.7 copy-start.15
  88.1 0.7 copy-start.26
  88.8 21.1 %copy-start.2 = (f32[2,512,512]{2,1,0:T(8,128)S(1)}, f32[2,512,512]{2,1,0:T(8,128)}, u32[]{:S(2)}) copy-start(f32[2,512,512]{2,1,0:T(8,128)} %copy-done.1) | copy-start | bytes 6291460
  88.8 21.1 %copy-start.7 = (bf16[1,512,256]{2,1,0:T(8,128)(2,1)S(1)}, bf16[1,512,256]{2,1,0:T(8,128)(2,1)}, u32[]{:S(2)}) copy-start(bf16[1,512,256]{2,1,0:T(8,128)(2,1)} %param.10) | copy-start | bytes 786436
  88.8 30.8 %all-to-all-start = ((f32[8,72,128]{2,1,0:T(8,128)}), f32[8,72,128]{2,1,0:T(8,128)S(1)}, u32[]{:S(2)}, u32[]{:S(2)}) async-start(f32[8,72,128]{2,1,0:T(8,128)} %copy-done.15), calls=%async_computation | async-start | bytes 589824 | tf_op jit(solution)/shard_map/all_to_all | solution.py:408
  93.2 16.6 %copy-start.11 = (bf16[1,512,128]{2,1,0:T(8,128)(2,1)S(1)}, bf16[1,512,128]{2,1,0:T(8,128)(2,1)}, u32[]{:S(2)}) copy-start(bf16[1,512,128]{2,1,0:T(8,128)(2,1)} %param.11) | copy-start | bytes 393220
  93.3 1.0 copy-start.21
  94.2 0.9 copy-start.23
  95.2 0.9 copy-start.25
  96.1 13.7 %copy-start.29 = (bf16[1,512,128]{2,1,0:T(8,128)(2,1)S(1)}, bf16[1,512,128]{2,1,0:T(8,128)(2,1)}, u32[]{:S(2)}) copy-start(bf16[1,512,128]{2,1,0:T(8,128)(2,1)} %param.12) | copy-start | bytes 393220
  99.0 0.7 copy-start.34
  99.6 8.1 %collective-permute-start.8 = (f32[128,256]{1,0:T(8,128)S(1)}, f32[128,256]{1,0:T(8,128)S(1)}, u32[]{:S(2)}, u32[]{:S(2)}) collective-permute-start(f32[128,256]{1,0:T(8,128)S(1)} %get-tuple-element.69), channel_id=1, source_target_pairs={{0,16},{8,24},{16,32},{24,40},{32,48},{40,56},{48,0},{56,8},{64,80... | collective-permute-start | bytes 393224 | tf_op jit(solution)/shard_map/ppermute | solution.py:398
  100.2 20.0 %collective-permute-start.9 = (f32[128,256]{1,0:T(8,128)}, f32[128,256]{1,0:T(8,128)}, u32[]{:S(2)}, u32[]{:S(2)}) collective-permute-start(f32[128,256]{1,0:T(8,128)} %get-tuple-element.70), channel_id=1, source_target_pairs={{0,32},{8,40},{16,48},{24,56},{32,0},{40,8},{48,16},{56,24},{64,96... | collective-permute-start | bytes 393224 | tf_op jit(solution)/shard_map/ppermute | solution.py:398
  101.3 18.9 %collective-permute-start.10 = (f32[128,256]{1,0:T(8,128)}, f32[128,256]{1,0:T(8,128)}, u32[]{:S(2)}, u32[]{:S(2)}) collective-permute-start(f32[128,256]{1,0:T(8,128)} %get-tuple-element.71), channel_id=1, source_target_pairs={{0,48},{8,56},{16,0},{24,8},{32,16},{40,24},{48,32},{56,40},{64,11... | collective-permute-start | bytes 393224 | tf_op jit(solution)/shard_map/ppermute | solution.py:398
  102.9 17.4 %collective-permute-start.11 = (f32[128,256]{1,0:T(8,128)}, f32[128,256]{1,0:T(8,128)}, u32[]{:S(2)}, u32[]{:S(2)}) collective-permute-start(f32[128,256]{1,0:T(8,128)} %get-tuple-element.73), channel_id=1, source_target_pairs={{0,64},{8,72},{16,80},{24,88},{32,96},{40,104},{48,112},{56,120},{... | collective-permute-start | bytes 393224 | tf_op jit(solution)/shard_map/ppermute | solution.py:399
  105.8 14.4 %collective-permute-start.12 = (f32[128,256]{1,0:T(8,128)}, f32[128,256]{1,0:T(8,128)}, u32[]{:S(2)}, u32[]{:S(2)}) collective-permute-start(f32[128,256]{1,0:T(8,128)} %get-tuple-element.74), channel_id=1, source_target_pairs={{0,128},{8,136},{16,144},{24,152},{32,160},{40,168},{48,176},{56,1... | collective-permute-start | bytes 393224 | tf_op jit(solution)/shard_map/ppermute | solution.py:399
  107.7 0.6 copy-start.36
  108.3 11.9 %collective-permute-start.13 = (f32[128,256]{1,0:T(8,128)}, f32[128,256]{1,0:T(8,128)}, u32[]{:S(2)}, u32[]{:S(2)}) collective-permute-start(f32[128,256]{1,0:T(8,128)} %get-tuple-element.75), channel_id=1, source_target_pairs={{0,192},{8,200},{16,208},{24,216},{32,224},{40,232},{48,240},{56,2... | collective-permute-start | bytes 393224 | tf_op jit(solution)/shard_map/ppermute | solution.py:399
  109.8 1.2 copy-start.5
  111.1 1.0 copy-start.14
  112.1 0.9 copy-start.27
  113.0 0.9 copy-start.31
  118.0 0.8 copy-start.8
  118.8 0.7 copy-start.18
  119.5 56.0 %copy-start.12 = (bf16[1,512,128]{2,1,0:T(8,128)(2,1)S(1)}, bf16[1,512,128]{2,1,0:T(8,128)(2,1)}, u32[]{:S(2)}) copy-start(bf16[1,512,128]{2,1,0:T(8,128)(2,1)} %param.11) | copy-start | bytes 393220
  119.5 56.0 %copy-start.9 = (f32[512,256]{1,0:T(8,128)S(1)}, f32[512,256]{1,0:T(8,128)}, u32[]{:S(2)}) copy-start(f32[512,256]{1,0:T(8,128)} %copy-done.8) | copy-start | bytes 1572868
  119.5 56.0 %copy-start.19 = (f32[512,128]{1,0:T(8,128)S(1)}, f32[512,128]{1,0:T(8,128)}, u32[]{:S(2)}) copy-start(f32[512,128]{1,0:T(8,128)} %copy-done.18) | copy-start | bytes 786436
  120.2 11.6 %collective-permute-start.14 = (f32[8,128]{1,0:T(8,128)S(1)}, f32[8,128]{1,0:T(8,128)S(1)}, u32[]{:S(2)}, u32[]{:S(2)}) collective-permute-start(f32[8,128]{1,0:T(8,128)S(1)} %get-tuple-element.76), channel_id=1, source_target_pairs={{0,8},{8,0},{16,24},{24,16},{32,40},{40,32},{48,56},{56,48},{64,72... | collective-permute-start | bytes 12296 | tf_op jit(solution)/shard_map/ppermute | solution.py:425
  120.3 0.9 copy-start.33
  121.2 0.9 copy-start.35
  122.1 0.9 copy-start.37
  124.9 22.4 %all-to-all-start.2 = ((f32[8,32,256]{2,1,0:T(8,128)}), f32[8,32,256]{2,1,0:T(8,128)S(1)}, u32[]{:S(2)}, u32[]{:S(2)}) async-start(f32[8,32,256]{2,1,0:T(8,128)} %shard_map.128), calls=%async_computation.2 | async-start | bytes 524288 | tf_op jit(solution)/shard_map/all_to_all | solution.py:402
  131.9 4.9 %collective-permute-start.17 = (f32[8,128]{1,0:T(8,128)S(1)}, f32[8,128]{1,0:T(8,128)S(1)}, u32[]{:S(2)}, u32[]{:S(2)}) collective-permute-start(f32[8,128]{1,0:T(8,128)S(1)} %add.40), channel_id=1, source_target_pairs={{0,48},{8,56},{16,32},{24,40},{32,16},{40,24},{48,0},{56,8},{64,11... | collective-permute-start | bytes 12296 | tf_op jit(solution)/shard_map/ppermute | solution.py:427
  132.0 4.8 %collective-permute-start.16 = (f32[8,128]{1,0:T(8,128)S(1)}, f32[8,128]{1,0:T(8,128)S(1)}, u32[]{:S(2)}, u32[]{:S(2)}) collective-permute-start(f32[8,128]{1,0:T(8,128)S(1)} %add.40), channel_id=1, source_target_pairs={{0,16},{8,24},{16,0},{24,8},{32,48},{40,56},{48,32},{56,40},{64,80... | collective-permute-start | bytes 12296 | tf_op jit(solution)/shard_map/ppermute | solution.py:427
  133.8 5.1 %collective-permute-start.15 = (f32[8,128]{1,0:T(8,128)S(1)}, f32[8,128]{1,0:T(8,128)S(1)}, u32[]{:S(2)}, u32[]{:S(2)}) collective-permute-start(f32[8,128]{1,0:T(8,128)S(1)} %add.40), channel_id=1, source_target_pairs={{0,32},{8,40},{16,48},{24,56},{32,0},{40,8},{48,16},{56,24},{64,96... | collective-permute-start | bytes 12296 | tf_op jit(solution)/shard_map/ppermute | solution.py:427
  138.9 4.7 %collective-permute-start.20 = (f32[8,128]{1,0:T(8,128)S(1)}, f32[8,128]{1,0:T(8,128)S(1)}, u32[]{:S(2)}, u32[]{:S(2)}) collective-permute-start(f32[8,128]{1,0:T(8,128)S(1)} %add_add_fusion.1), channel_id=1, source_target_pairs={{0,192},{8,200},{16,208},{24,216},{32,224},{40,232},{48,240},{56,2... | collective-permute-start | bytes 12296 | tf_op jit(solution)/shard_map/ppermute | solution.py:427
  139.5 4.2 %collective-permute-start.19 = (f32[8,128]{1,0:T(8,128)S(1)}, f32[8,128]{1,0:T(8,128)S(1)}, u32[]{:S(2)}, u32[]{:S(2)}) collective-permute-start(f32[8,128]{1,0:T(8,128)S(1)} %add_add_fusion.1), channel_id=1, source_target_pairs={{0,64},{8,72},{16,80},{24,88},{32,96},{40,104},{48,112},{56,120},{... | collective-permute-start | bytes 12296 | tf_op jit(solution)/shard_map/ppermute | solution.py:427
  142.2 5.1 %collective-permute-start.18 = (f32[8,128]{1,0:T(8,128)S(1)}, f32[8,128]{1,0:T(8,128)S(1)}, u32[]{:S(2)}, u32[]{:S(2)}) collective-permute-start(f32[8,128]{1,0:T(8,128)S(1)} %add_add_fusion.1), channel_id=1, source_target_pairs={{0,128},{8,136},{16,144},{24,152},{32,160},{40,168},{48,176},{56,1... | collective-permute-start | bytes 12296 | tf_op jit(solution)/shard_map/ppermute | solution.py:427
  147.9 15.2 %all-to-all-start.3 = ((f32[8,8,128]{2,1,0:T(8,128)}), f32[8,8,128]{2,1,0:T(8,128)S(1)}, u32[]{:S(2)}, u32[]{:S(2)}) async-start(f32[8,8,128]{2,1,0:T(8,128)} %broadcast_in_dim.15), calls=%async_computation.3 | async-start | bytes 65536 | tf_op jit(solution)/shard_map/all_to_all | solution.py:429
  163.1 12.4 %all-to-all-start.1 = ((f32[8,32,128]{2,1,0:T(8,128)}), f32[8,32,128]{2,1,0:T(8,128)S(1)}, u32[]{:S(2)}, u32[]{:S(2)}) async-start(f32[8,32,128]{2,1,0:T(8,128)} %get-tuple-element.55), calls=%async_computation.1 | async-start | bytes 262144 | tf_op jit(solution)/shard_map/all_to_all | solution.py:419
  (1 other events, 0.6 us)
Sparse Core Ops, SparseCore 0:
  10.4 44.0 all-gather.2

commit v2 on v1

v2 whole, which is shorter than its diff:
```python
import functools

import jax
import jax.numpy as jnp
from jax import lax
from jax.experimental import pallas as pl
from jax.experimental.pallas import tpu as pltpu
from jax.sharding import PartitionSpec as P

F32 = jnp.float32
BF16 = jnp.bfloat16
T = 512
D = 8192
HP = 256
N = 128
ROWS = 128
PLANE = 16
DEPTH = 8
VMEM_LIMIT = 60 << 20


def dot(a, b, contract):
    return lax.dot_general(a, b, (contract, ((), ())), preferred_element_type=F32)


def nn(a, b):
    return dot(a, b, ((1,), (0,)))


def nt(a, b):
    return dot(a, b, ((1,), (1,)))


def tn(a, b):
    return dot(a, b, ((0,), (0,)))


def split(a):
    high = a.astype(BF16)
    return high, (a - high.astype(F32)).astype(BF16)


def call(kernel, outs, args, smem=(), hbm=(), scratch=(), flops=0, bytes_accessed=0):
    def whole(dims):
        return pl.BlockSpec(dims, lambda _: (0,) * len(dims))

    def spec(i, arg):
        if i in smem:
            return pl.BlockSpec(memory_space=pltpu.SMEM)
        return pl.BlockSpec(memory_space=pl.ANY) if i in hbm else whole(arg.shape)

    return pl.pallas_call(
        kernel,
        grid=(1,),
        out_shape=outs,
        in_specs=[spec(i, arg) for i, arg in enumerate(args)],
        out_specs=jax.tree.map(lambda out: whole(out.shape), outs),
        scratch_shapes=scratch,
        compiler_params=pltpu.CompilerParams(vmem_limit_bytes=VMEM_LIMIT),
        cost_estimate=pl.CostEstimate(
            flops=flops, bytes_accessed=bytes_accessed, transcendentals=0
        ),
    )(*args)


def shape(dims, kind=F32):
    return jax.ShapeDtypeStruct(dims, kind)


def counts(code):
    rows = lax.broadcasted_iota(jnp.int32, (T, T), 0)
    cols = lax.broadcasted_iota(jnp.int32, (T, T), 1)
    lower = jnp.where(rows >= cols, 1.0, 0.0).astype(BF16)
    pad = jnp.zeros((126, T), F32)
    high = jnp.concatenate([(code >> 8).astype(F32), pad], axis=0).astype(BF16)
    low = jnp.concatenate([(code & 255).astype(F32), pad], axis=0).astype(BF16)
    return lower, high, low, 256.0 * nt(lower, high) + nt(lower, low)


def payload_kernel(place_ref, rate_ref, half_ref, x_ref, inj_ref, code_ref, state_ref, pay_ref, chain_ref):
    pay_ref[:HP, :] = half_ref[...]
    count = counts(code_ref[...])[3]
    inject_f = inj_ref[...].astype(F32)
    for h in range(2):
        rate = rate_ref[h]
        x = x_ref[:, h * 128 : h * 128 + 128]
        end = count[T - 1 :, h : h + 1]
        span = -rate * (end - count[:, h : h + 1])
        b_hi, b_lo = split(span * jnp.exp(span) * inject_f)
        cum_end = -rate * end
        end_w = jnp.exp(cum_end)
        chain = tn(x, b_hi) + tn(x, b_lo) + (cum_end * end_w) * state_ref[h]
        chain_ref[h, :N, :] = chain
        chain_ref[h, N:, :] = jnp.broadcast_to(end_w, (8, 128))
        for k, term in enumerate(split(chain_ref[h])):
            at = (2 * k + h) * 128
            pay_ref[HP : HP + N + 8, at : at + 128] = term


def forward_kernel(
    rate_ref, x_ref, inj_ref, rd_ref, code_ref, state_ref,
    out_t_ref, mix_ref, wts_ref, part_ref, fr_ref, aux_ref,
):
    rows = lax.broadcasted_iota(jnp.int32, (T, T), 0)
    cols = lax.broadcasted_iota(jnp.int32, (T, T), 1)
    lower, high, low, count = counts(code_ref[...])
    upper = jnp.where(rows <= cols, 1.0, 0.0).astype(BF16)
    count_t = 256.0 * nn(high, upper) + nn(low, upper)
    inject = inj_ref[...]
    read = rd_ref[...]
    read_f = read.astype(F32)
    lane = lax.broadcasted_iota(jnp.int32, (T, 128), 1)
    aux = jnp.zeros((T, 128), F32)
    for h in range(2):
        rate = rate_ref[h]
        hs = slice(h * 128, h * 128 + 128)
        x = x_ref[:, hs]
        state = state_ref[h]
        s_hi, s_lo = split(state)
        cum = -rate * count[:, h : h + 1]
        start_w = jnp.exp(cum)
        to_end = jnp.exp(-rate * (count[T - 1 :, h : h + 1] - count[:, h : h + 1]))
        aux = jnp.where(lane == h, to_end, aux)
        aux = jnp.where(lane == 2 + h, start_w, aux)
        fr_ref[h] = (start_w * read_f).astype(BF16)
        carried = (nt(read, s_hi) + nt(read, s_lo)) * start_w
        weighted = carried * cum
        for i in range(T // ROWS):
            rs = slice(i * ROWS, i * ROWS + ROWS)
            width = (i + 1) * ROWS
            inter = nt(read[rs], inject[:width])
            spread = -rate * (count[rs, h : h + 1] - count_t[h : h + 1, :width])
            keep = rows[rs, :width] >= cols[rs, :width]
            spread = jnp.where(keep, spread, 0.0)
            wts = jnp.where(keep, jnp.exp(spread), 0.0)
            mixed = inter * wts
            narrow = mixed.astype(BF16)
            wts_ref[h, rs, :width] = wts
            r_hi, r_lo = split(mixed * spread)
            part_ref[rs, hs] = weighted[rs] + nn(r_hi, x[:width]) + nn(r_lo, x[:width])
            mix_ref[h, rs, :width] = narrow
            within = nn(narrow, x[:width])
            out = within + carried[rs]
            out_t_ref[hs, rs] = out.T.astype(BF16)
    aux_ref[...] = aux


def fetch(source, target, sem):
    copy = pltpu.make_async_copy(source, target, sem)
    copy.start()
    return copy


def weight_kernel(place_ref, out_t_ref, cot_ref, send_ref, keep_ref):
    core = place_ref[0]
    for k in range(4):
        for ref, side in ((send_ref, 1 - core), (keep_ref, core)):
            block = cot_ref[:, pl.ds(pl.multiple_of((2 * k + side) * 256, 256), 256)]
            ref[k] = nn(out_t_ref[...], block).astype(BF16)


def gridded(kernel, steps, in_specs, out_specs, outs, args, scratch=()):
    return pl.pallas_call(
        kernel,
        out_shape=outs,
        grid_spec=pltpu.PrefetchScalarGridSpec(
            num_scalar_prefetch=1,
            grid=(steps,),
            in_specs=in_specs,
            out_specs=out_specs,
            scratch_shapes=scratch,
        ),
        compiler_params=pltpu.CompilerParams(vmem_limit_bytes=VMEM_LIMIT),
        cost_estimate=pl.CostEstimate(flops=0, bytes_accessed=0, transcendentals=0),
    )(*args)


def fixed(dims):
    return pl.BlockSpec(dims, lambda i, place: (0,) * len(dims))


def core_sum_kernel(kept_ref, recv_ref, o_ref):
    o_ref[...] = (kept_ref[...].astype(F32) + recv_ref[...].astype(F32)).astype(BF16)


def plane_sum_kernel(in_ref, rate_ref, out_ref):
    for z in range(DEPTH):
        rs = slice(z * 32, z * 32 + 32)
        total = in_ref[0, rs, :].astype(F32)
        for k in range(1, PLANE):
            total = total + in_ref[k, rs, :].astype(F32)
        out_ref[z, :32, :] = total
        out_ref[z, 32:, :128] = rate_ref[...]
        out_ref[z, 32:, 128:] = rate_ref[...]


def depth_sum_kernel(tokens, in_ref, out_ref, rate_ref):
    total = in_ref[0]
    for k in range(1, DEPTH):
        total = total + in_ref[k]
    out_ref[...] = total[:32]
    rate_ref[...] = total[32:, :128] / tokens


def rate_vector_kernel(place_ref, part_ref, rd_ref, aux_ref, all_ref, o_ref, later_ref):
    for h in range(2):
        hs = slice(h * 128, h * 128 + 128)
        low = slice(256 + h * 128, 384 + h * 128)
        running = jnp.zeros((N, 128), F32)
        for c in range(DEPTH):
            term = all_ref[c, :, hs].astype(F32) + all_ref[c, :, low].astype(F32)
            decay = term[N : N + 1, :]
            later_ref[c, 8 * h : 8 * h + 8, :] = term[N:, :]
            running = jnp.where(c < place_ref[1], term[:N] + decay * running, running)
        q_hi, q_lo = split(running)
        through = nt(rd_ref[...], q_hi) + nt(rd_ref[...], q_lo)
        o_ref[:, hs] = part_ref[:, hs] + aux_ref[:, 2 + h : 3 + h] * through


def output_grad_kernel(place_ref, cot_ref, mine_ref, other_ref, fr_ref, og_ref, pay_ref, acc):
    core = place_ref[0]
    step = pl.program_id(0)
    total = None
    for k in range(2):
        first = cot_ref[:, pl.ds(pl.multiple_of((2 * k + core) * 512, 512), 512)]
        second = cot_ref[:, pl.ds(pl.multiple_of((2 * k + 1 - core) * 512, 512), 512)]
        terms = nt(first, mine_ref[k]) + nt(second, other_ref[k])
        total = terms if total is None else total + terms

    @pl.when(step == 0)
    def _():
        acc[...] = total

    @pl.when(step > 0)
    def _():
        acc[...] += total

    @pl.when(step == pl.num_programs(0) - 1)
    def _():
        grad = acc[...].astype(BF16)
        og_ref[...] = grad
        for h in range(2):
            hs = slice(h * 128, h * 128 + 128)
            narrow = tn(grad[:, hs], fr_ref[h]).astype(BF16)
            for z in range(DEPTH):
                pay_ref[z, hs, :] = narrow


def rate_kernel(og_ref, vec_ref, rate_ref):
    rates = []
    for h in range(2):
        hs = slice(h * 128, h * 128 + 128)
        rate = jnp.sum(og_ref[:, hs].astype(F32) * vec_ref[:, hs], axis=0, keepdims=True)
        rates.append(jnp.broadcast_to(jnp.sum(rate, axis=1, keepdims=True), (1, 128)))
    rate_ref[...] = jnp.concatenate(rates + [jnp.zeros((6, 128), F32)], axis=0)


def backward_kernel(
    g_ref, x_ref, inj_ref, rd_ref, state_ref, mix_ref, wts_ref, aux_ref, gi_ref, ginj_ref,
    gread_ref,
):
    inject = inj_ref[...]
    read = rd_ref[...]
    gi_ref[...] = jnp.zeros((T, HP), F32)
    ginj_ref[...] = jnp.zeros((T, N), F32)
    for h in range(2):
        hs = slice(h * 128, h * 128 + 128)
        x = x_ref[:, hs]
        g = g_ref[:, hs]
        state = state_ref[h].astype(BF16)
        for i in range(T // ROWS):
            rs = slice(i * ROWS, i * ROWS + ROWS)
            width = (i + 1) * ROWS
            pairing = (nt(g[rs], x[:width]) * wts_ref[h, rs, :width]).astype(BF16)
            through = nn(g[rs], state) * aux_ref[rs, 2 + h : 3 + h]
            read_part = nn(pairing, inject[:width]) + through
            if h == 0:
                gread_ref[rs, :] = read_part
            else:
                gread_ref[rs, :] += read_part
            ginj_ref[:width, :] += tn(pairing, read[rs])
            gi_ref[:width, hs] += tn(mix_ref[h, rs, :width], g[rs])


def finish_kernel(
    place_ref, gi_ref, ginj_ref, x_ref, inj_ref, aux_ref, adj_ref, decay_ref, o_gi_ref, o_ginj_ref,
):
    total = ginj_ref[...]
    inject = inj_ref[...]
    for h in range(2):
        hs = slice(h * 128, h * 128 + 128)
        running = jnp.zeros((128, N), F32)
        for c in range(DEPTH - 1, 0, -1):
            decay = decay_ref[c, 8 * h : 8 * h + 1, :]
            later = adj_ref[c, hs, :].astype(F32) + decay * running
            running = jnp.where(c > place_ref[1], later, running)
        incoming = running.astype(BF16)
        to_end = aux_ref[:, h : h + 1]
        o_gi_ref[:, hs] = (gi_ref[:, hs] + to_end * nt(inject, incoming)).astype(BF16)
        total = total + to_end * nn(x_ref[:, hs], incoming)
    o_ginj_ref[...] = total


def swap_cores(value):
    return lax.ppermute(value, "dp", [(i, i ^ 1) for i in range(2 * PLANE)])


def local(
    cotangent, out_weight, head_input, injector, readout, decay_code, decay_rate, start_state
):
    cot = cotangent[0]
    x = head_input[0]
    inject = injector[0]
    read = readout[0]
    state = start_state[0, 0]
    code = decay_code[0]
    core = lax.axis_index("dp") % 2
    place = jnp.stack([core, lax.axis_index("ctx")]).astype(jnp.int32)

    pay, chain = gridded(
        payload_kernel, 1,
        [
            pl.BlockSpec(memory_space=pltpu.SMEM),
            pl.BlockSpec((HP, 512), lambda i, place: (0, place[0])),
            fixed((T, HP)), fixed((T, N)), fixed((2, T)), fixed((2, N, N)),
        ],
        [fixed((HP + N + 8, 512)), fixed((2, N + 8, 128))],
        [shape((HP + N + 8, 512), BF16), shape((2, N + 8, 128))],
        (place, decay_rate, out_weight, x, inject, code.T, state),
    )
    gathered = lax.all_gather(pay, "ctx", axis=0)
    x, _ = lax.optimization_barrier((x, chain))
    out_t, mix, wts, part, from_start, aux = call(
        forward_kernel,
        [
            shape((HP, T), BF16), shape((2, T, T), BF16), shape((2, T, T)), shape((T, HP)),
            shape((2, T, N), BF16), shape((T, 128)),
        ],
        (decay_rate, x, inject, read, code.T, state), smem=(0,),
    )
    half_terms = shape((PLANE, 256, 256), BF16)
    quarter = pl.BlockSpec((4, 256, 256), lambda i, place: (i, 0, 0))
    sent, kept = gridded(
        weight_kernel, 4,
        [fixed((HP, T)), pl.BlockSpec((T, 2048), lambda i, place: (0, i))],
        [quarter, quarter], [half_terms, half_terms], (place, out_t, cot),
    )
    blocks = call(core_sum_kernel, half_terms, (kept, swap_cores(sent)))
    groups = [[2 * k + c for k in range(PLANE)] for c in range(2)]
    swapped = lax.all_to_all(blocks, "dp", 0, 0, tiled=True, axis_index_groups=groups)

    gathered, _ = lax.optimization_barrier((gathered, swapped))
    mine = gathered[:, :HP, :]
    other = swap_cores(mine)
    vector, decay = call(
        rate_vector_kernel, [shape((T, HP)), shape((DEPTH, 16, 128))],
        (place, part, read, aux, gathered[:, HP:, :]), smem=(0,),
    )
    from_start, _ = lax.optimization_barrier((from_start, vector))
    pair = pl.BlockSpec((2, HP, 512), lambda i, place: (i, 0, 0))
    grad, pay = gridded(
        output_grad_kernel, 4,
        [pl.BlockSpec((T, 2048), lambda i, place: (0, i)), pair, pair, fixed((2, T, N))],
        [fixed((T, HP)), fixed((DEPTH, HP, 128))],
        [shape((T, HP), BF16), shape((DEPTH, HP, 128), BF16)],
        (place, cot, mine, other, from_start), [pltpu.VMEM((T, HP), F32)],
    )
    pay = lax.all_to_all(pay, "ctx", 0, 0, tiled=True)
    rate = plane_total(call(rate_kernel, shape((8, 128)), (grad, vector)))
    gi, ginj, grad_read = call(
        backward_kernel, [shape((T, HP)), shape((T, N)), shape((T, N))],
        (grad, x, inject, read, state, mix, wts, aux),
    )
    swapped, _ = lax.optimization_barrier((swapped, gi))
    blocks = call(plane_sum_kernel, shape((DEPTH, 40, 256)), (swapped, rate))
    blocks, _ = lax.optimization_barrier((blocks, pay))
    blocks = lax.all_to_all(blocks, "ctx", 0, 0, tiled=True)
    grad_input, grad_inject = call(
        finish_kernel, [shape((T, HP), BF16), shape((T, N))],
        (place, gi, ginj, x, inject, aux, pay, decay), smem=(0,),
    )
    tokens = T * lax.axis_size("dp") * lax.axis_size("ctx")
    grad_weight, rate = call(
        functools.partial(depth_sum_kernel, tokens), [shape((32, 256)), shape((8, 128))],
        (blocks,),
    )
    return grad_input[None], grad_inject[None], grad_read[None], grad_weight, rate[:2, 0]


def flipped(value, bits):
    return lax.ppermute(value, "dp", [(i, i ^ bits) for i in range(2 * PLANE)])


def plane_total(value):
    value = value + flipped(value, 1)
    for unit in (2, 8):
        one, two, three = (flipped(value, unit * k) for k in (1, 2, 3))
        value = (value + two) + (one + three)
    return value


def solution(mesh):
    in_specs = (
        P("dp", "ctx", None),
        P(None, "ctx"),
        P("dp", "ctx", None),
        P("dp", "ctx", None),
        P("dp", "ctx", None),
        P("dp", "ctx", None),
        P(),
        P("dp", "ctx", None, None, None),
    )
    out_specs = (
        P("dp", "ctx", None),
        P("dp", "ctx", None),
        P("dp", "ctx", None),
        P("ctx", "dp"),
        P(),
    )
    return jax.shard_map(local, mesh=mesh, in_specs=in_specs, out_specs=out_specs, check_vma=False)
```

time: 185 us -> 146 us (0.79)
  blocking collectives: 0 us -> 34 us
  waiting for transfers between devices: 50.8 us -> 17.3 us
  starting transfers between devices: 50.3 us -> 24 us
  local copies, waits for them, and re-layouts: 25.8 us -> 8.06 us
  Pallas kernels: 41.5 us -> 45 us
    all_to_all x0 -> x1, blocking collectives: none -> 34 us  [local(): lax.all_to_all(blocks, 'dp', 0, 0, tiled=True, axis_index_groups=groups)]
    all_gather x1, waiting for transfers between devices: 27.8 us -> 0.01 us  [local(): gathered = lax.all_gather(pay, 'ctx', axis=0)]
    unnamed x79 -> x8, local copies, waits for them, and re-layouts: 23.7 us -> 2.03 us
    ppermute x21 -> x9, starting transfers between devices: 28.2 us -> 8.29 us  [the longest x7 8.19 us: flipped(): return lax.ppermute(value, 'dp', [(i, i ^ bits) for i in range(2 * PLANE)])]
    all_to_all x2 -> x0, waiting for transfers between devices: 15.8 us -> none  [the longest x1 8.36 us: local(): incoming = lax.all_to_all(incoming, 'ctx', 0, 0, tiled=True)]
    all_to_all x2 -> x0, starting transfers between devices: 10.6 us -> none  [the longest x1 7.2 us: local(): lax.all_to_all(jnp.broadcast_to(rate, (DEPTH, 8, 128)), 'ctx', 0, 0, tile...]
    all_to_all x1, waiting for transfers between devices: 0.01 us -> 8.73 us  [local(): blocks = lax.all_to_all(blocks, 'ctx', 0, 0, tiled=True)]
    slice x0 -> x3, local copies, waits for them, and re-layouts: none -> 6.03 us  [the longest x1 3.01 us: local(): gathered[:, HP:, :]]
  transfers between devices with their start and end apart: 26 -> 12, of which waited for: 8 -> 6; matrix products, arithmetic and copies ran while one was open for 1% -> 3% of each run, Pallas kernels for 22% -> 22%
where the time goes in v2:
time: 146 us; the launch traced here: 144 us
  Pallas kernels  45 us (31%)
  blocking collectives  34 us (23%)
  starting transfers between devices  24 us (16%)
  waiting for transfers between devices  17.3 us (12%)
  between operations  14.1 us (10%)
  local copies, waits for them, and re-layouts  8.06 us (6%)
  other arithmetic  1.93 us (1%)
    all_to_all x1, blocking collectives, local(): lax.all_to_all(blocks, 'dp', 0, 0, tiled=True, axis_index_groups=groups)  34 us
    pallas_call x8, Pallas kernels, call(): pl.pallas_call(kernel, grid=(1,), out_shape=outs, in_specs=[spec(i, arg)...  25.2 us
    pallas_call x3, Pallas kernels, gridded(): pl.pallas_call(kernel, out_shape=outs, grid_spec=pltpu.PrefetchScalarGrid...  19.7 us
    all_to_all x1, waiting for transfers between devices, local(): blocks = lax.all_to_all(blocks, 'ctx', 0, 0, tiled=True)  8.73 us
    all_to_all x1, starting transfers between devices, local(): pay = lax.all_to_all(pay, 'ctx', 0, 0, tiled=True)  8.5 us
    ppermute x7, starting transfers between devices, flipped(): return lax.ppermute(value, 'dp', [(i, i ^ bits) for i in range(2 * PLANE)])  8.19 us
    all_to_all x1, starting transfers between devices, local(): blocks = lax.all_to_all(blocks, 'ctx', 0, 0, tiled=True)  7.21 us
    ppermute x2, waiting for transfers between devices, swap_cores(): return lax.ppermute(value, 'dp', [(i, i ^ 1) for i in range(2 * PLANE)])  4.37 us
  transfers between devices with their start and end apart: 12, of which 6 were waited for; matrix products, arithmetic and copies ran while one was open for 3% of the time, Pallas kernels for 22%

profile of v2, /device:TPU:2, one launch (start us, length us, event | category | flops | bytes accessed | tf_op | source)
XLA Modules:
  0.0 144.3 jit_solution(4208651524246424026)
XLA Ops:
  7.2 0.0 all-gather.3.cloned.1.call-start
  7.2 0.6 pad_add_fusion.place_ref
  7.9 3.5 %shard_map.119 = (bf16[392,512]{1,0:T(8,128)(2,1)}, f32[2,136,128]{2,1,0:T(8,128)}) custom-call(s32[2]{0:T(128)} %pad_add_fusion.place_ref, f32[2]{0:T(128)} %rate_ref.3, bf16[256,1024]{1,0:T(8,128)(2,1)} %half_ref.1, bf16[512,256]{1,0:T(8,128)(2,1)} %bitcast.16, bf16[512,128]{1,0:T(8,128)(2,1)} %bitcast.22, s32[2,512]{1,0:T(2,128)} %bitcast.32, ...), custom_call_target="tpu_custom_call" | custom-call | tf_op jit(solution)/shard_map/pallas_call | solution.py:163
  11.3 0.0 all-gather.3.cloned.1.call-update
  11.3 4.6 %shard_map.120 = (bf16[256,512]{1,0:T(8,128)(2,1)}, bf16[2,512,512]{2,1,0:T(8,128)(2,1)}, f32[2,512,512]{2,1,0:T(8,128)}, f32[512,256]{1,0:T(8,128)}, bf16[2,512,128]{2,1,0:T(8,128)(2,1)}, /*index=5*/f32[512,128]{1,0:T(8,128)}) custom-call(f32[2]{0:T(128)} %rate_ref.3, bf16[512,256]{1,0:T(8,128)(2,1)} %bitcast.17, bf16[512,128]{1,0:T(8,128)(2,1)} %bitcast.23, ...), custom_call_target="tpu_custom_call" | custom-call | tf_op jit(solution)/shard_map/pallas_call | solution.py:52
  15.9 7.8 %shard_map.121 = (bf16[16,256,256]{2,1,0:T(8,128)(2,1)}, bf16[16,256,256]{2,1,0:T(8,128)(2,1)}) custom-call(s32[2]{0:T(128)} %pad_add_fusion.place_ref, bf16[256,512]{1,0:T(8,128)(2,1)} %get-tuple-element.30.out_t_ref, bf16[512,8192]{1,0:T(8,128)(2,1)} %bitcast.14), custom_call_target="tpu_custom_call" | custom-call | tf_op jit(solution)/shard_map/pallas_call | solution.py:163
  23.8 0.0 collective-permute-start
  23.8 4.4 %collective-permute-done.recv_ref = bf16[16,256,256]{2,1,0:T(8,128)(2,1)S(1)} collective-permute-done((bf16[16,256,256]{2,1,0:T(8,128)(2,1)}, bf16[16,256,256]{2,1,0:T(8,128)(2,1)S(1)}, u32[]{:S(2)}, u32[]{:S(2)}) %collective-permute-start) | collective-permute-done | bytes 2097184 | tf_op jit(solution)/shard_map/ppermute | solution.py:305
  28.2 0.0 copy-start.1
  28.2 1.3 copy-done.1
  29.5 4.1 %shard_map.122 = bf16[16,256,256]{2,1,0:T(8,128)(2,1)} custom-call(bf16[16,256,256]{2,1,0:T(8,128)(2,1)} %get-tuple-element.31.kept_ref, bf16[16,256,256]{2,1,0:T(8,128)(2,1)} %copy-done.1), custom_call_target="tpu_custom_call" | custom-call | tf_op jit(solution)/shard_map/pallas_call | solution.py:52
  33.6 34.0 %all_to_all.15.in_ref = bf16[16,256,256]{2,1,0:T(8,128)(2,1)} all-to-all(bf16[16,256,256]{2,1,0:T(8,128)(2,1)} %shard_map.122), channel_id=1, replica_groups={{0,16,32,48,64,80,96,112,128,144,160,176,192,208,224,240},{8,24,40,56,7..., dimensions={0} | all-to-all | bytes 4194304 | tf_op jit(solution)/shard_map/all_to_all | solution.py:350
  67.5 0.0 all-gather.3.cloned.1.call-done
  67.5 1.7 %slice.9.mine_ref = bf16[8,256,512]{2,1,0:T(8,128)(2,1)S(1)} slice(bf16[8,392,512]{2,1,0:T(8,128)(2,1)} %bitcast.20), slice={[0:8], [0:256], [0:512]} | slice | bytes 4194304 | tf_op jit(solution)/shard_map/slice | solution.py:353
  69.2 0.0 copy-start
  69.3 0.1 collective-permute-start.1
  69.4 3.0 %slice.10.all_ref = bf16[8,136,512]{2,1,0:T(8,128)(2,1)} slice(bf16[8,392,512]{2,1,0:T(8,128)(2,1)} %bitcast.21), slice={[0:8], [256:392], [0:512]} | slice | bytes 2228224 | tf_op jit(solution)/shard_map/slice | solution.py:357
  72.4 2.9 %shard_map.123 = (f32[512,256]{1,0:T(8,128)}, f32[8,16,128]{2,1,0:T(8,128)}) custom-call(s32[2]{0:T(128)} %pad_add_fusion.place_ref, f32[512,256]{1,0:T(8,128)} %get-tuple-element.35.part_ref, bf16[512,128]{1,0:T(8,128)(2,1)} %bitcast.30, f32[512,128]{1,0:T(8,128)} %get-tuple-element.36.aux_ref, bf16[8,136,512]{2,1,0:T(8,128)(2,1)} %slice.10.all_ref), custom_call_target="tpu_custom_call" | custom-call | tf_op jit(solution)/shard_map/pallas_call | solution.py:52
  75.2 0.0 copy-done
  75.2 0.0 collective-permute-done.1.other_ref
  75.3 8.4 %shard_map.124 = (bf16[512,256]{1,0:T(8,128)(2,1)}, bf16[8,256,128]{2,1,0:T(8,128)(2,1)}) custom-call(s32[2]{0:T(128)} %pad_add_fusion.place_ref, bf16[512,8192]{1,0:T(8,128)(2,1)} %bitcast.15, bf16[8,256,512]{2,1,0:T(8,128)(2,1)} %copy-done, bf16[8,256,512]{2,1,0:T(8,128)(2,1)} %collective-permute-done.1.other_ref, ...), custom_call_target="tpu_custom_call" | custom-call | tf_op jit(solution)/shard_map/pallas_call | solution.py:163
  83.7 8.5 %all-to-all-start.1 = ((bf16[8,256,128]{2,1,0:T(8,128)(2,1)}), bf16[8,256,128]{2,1,0:T(8,128)(2,1)S(1)}, u32[]{:S(2)}, u32[]{:S(2)}) async-start(bf16[8,256,128]{2,1,0:T(8,128)(2,1)} %get-tuple-element.44), calls=%async_computation.1 | async-start | bytes 1048576 | tf_op jit(solution)/shard_map/all_to_all | solution.py:368
  92.2 1.9 %shard_map.127 = f32[8,128]{1,0:T(8,128)} custom-call(bf16[512,256]{1,0:T(8,128)(2,1)} %get-tuple-element.39.g_ref.og_ref, f32[512,256]{1,0:T(8,128)} %get-tuple-element.37.vec_ref), custom_call_target="tpu_custom_call" | custom-call | tf_op jit(solution)/shard_map/pallas_call | solution.py:52
  94.1 0.0 collective-permute-start.2
  94.1 1.4 collective-permute-done.2
  95.5 0.7 add.26
  96.1 1.8 %collective-permute-start.3 = (f32[8,128]{1,0:T(8,128)S(1)}, f32[8,128]{1,0:T(8,128)S(1)}, u32[]{:S(2)}, u32[]{:S(2)}) collective-permute-start(f32[8,128]{1,0:T(8,128)S(1)} %add.26), channel_id=1, source_target_pairs={{0,32},{8,40},{16,48},{24,56},{32,0},{40,8},{48,16},{56,24},{64,96... | collective-permute-start | bytes 12296 | tf_op jit(solution)/shard_map/ppermute | solution.py:391
  97.9 0.3 collective-permute-start.4
  98.2 2.1 %collective-permute-start.5 = (f32[8,128]{1,0:T(8,128)S(1)}, f32[8,128]{1,0:T(8,128)S(1)}, u32[]{:S(2)}, u32[]{:S(2)}) collective-permute-start(f32[8,128]{1,0:T(8,128)S(1)} %add.26), channel_id=1, source_target_pairs={{0,48},{8,56},{16,32},{24,40},{32,16},{40,24},{48,0},{56,8},{64,11... | collective-permute-start | bytes 12296 | tf_op jit(solution)/shard_map/ppermute | solution.py:391
  100.2 1.0 collective-permute-done.3
  101.3 0.3 collective-permute-done.4
  101.5 1.5 %collective-permute-done.5 = f32[8,128]{1,0:T(8,128)S(1)} collective-permute-done((f32[8,128]{1,0:T(8,128)S(1)}, f32[8,128]{1,0:T(8,128)S(1)}, u32[]{:S(2)}, u32[]{:S(2)}) %collective-permute-start.5) | collective-permute-done | bytes 4128 | tf_op jit(solution)/shard_map/ppermute | solution.py:391
  103.0 1.8 %collective-permute-start.6 = (f32[8,128]{1,0:T(8,128)S(1)}, f32[8,128]{1,0:T(8,128)S(1)}, u32[]{:S(2)}, u32[]{:S(2)}) collective-permute-start(f32[8,128]{1,0:T(8,128)S(1)} %add_add_fusion.1), channel_id=1, source_target_pairs={{0,128},{8,136},{16,144},{24,152},{32,160},{40,168},{48,176},{56,1... | collective-permute-start | bytes 12296 | tf_op jit(solution)/shard_map/ppermute | solution.py:391
  104.8 1.5 %collective-permute-start.7 = (f32[8,128]{1,0:T(8,128)S(1)}, f32[8,128]{1,0:T(8,128)S(1)}, u32[]{:S(2)}, u32[]{:S(2)}) collective-permute-start(f32[8,128]{1,0:T(8,128)S(1)} %add_add_fusion.1), channel_id=1, source_target_pairs={{0,64},{8,72},{16,80},{24,88},{32,96},{40,104},{48,112},{56,120},{... | collective-permute-start | bytes 12296 | tf_op jit(solution)/shard_map/ppermute | solution.py:391
  106.3 0.8 collective-permute-start.8
  107.1 4.9 %shard_map.125 = (f32[512,256]{1,0:T(8,128)}, f32[512,128]{1,0:T(8,128)}, f32[512,128]{1,0:T(8,128)}) custom-call(bf16[512,256]{1,0:T(8,128)(2,1)} %get-tuple-element.39.g_ref.og_ref, bf16[512,256]{1,0:T(8,128)(2,1)} %bitcast.18, bf16[512,128]{1,0:T(8,128)(2,1)} %bitcast.24, bf16[512,128]{1,0:T(8,128)(2,1)} %bitcast.31, f32[2,128,128]{2,1,0:T(8,128)} %bitcast.28, ...), custom_call_target="tpu_custom_call" | custom-call | tf_op jit(solution)/shard_map/pallas_call | solution.py:52
  112.0 0.0 collective-permute-done.6
  112.0 0.0 collective-permute-done.7
  112.0 0.0 collective-permute-done.8
  112.0 0.6 add_add_fusion.rate_ref
  112.6 2.6 %shard_map.128 = f32[8,40,256]{2,1,0:T(8,128)} custom-call(bf16[16,256,256]{2,1,0:T(8,128)(2,1)} %all_to_all.15.in_ref, f32[8,128]{1,0:T(8,128)} %add_add_fusion.rate_ref), custom_call_target="tpu_custom_call" | custom-call | tf_op jit(solution)/shard_map/pallas_call | solution.py:52
  115.2 0.0 all-to-all-done.1.adj_ref
  115.2 0.0 copy-start.2
  115.2 7.2 %all-to-all-start.2 = ((f32[8,40,256]{2,1,0:T(8,128)}), f32[8,40,256]{2,1,0:T(8,128)S(1)}, u32[]{:S(2)}, u32[]{:S(2)}) async-start(f32[8,40,256]{2,1,0:T(8,128)} %shard_map.128), calls=%async_computation.2 | async-start | bytes 655360 | tf_op jit(solution)/shard_map/all_to_all | solution.py:377
  122.4 0.0 copy-done.2
  122.4 2.6 %shard_map.126 = (bf16[512,256]{1,0:T(8,128)(2,1)}, f32[512,128]{1,0:T(8,128)}) custom-call(s32[2]{0:T(128)} %pad_add_fusion.place_ref, f32[512,256]{1,0:T(8,128)} %get-tuple-element.42.gi_ref, f32[512,128]{1,0:T(8,128)} %get-tuple-element.43.ginj_ref, bf16[512,256]{1,0:T(8,128)(2,1)} %bitcast.19, bf16[512,128]{1,0:T(8,128)(2,1)} %bitcast.25, ...), custom_call_target="tpu_custom_call" | custom-call | tf_op jit(solution)/shard_map/pallas_call | solution.py:52
  125.1 8.7 %all-to-all-done.2.in_ref = f32[8,40,256]{2,1,0:T(8,128)S(1)} async-done(((f32[8,40,256]{2,1,0:T(8,128)}), f32[8,40,256]{2,1,0:T(8,128)S(1)}, u32[]{:S(2)}, u32[]{:S(2)}) %all-to-all-start.2) | async-done | bytes 327712 | tf_op jit(solution)/shard_map/all_to_all | solution.py:377
  133.8 0.0 copy-start.3
  133.8 0.7 copy-done.3
  134.5 1.6 %shard_map.129 = (f32[32,256]{1,0:T(8,128)}, f32[8,128]{1,0:T(8,128)}) custom-call(f32[8,40,256]{2,1,0:T(8,128)} %copy-done.3), custom_call_target="tpu_custom_call" | custom-call | tf_op jit(solution)/shard_map/pallas_call | solution.py:52
  136.1 1.3 slice_reduce_fusion
  (1 shorter events, 0.0 us)
Async XLA Ops:
  7.2 60.3 %all-gather.3.cloned.1.call-start = ((), (), s32[]{:S(2)}) async-start(), calls=%async_computation.3 | async-start | bytes 3612672 | tf_op jit(solution)/shard_map/all_gather | solution.py:331
  23.8 4.4 %collective-permute-start = (bf16[16,256,256]{2,1,0:T(8,128)(2,1)}, bf16[16,256,256]{2,1,0:T(8,128)(2,1)S(1)}, u32[]{:S(2)}, u32[]{:S(2)}) collective-permute-start(bf16[16,256,256]{2,1,0:T(8,128)(2,1)} %get-tuple-element.32), channel_id=1, source_target_pairs={{0,8},{8,0},{16,24},{24,16},{32,40},{40,32},{48,56},{56,48},{64,72... | collective-permute-start | bytes 6291464 | tf_op jit(solution)/shard_map/ppermute | solution.py:305
  28.2 1.3 copy-start.1
  69.2 6.0 %copy-start = (bf16[8,256,512]{2,1,0:T(8,128)(2,1)}, bf16[8,256,512]{2,1,0:T(8,128)(2,1)S(1)}, u32[]{:S(2)}) copy-start(bf16[8,256,512]{2,1,0:T(8,128)(2,1)S(1)} %slice.9.mine_ref) | copy-start | bytes 6291460
  69.3 6.0 %collective-permute-start.1 = (bf16[8,256,512]{2,1,0:T(8,128)(2,1)S(1)}, bf16[8,256,512]{2,1,0:T(8,128)(2,1)}, u32[]{:S(2)}, u32[]{:S(2)}) collective-permute-start(bf16[8,256,512]{2,1,0:T(8,128)(2,1)S(1)} %slice.9.mine_ref), channel_id=1, source_target_pairs={{0,8},{8,0},{16,24},{24,16},{32,40},{40,32},{48,56},{56,48},{64,72... | collective-permute-start | bytes 6291464 | tf_op jit(solution)/shard_map/ppermute | solution.py:305
  83.7 31.5 %all-to-all-start.1 = ((bf16[8,256,128]{2,1,0:T(8,128)(2,1)}), bf16[8,256,128]{2,1,0:T(8,128)(2,1)S(1)}, u32[]{:S(2)}, u32[]{:S(2)}) async-start(bf16[8,256,128]{2,1,0:T(8,128)(2,1)} %get-tuple-element.44), calls=%async_computation.1 | async-start | bytes 1048576 | tf_op jit(solution)/shard_map/all_to_all | solution.py:368
  94.1 1.4 collective-permute-start.2
  96.1 5.1 %collective-permute-start.3 = (f32[8,128]{1,0:T(8,128)S(1)}, f32[8,128]{1,0:T(8,128)S(1)}, u32[]{:S(2)}, u32[]{:S(2)}) collective-permute-start(f32[8,128]{1,0:T(8,128)S(1)} %add.26), channel_id=1, source_target_pairs={{0,32},{8,40},{16,48},{24,56},{32,0},{40,8},{48,16},{56,24},{64,96... | collective-permute-start | bytes 12296 | tf_op jit(solution)/shard_map/ppermute | solution.py:391
  97.9 3.6 %collective-permute-start.4 = (f32[8,128]{1,0:T(8,128)S(1)}, f32[8,128]{1,0:T(8,128)S(1)}, u32[]{:S(2)}, u32[]{:S(2)}) collective-permute-start(f32[8,128]{1,0:T(8,128)S(1)} %add.26), channel_id=1, source_target_pairs={{0,16},{8,24},{16,0},{24,8},{32,48},{40,56},{48,32},{56,40},{64,80... | collective-permute-start | bytes 12296 | tf_op jit(solution)/shard_map/ppermute | solution.py:391
  98.2 4.8 %collective-permute-start.5 = (f32[8,128]{1,0:T(8,128)S(1)}, f32[8,128]{1,0:T(8,128)S(1)}, u32[]{:S(2)}, u32[]{:S(2)}) collective-permute-start(f32[8,128]{1,0:T(8,128)S(1)} %add.26), channel_id=1, source_target_pairs={{0,48},{8,56},{16,32},{24,40},{32,16},{40,24},{48,0},{56,8},{64,11... | collective-permute-start | bytes 12296 | tf_op jit(solution)/shard_map/ppermute | solution.py:391
  103.0 9.0 %collective-permute-start.6 = (f32[8,128]{1,0:T(8,128)S(1)}, f32[8,128]{1,0:T(8,128)S(1)}, u32[]{:S(2)}, u32[]{:S(2)}) collective-permute-start(f32[8,128]{1,0:T(8,128)S(1)} %add_add_fusion.1), channel_id=1, source_target_pairs={{0,128},{8,136},{16,144},{24,152},{32,160},{40,168},{48,176},{56,1... | collective-permute-start | bytes 12296 | tf_op jit(solution)/shard_map/ppermute | solution.py:391
  104.8 7.2 %collective-permute-start.7 = (f32[8,128]{1,0:T(8,128)S(1)}, f32[8,128]{1,0:T(8,128)S(1)}, u32[]{:S(2)}, u32[]{:S(2)}) collective-permute-start(f32[8,128]{1,0:T(8,128)S(1)} %add_add_fusion.1), channel_id=1, source_target_pairs={{0,64},{8,72},{16,80},{24,88},{32,96},{40,104},{48,112},{56,120},{... | collective-permute-start | bytes 12296 | tf_op jit(solution)/shard_map/ppermute | solution.py:391
  106.3 5.7 %collective-permute-start.8 = (f32[8,128]{1,0:T(8,128)S(1)}, f32[8,128]{1,0:T(8,128)S(1)}, u32[]{:S(2)}, u32[]{:S(2)}) collective-permute-start(f32[8,128]{1,0:T(8,128)S(1)} %add_add_fusion.1), channel_id=1, source_target_pairs={{0,192},{8,200},{16,208},{24,216},{32,224},{40,232},{48,240},{56,2... | collective-permute-start | bytes 12296 | tf_op jit(solution)/shard_map/ppermute | solution.py:391
  115.2 7.2 %copy-start.2 = (bf16[8,256,128]{2,1,0:T(8,128)(2,1)}, bf16[8,256,128]{2,1,0:T(8,128)(2,1)S(1)}, u32[]{:S(2)}) copy-start(bf16[8,256,128]{2,1,0:T(8,128)(2,1)S(1)} %all-to-all-done.1.adj_ref) | copy-start | bytes 1572868
  115.2 18.6 %all-to-all-start.2 = ((f32[8,40,256]{2,1,0:T(8,128)}), f32[8,40,256]{2,1,0:T(8,128)S(1)}, u32[]{:S(2)}, u32[]{:S(2)}) async-start(f32[8,40,256]{2,1,0:T(8,128)} %shard_map.128), calls=%async_computation.2 | async-start | bytes 655360 | tf_op jit(solution)/shard_map/all_to_all | solution.py:377
  133.8 0.7 copy-start.3
Sparse Core Ops, SparseCore 0:
  11.5 48.5 all-gather.2

commit v3 on v2

--- a/solution.py
+++ b/solution.py
@@ -13,6 +13,7 @@
 D = 8192
 HP = 256
 N = 128
+SIDE = 4
 ROWS = 128
 PLANE = 16
 DEPTH = 8
@@ -75,6 +76,14 @@
     high = jnp.concatenate([(code >> 8).astype(F32), pad], axis=0).astype(BF16)
     low = jnp.concatenate([(code & 255).astype(F32), pad], axis=0).astype(BF16)
     return lower, high, low, 256.0 * nt(lower, high) + nt(lower, low)
+
+
+def both_counts(code):
+    rows = lax.broadcasted_iota(jnp.int32, (T, T), 0)
+    cols = lax.broadcasted_iota(jnp.int32, (T, T), 1)
+    upper = jnp.where(rows <= cols, 1.0, 0.0).astype(BF16)
+    _, high, low, count = counts(code)
+    return rows, cols, count, 256.0 * nn(high, upper) + nn(low, upper)
 
 
 def payload_kernel(place_ref, rate_ref, half_ref, x_ref, inj_ref, code_ref, state_ref, pay_ref, chain_ref):
@@ -97,15 +106,33 @@
             pay_ref[HP : HP + N + 8, at : at + 128] = term
 
 
-def forward_kernel(
-    rate_ref, x_ref, inj_ref, rd_ref, code_ref, state_ref,
-    out_t_ref, mix_ref, wts_ref, part_ref, fr_ref, aux_ref,
-):
-    rows = lax.broadcasted_iota(jnp.int32, (T, T), 0)
-    cols = lax.broadcasted_iota(jnp.int32, (T, T), 1)
-    lower, high, low, count = counts(code_ref[...])
-    upper = jnp.where(rows <= cols, 1.0, 0.0).astype(BF16)
-    count_t = 256.0 * nn(high, upper) + nn(low, upper)
+def forward_kernel(rate_ref, x_ref, inj_ref, rd_ref, code_ref, state_ref, out_t_ref, mix_ref):
+    rows, cols, count, count_t = both_counts(code_ref[...])
+    inject = inj_ref[...]
+    read = rd_ref[...]
+    for h in range(2):
+        rate = rate_ref[h]
+        hs = slice(h * 128, h * 128 + 128)
+        x = x_ref[:, hs]
+        s_hi, s_lo = split(state_ref[h])
+        start_w = jnp.exp(-rate * count[:, h : h + 1])
+        carried = (nt(read, s_hi) + nt(read, s_lo)) * start_w
+        for i in range(T // ROWS):
+            rs = slice(i * ROWS, i * ROWS + ROWS)
+            width = (i + 1) * ROWS
+            inter = nt(read[rs], inject[:width])
+            spread = -rate * (count[rs, h : h + 1] - count_t[h : h + 1, :width])
+            keep = rows[rs, :width] >= cols[rs, :width]
+            wts = jnp.where(keep, jnp.exp(jnp.where(keep, spread, 0.0)), 0.0)
+            narrow = (inter * wts).astype(BF16)
+            mix_ref[h, rs, :width] = narrow
+            out_t_ref[hs, rs] = (nn(narrow, x[:width]) + carried[rs]).T.astype(BF16)
+
+
+def prepare_kernel(
+    rate_ref, x_ref, inj_ref, rd_ref, code_ref, state_ref, wts_ref, part_ref, fr_ref, aux_ref,
+):
+    rows, cols, count, count_t = both_counts(code_ref[...])
     inject = inj_ref[...]
     read = rd_ref[...]
     read_f = read.astype(F32)
@@ -115,16 +142,14 @@
         rate = rate_ref[h]
         hs = slice(h * 128, h * 128 + 128)
         x = x_ref[:, hs]
-        state = state_ref[h]
-        s_hi, s_lo = split(state)
+        s_hi, s_lo = split(state_ref[h])
         cum = -rate * count[:, h : h + 1]
         start_w = jnp.exp(cum)
         to_end = jnp.exp(-rate * (count[T - 1 :, h : h + 1] - count[:, h : h + 1]))
         aux = jnp.where(lane == h, to_end, aux)
         aux = jnp.where(lane == 2 + h, start_w, aux)
         fr_ref[h] = (start_w * read_f).astype(BF16)
-        carried = (nt(read, s_hi) + nt(read, s_lo)) * start_w
-        weighted = carried * cum
+        weighted = (nt(read, s_hi) + nt(read, s_lo)) * (start_w * cum)
         for i in range(T // ROWS):
             rs = slice(i * ROWS, i * ROWS + ROWS)
             width = (i + 1) * ROWS
@@ -133,15 +158,9 @@
             keep = rows[rs, :width] >= cols[rs, :width]
             spread = jnp.where(keep, spread, 0.0)
             wts = jnp.where(keep, jnp.exp(spread), 0.0)
-            mixed = inter * wts
-            narrow = mixed.astype(BF16)
             wts_ref[h, rs, :width] = wts
-            r_hi, r_lo = split(mixed * spread)
+            r_hi, r_lo = split(inter * wts * spread)
             part_ref[rs, hs] = weighted[rs] + nn(r_hi, x[:width]) + nn(r_lo, x[:width])
-            mix_ref[h, rs, :width] = narrow
-            within = nn(narrow, x[:width])
-            out = within + carried[rs]
-            out_t_ref[hs, rs] = out.T.astype(BF16)
     aux_ref[...] = aux
 
 
@@ -179,30 +198,49 @@
     return pl.BlockSpec(dims, lambda i, place: (0,) * len(dims))
 
 
-def core_sum_kernel(kept_ref, recv_ref, o_ref):
-    o_ref[...] = (kept_ref[...].astype(F32) + recv_ref[...].astype(F32)).astype(BF16)
-
-
-def plane_sum_kernel(in_ref, rate_ref, out_ref):
-    for z in range(DEPTH):
-        rs = slice(z * 32, z * 32 + 32)
-        total = in_ref[0, rs, :].astype(F32)
-        for k in range(1, PLANE):
-            total = total + in_ref[k, rs, :].astype(F32)
-        out_ref[z, :32, :] = total
-        out_ref[z, 32:, :128] = rate_ref[...]
-        out_ref[z, 32:, 128:] = rate_ref[...]
-
-
-def depth_sum_kernel(tokens, in_ref, out_ref, rate_ref):
+def core_sum_kernel(place_ref, kept_a, recv_a, kept_b, recv_b, *outs):
+    rows = (kept_a[0].astype(F32) + recv_a[0].astype(F32)).astype(BF16)
+    cols = (kept_b[:, 0].astype(F32) + recv_b[:, 0].astype(F32)).astype(BF16)
+    for d in range(SIDE):
+
+        @pl.when(pl.program_id(0) == d)
+        def _(d=d):
+            outs[d][...] = rows
+            outs[SIDE + d][...] = cols
+
+
+def line_sum_kernel(place_ref, *refs):
+    ins, outs = refs[:8], refs[8:]
+    for part in range(2):
+        mine = place_ref[3 - part]
+        for d in range(SIDE):
+            at = lax.rem(mine + d, SIDE)
+            total = ins[part * 4][at].astype(F32)
+            for j in range(1, SIDE):
+                total = total + ins[part * 4 + j][at].astype(F32)
+            outs[part * 4 + d][...] = total
+
+
+def plane_sum_kernel(*refs):
+    ins, out_ref = refs[:8], refs[8]
+    for part in range(2):
+        total = ins[part * 4][...] + ins[part * 4 + 1][...]
+        total = total + ins[part * 4 + 2][...] + ins[part * 4 + 3][...]
+        for k in range(4):
+            out_ref[part * 4 + k] = total[k * 32 : k * 32 + 32, :]
+
+
+def depth_sum_kernel(in_ref, out_ref):
     total = in_ref[0]
     for k in range(1, DEPTH):
         total = total + in_ref[k]
-    out_ref[...] = total[:32]
-    rate_ref[...] = total[32:, :128] / tokens
-
-
-def rate_vector_kernel(place_ref, part_ref, rd_ref, aux_ref, all_ref, o_ref, later_ref):
+    out_ref[...] = total
+
+
+def rate_vector_kernel(
+    place_ref, part_ref, rd_ref, aux_ref, gathered_ref, o_ref, later_ref, all_ref, sem,
+):
+    fetch(gathered_ref.at[:, pl.ds(HP, N + 8), :], all_ref, sem).wait()
     for h in range(2):
         hs = slice(h * 128, h * 128 + 128)
         low = slice(256 + h * 128, 384 + h * 128)
@@ -217,7 +255,9 @@
         o_ref[:, hs] = part_ref[:, hs] + aux_ref[:, 2 + h : 3 + h] * through
 
 
-def output_grad_kernel(place_ref, cot_ref, mine_ref, other_ref, fr_ref, og_ref, pay_ref, acc):
+def output_grad_kernel(
+    place_ref, cot_ref, mine_ref, other_ref, fr_ref, vec_ref, og_ref, pay_ref, acc,
+):
     core = place_ref[0]
     step = pl.program_id(0)
     total = None
@@ -239,20 +279,24 @@
     def _():
         grad = acc[...].astype(BF16)
         og_ref[...] = grad
+        tail = []
         for h in range(2):
             hs = slice(h * 128, h * 128 + 128)
             narrow = tn(grad[:, hs], fr_ref[h]).astype(BF16)
             for z in range(DEPTH):
                 pay_ref[z, hs, :] = narrow
-
-
-def rate_kernel(og_ref, vec_ref, rate_ref):
-    rates = []
-    for h in range(2):
-        hs = slice(h * 128, h * 128 + 128)
-        rate = jnp.sum(og_ref[:, hs].astype(F32) * vec_ref[:, hs], axis=0, keepdims=True)
-        rates.append(jnp.broadcast_to(jnp.sum(rate, axis=1, keepdims=True), (1, 128)))
-    rate_ref[...] = jnp.concatenate(rates + [jnp.zeros((6, 128), F32)], axis=0)
+            rate = jnp.sum(grad[:, hs].astype(F32) * vec_ref[:, hs], axis=0, keepdims=True)
+            rest = jnp.broadcast_to(jnp.sum(rate, axis=1, keepdims=True), (8, 128))
+            rest_row = lax.broadcasted_iota(jnp.int32, (8, 128), 0)
+            terms = jnp.zeros((8, 128), F32)
+            for k in range(3):
+                term = rest.astype(BF16).astype(F32)
+                terms = jnp.where(rest_row == k, term, terms)
+                rest = rest - term
+            tail.append(terms)
+        tail = jnp.concatenate(tail, axis=0).astype(BF16)
+        for z in range(DEPTH):
+            pay_ref[z, HP:, :] = tail
 
 
 def backward_kernel(
@@ -315,7 +359,8 @@
     state = start_state[0, 0]
     code = decay_code[0]
     core = lax.axis_index("dp") % 2
-    place = jnp.stack([core, lax.axis_index("ctx")]).astype(jnp.int32)
+    me = lax.axis_index("dp")
+    place = jnp.stack([core, lax.axis_index("ctx"), me // 8, me // 2 % SIDE]).astype(jnp.int32)
 
     pay, chain = gridded(
         payload_kernel, 1,
@@ -330,61 +375,94 @@
     )
     gathered = lax.all_gather(pay, "ctx", axis=0)
     x, _ = lax.optimization_barrier((x, chain))
-    out_t, mix, wts, part, from_start, aux = call(
-        forward_kernel,
-        [
-            shape((HP, T), BF16), shape((2, T, T), BF16), shape((2, T, T)), shape((T, HP)),
-            shape((2, T, N), BF16), shape((T, 128)),
-        ],
+    out_t, mix = call(
+        forward_kernel, [shape((HP, T), BF16), shape((2, T, T), BF16)],
         (decay_rate, x, inject, read, code.T, state), smem=(0,),
     )
     half_terms = shape((PLANE, 256, 256), BF16)
-    quarter = pl.BlockSpec((4, 256, 256), lambda i, place: (i, 0, 0))
+    part_spec = pl.BlockSpec((4, 256, 256), lambda i, place: (i, 0, 0))
     sent, kept = gridded(
         weight_kernel, 4,
         [fixed((HP, T)), pl.BlockSpec((T, 2048), lambda i, place: (0, i))],
-        [quarter, quarter], [half_terms, half_terms], (place, out_t, cot),
-    )
-    blocks = call(core_sum_kernel, half_terms, (kept, swap_cores(sent)))
-    groups = [[2 * k + c for k in range(PLANE)] for c in range(2)]
-    swapped = lax.all_to_all(blocks, "dp", 0, 0, tiled=True, axis_index_groups=groups)
-
-    gathered, _ = lax.optimization_barrier((gathered, swapped))
+        [part_spec, part_spec], [half_terms, half_terms], (place, out_t, cot),
+    )
+    parts = core_sum(place, kept, swap_cores(sent))
+    first = exchanged(parts[:SIDE], 8)
+    second = exchanged(parts[SIDE:], 2)
+    parts = call(line_sum_kernel, [shape((128, 256))] * 8, (place, *first, *second), smem=(0,))
+
+    read_later, _ = lax.optimization_barrier((read, kept))
+    wts, part, from_start, aux = call(
+        prepare_kernel,
+        [shape((2, T, T)), shape((T, HP)), shape((2, T, N), BF16), shape((T, 128))],
+        (decay_rate, x, inject, read_later, code.T, state), smem=(0,),
+    )
+
+    gathered, _ = lax.optimization_barrier((gathered, (parts, aux)))
     mine = gathered[:, :HP, :]
     other = swap_cores(mine)
     vector, decay = call(
         rate_vector_kernel, [shape((T, HP)), shape((DEPTH, 16, 128))],
-        (place, part, read, aux, gathered[:, HP:, :]), smem=(0,),
-    )
-    from_start, _ = lax.optimization_barrier((from_start, vector))
-    pair = pl.BlockSpec((2, HP, 512), lambda i, place: (i, 0, 0))
+        (place, part, read, aux, gathered), smem=(0,), hbm=(4,),
+        scratch=[pltpu.VMEM((DEPTH, N + 8, 512), BF16), pltpu.SemaphoreType.DMA],
+    )
+    one = pl.BlockSpec((2, HP, 512), lambda i, place: (i, 0, 0))
     grad, pay = gridded(
         output_grad_kernel, 4,
-        [pl.BlockSpec((T, 2048), lambda i, place: (0, i)), pair, pair, fixed((2, T, N))],
-        [fixed((T, HP)), fixed((DEPTH, HP, 128))],
-        [shape((T, HP), BF16), shape((DEPTH, HP, 128), BF16)],
-        (place, cot, mine, other, from_start), [pltpu.VMEM((T, HP), F32)],
-    )
+        [
+            pl.BlockSpec((T, 2048), lambda i, place: (0, i)), one, one, fixed((2, T, N)),
+            fixed((T, HP)),
+        ],
+        [fixed((T, HP)), fixed((DEPTH, HP + 16, 128))],
+        [shape((T, HP), BF16), shape((DEPTH, HP + 16, 128), BF16)],
+        (place, cot, mine, other, from_start, vector), [pltpu.VMEM((T, HP), F32)],
+    )
+    parts, _ = lax.optimization_barrier((parts, pay))
+    first = exchanged(parts[:SIDE], 2)
+    second = exchanged(parts[SIDE:], 8)
     pay = lax.all_to_all(pay, "ctx", 0, 0, tiled=True)
-    rate = plane_total(call(rate_kernel, shape((8, 128)), (grad, vector)))
     gi, ginj, grad_read = call(
         backward_kernel, [shape((T, HP)), shape((T, N)), shape((T, N))],
         (grad, x, inject, read, state, mix, wts, aux),
     )
-    swapped, _ = lax.optimization_barrier((swapped, gi))
-    blocks = call(plane_sum_kernel, shape((DEPTH, 40, 256)), (swapped, rate))
-    blocks, _ = lax.optimization_barrier((blocks, pay))
+    blocks = call(plane_sum_kernel, shape((DEPTH, 32, 256)), (*first, *second))
+    blocks, pay = lax.optimization_barrier((blocks, pay))
     blocks = lax.all_to_all(blocks, "ctx", 0, 0, tiled=True)
+    rate = jnp.sum(pay[:, HP:, :].astype(F32).reshape(DEPTH, 2, 8, 128), axis=(0, 2))
+    rate = plane_total(rate)
     grad_input, grad_inject = call(
         finish_kernel, [shape((T, HP), BF16), shape((T, N))],
         (place, gi, ginj, x, inject, aux, pay, decay), smem=(0,),
     )
+    grad_weight = call(depth_sum_kernel, shape((32, 256)), (blocks,))
     tokens = T * lax.axis_size("dp") * lax.axis_size("ctx")
-    grad_weight, rate = call(
-        functools.partial(depth_sum_kernel, tokens), [shape((32, 256)), shape((8, 128))],
-        (blocks,),
-    )
-    return grad_input[None], grad_inject[None], grad_read[None], grad_weight, rate[:2, 0]
+    return grad_input[None], grad_inject[None], grad_read[None], grad_weight, rate[:, 0] / tokens
+
+
+def core_sum(place, kept, recv):
+    kept, recv = (a.reshape(SIDE, SIDE, 256, 256) for a in (kept, recv))
+    by_x = pl.BlockSpec(
+        (1, SIDE, 128, 256), lambda d, place: (lax.rem(place[2] + d, SIDE), 0, 0, 0)
+    )
+    by_y = pl.BlockSpec(
+        (SIDE, 1, 128, 256), lambda d, place: (0, lax.rem(place[3] + d, SIDE), 1, 0)
+    )
+    part = (SIDE, 128, 256)
+    return gridded(
+        core_sum_kernel, SIDE, [by_x, by_x, by_y, by_y], [fixed(part)] * 8,
+        [shape(part, BF16)] * 8, (place, kept, recv, kept, recv),
+    )
+
+
+def exchanged(parts, unit):
+    def pairs(d):
+        def target(i):
+            at = i // unit % SIDE
+            return i + ((at + d) % SIDE - at) * unit
+
+        return [(i, target(i)) for i in range(2 * PLANE)]
+
+    return [parts[0]] + [lax.ppermute(parts[d], "dp", pairs(d)) for d in range(1, SIDE)]
 
 
 def flipped(value, bits):

time: 146 us -> 135 us (0.925)
  blocking collectives: 34 us -> 0 us
  starting transfers between devices: 24 us -> 41.4 us
  Pallas kernels: 45 us -> 50.7 us
  local copies, waits for them, and re-layouts: 8.06 us -> 5.23 us
  waiting for transfers between devices: 17.3 us -> 19.6 us
    all_to_all x1 -> x0, blocking collectives: 34 us -> none  [local(): lax.all_to_all(blocks, 'dp', 0, 0, tiled=True, axis_index_groups=groups)]
    ppermute x0 -> x12, starting transfers between devices: none -> 20.8 us  [exchanged(): lax.ppermute(parts[d], 'dp', pairs(d))]
    ppermute x0 -> x12, waiting for transfers between devices: none -> 9.83 us  [exchanged(): lax.ppermute(parts[d], 'dp', pairs(d))]
    all_to_all x1, waiting for transfers between devices: 8.73 us -> 0.01 us  [local(): blocks = lax.all_to_all(blocks, 'ctx', 0, 0, tiled=True)]
    pallas_call x3 -> x4, Pallas kernels: 19.7 us -> 25.5 us  [gridded(): pl.pallas_call(kernel, out_shape=outs, grid_spec=pltpu.PrefetchScalarGrid...]
    slice x2 -> x0, local copies, waits for them, and re-layouts: 4.3 us -> none  [the longest x1 3.01 us: local(): gathered[:, HP:, :]]
    ppermute x7, waiting for transfers between devices: 4.14 us -> 1.14 us  [flipped(): return lax.ppermute(value, 'dp', [(i, i ^ bits) for i in range(2 * PLANE)])]
    all_to_all x1, starting transfers between devices: 8.5 us -> 6.05 us  [local(): pay = lax.all_to_all(pay, 'ctx', 0, 0, tiled=True)]
  transfers between devices with their start and end apart: 12 -> 24, of which waited for: 6 -> 13; matrix products, arithmetic and copies ran while one was open for 3% -> 0% of each run, Pallas kernels for 22% -> 28%
where the time goes in v3:
time: 135 us; the launch traced here: 133 us
  Pallas kernels  50.7 us (38%)
  starting transfers between devices  41.4 us (31%)
  waiting for transfers between devices  19.6 us (15%)
  between operations  14.3 us (11%)
  local copies, waits for them, and re-layouts  5.23 us (4%)
    pallas_call x4, Pallas kernels, gridded(): pl.pallas_call(kernel, out_shape=outs, grid_spec=pltpu.PrefetchScalarGrid...  25.5 us
    pallas_call x8, Pallas kernels, call(): pl.pallas_call(kernel, grid=(1,), out_shape=outs, in_specs=[spec(i, arg)...  25.3 us
    ppermute x12, starting transfers between devices, exchanged(): lax.ppermute(parts[d], 'dp', pairs(d))  20.8 us
    ppermute x12, waiting for transfers between devices, exchanged(): lax.ppermute(parts[d], 'dp', pairs(d))  9.83 us
    ppermute x7, starting transfers between devices, flipped(): return lax.ppermute(value, 'dp', [(i, i ^ bits) for i in range(2 * PLANE)])  9.08 us
    all_to_all x1, starting transfers between devices, local(): pay = lax.all_to_all(pay, 'ctx', 0, 0, tiled=True)  6.05 us
    all_to_all x1, starting transfers between devices, local(): blocks = lax.all_to_all(blocks, 'ctx', 0, 0, tiled=True)  5.1 us
    ppermute x2, waiting for transfers between devices, swap_cores(): return lax.ppermute(value, 'dp', [(i, i ^ 1) for i in range(2 * PLANE)])  4.47 us
  transfers between devices with their start and end apart: 24, of which 13 were waited for; matrix products, arithmetic and copies ran while one was open for 0% of the time, Pallas kernels for 28%

profile of v3, /device:TPU:2, one launch (start us, length us, event | category | flops | bytes accessed | tf_op | source)
XLA Modules:
  0.0 132.5 jit_solution(12606573930967546058)
XLA Ops:
  7.2 0.0 all-gather.3.cloned.1.call-start
  7.3 0.6 pad_add_fusion.place_ref
  7.8 3.5 %shard_map.119 = (bf16[392,512]{1,0:T(8,128)(2,1)}, f32[2,136,128]{2,1,0:T(8,128)}) custom-call(s32[4]{0:T(128)} %pad_add_fusion.place_ref, f32[2]{0:T(128)} %rate_ref.5, bf16[256,1024]{1,0:T(8,128)(2,1)} %half_ref.1, bf16[512,256]{1,0:T(8,128)(2,1)} %bitcast.28, bf16[512,128]{1,0:T(8,128)(2,1)} %bitcast.33, s32[2,512]{1,0:T(2,128)} %bitcast.46, ...), custom_call_target="tpu_custom_call" | custom-call | tf_op jit(solution)/shard_map/pallas_call | solution.py:182
  11.4 0.0 all-gather.3.cloned.1.call-update
  11.4 3.3 %shard_map.120 = (bf16[256,512]{1,0:T(8,128)(2,1)}, bf16[2,512,512]{2,1,0:T(8,128)(2,1)}) custom-call(f32[2]{0:T(128)} %rate_ref.5, bf16[512,256]{1,0:T(8,128)(2,1)} %bitcast.29, bf16[512,128]{1,0:T(8,128)(2,1)} %bitcast.34, bf16[512,128]{1,0:T(8,128)(2,1)} %bitcast.42, s32[2,512]{1,0:T(2,128)} %bitcast.47, f32[2,128,128]{2,1,0:T(8,128)} %bitcast.39), custom_call_target="tpu_custom_call" | custom-call | tf_op jit(solution)/shard_map/pallas_call | solution.py:53
  14.7 7.9 %shard_map.121 = (bf16[16,256,256]{2,1,0:T(8,128)(2,1)}, bf16[16,256,256]{2,1,0:T(8,128)(2,1)}) custom-call(s32[4]{0:T(128)} %pad_add_fusion.place_ref, bf16[256,512]{1,0:T(8,128)(2,1)} %get-tuple-element.52.out_t_ref, bf16[512,8192]{1,0:T(8,128)(2,1)} %bitcast.20), custom_call_target="tpu_custom_call" | custom-call | tf_op jit(solution)/shard_map/pallas_call | solution.py:182
  22.6 0.0 collective-permute-start
  22.6 4.4 %collective-permute-done = bf16[16,256,256]{2,1,0:T(8,128)(2,1)S(1)} collective-permute-done((bf16[16,256,256]{2,1,0:T(8,128)(2,1)}, bf16[16,256,256]{2,1,0:T(8,128)(2,1)S(1)}, u32[]{:S(2)}, u32[]{:S(2)}) %collective-permute-start) | collective-permute-done | bytes 2097184 | tf_op jit(solution)/shard_map/ppermute | solution.py:349
  26.9 1.3 %copy-done.1 = bf16[16,256,256]{2,1,0:T(8,128)(2,1)} copy-done((bf16[16,256,256]{2,1,0:T(8,128)(2,1)}, bf16[16,256,256]{2,1,0:T(8,128)(2,1)S(1)}, u32[]{:S(2)}) %copy-start.1) | copy-done | bytes 2097176
  28.3 5.3 %shard_map.122 = (bf16[4,128,256]{2,1,0:T(8,128)(2,1)}, bf16[4,128,256]{2,1,0:T(8,128)(2,1)}, bf16[4,128,256]{2,1,0:T(8,128)(2,1)}, bf16[4,128,256]{2,1,0:T(8,12...) custom-call(s32[4]{0:T(128)} %pad_add_fusion.place_ref, ...), custom_call_target="tpu_custom_call" | custom-call | tf_op jit(solution)/shard_map/pallas_call | solution.py:182
  33.6 1.5 %collective-permute-start.1 = (bf16[4,128,256]{2,1,0:T(8,128)(2,1)}, bf16[4,128,256]{2,1,0:T(8,128)(2,1)S(1)}, u32[]{:S(2)}, u32[]{:S(2)}) collective-permute-start(bf16[4,128,256]{2,1,0:T(8,128)(2,1)} %get-tuple-element.56), channel_id=1, source_target_pairs={{0,64},{8,72},{16,80},{24,88},{32,96},{40,104},{48,112},{56,120},{... | collective-permute-start | bytes 786440 | tf_op jit(solution)/shard_map/ppermute | solution.py:465
  35.1 2.9 %collective-permute-start.2 = (bf16[4,128,256]{2,1,0:T(8,128)(2,1)}, bf16[4,128,256]{2,1,0:T(8,128)(2,1)S(1)}, u32[]{:S(2)}, u32[]{:S(2)}) collective-permute-start(bf16[4,128,256]{2,1,0:T(8,128)(2,1)} %get-tuple-element.57), channel_id=1, source_target_pairs={{0,128},{8,136},{16,144},{24,152},{32,160},{40,168},{48,176},{56,1... | collective-permute-start | bytes 786440 | tf_op jit(solution)/shard_map/ppermute | solution.py:465
  37.9 0.4 collective-permute-start.3
  38.3 1.6 %collective-permute-start.4 = (bf16[4,128,256]{2,1,0:T(8,128)(2,1)}, bf16[4,128,256]{2,1,0:T(8,128)(2,1)S(1)}, u32[]{:S(2)}, u32[]{:S(2)}) collective-permute-start(bf16[4,128,256]{2,1,0:T(8,128)(2,1)} %get-tuple-element.60), channel_id=1, source_target_pairs={{0,16},{8,24},{16,32},{24,40},{32,48},{40,56},{48,0},{56,8},{64,80... | collective-permute-start | bytes 786440 | tf_op jit(solution)/shard_map/ppermute | solution.py:465
  39.9 2.9 %collective-permute-start.5 = (bf16[4,128,256]{2,1,0:T(8,128)(2,1)}, bf16[4,128,256]{2,1,0:T(8,128)(2,1)S(1)}, u32[]{:S(2)}, u32[]{:S(2)}) collective-permute-start(bf16[4,128,256]{2,1,0:T(8,128)(2,1)} %get-tuple-element.61), channel_id=1, source_target_pairs={{0,32},{8,40},{16,48},{24,56},{32,0},{40,8},{48,16},{56,24},{64,96... | collective-permute-start | bytes 786440 | tf_op jit(solution)/shard_map/ppermute | solution.py:465
  42.8 0.4 collective-permute-done.1.refs_1_
  43.2 2.8 %collective-permute-start.6 = (bf16[4,128,256]{2,1,0:T(8,128)(2,1)}, bf16[4,128,256]{2,1,0:T(8,128)(2,1)S(1)}, u32[]{:S(2)}, u32[]{:S(2)}) collective-permute-start(bf16[4,128,256]{2,1,0:T(8,128)(2,1)} %get-tuple-element.62), channel_id=1, source_target_pairs={{0,48},{8,56},{16,0},{24,8},{32,16},{40,24},{48,32},{56,40},{64,11... | collective-permute-start | bytes 786440 | tf_op jit(solution)/shard_map/ppermute | solution.py:465
  46.0 3.9 %shard_map.124 = (f32[2,512,512]{2,1,0:T(8,128)}, f32[512,256]{1,0:T(8,128)}, bf16[2,512,128]{2,1,0:T(8,128)(2,1)}, f32[512,128]{1,0:T(8,128)}) custom-call(f32[2]{0:T(128)} %rate_ref.5, bf16[512,256]{1,0:T(8,128)(2,1)} %bitcast.30, bf16[512,128]{1,0:T(8,128)(2,1)} %bitcast.35, bf16[512,128]{1,0:T(8,128)(2,1)} %bitcast.43, s32[2,512]{1,0:T(2,128)} %bitcast.48, ...), custom_call_target="tpu_custom_call" | custom-call | tf_op jit(solution)/shard_map/pallas_call | solution.py:53
  49.8 0.0 collective-permute-done.2.refs_2_
  49.9 0.6 collective-permute-done.3.refs_3_
  50.5 0.0 collective-permute-done.4.refs_5_
  50.5 3.6 %collective-permute-done.5.refs_6_ = bf16[4,128,256]{2,1,0:T(8,128)(2,1)S(1)} collective-permute-done((bf16[4,128,256]{2,1,0:T(8,128)(2,1)}, bf16[4,128,256]{2,1,0:T(8,128)(2,1)S(1)}, u32[]{:S(2)}, u32[]{:S(2)}) %collective-permute-start.5) | collective-permute-done | bytes 262176 | tf_op jit(solution)/shard_map/ppermute | solution.py:465
  54.1 0.0 collective-permute-done.6.refs_7_
  54.2 0.7 copy-done.8
  54.8 0.1 copy-done.9
  54.9 2.7 %shard_map.123 = (f32[128,256]{1,0:T(8,128)}, f32[128,256]{1,0:T(8,128)}, f32[128,256]{1,0:T(8,128)}, f32[128,256]{1,0:T(8,128)}, f32[128,256]{1,0:T(8,128)}, /*...) custom-call(s32[4]{0:T(128)} %pad_add_fusion.place_ref, bf16[4,128,256]{2,1,0:T(8,128)(2,1)} %get-tuple-element.55.refs_0_, ...), custom_call_target="tpu_custom_call" | custom-call | tf_op jit(solution)/shard_map/pallas_call | solution.py:53
  57.7 2.4 %all-gather.3.cloned.1.call-done = bf16[3136,512]{1,0:T(8,128)(2,1)} async-done(((bf16[392,512]{1,0:T(8,128)(2,1)}), bf16[3136,512]{1,0:T(8,128)(2,1)}) %all-gather.3.cloned.1.call-update) | async-done | bytes 3211280 | tf_op jit(solution)/shard_map/all_gather | solution.py:376
  60.1 1.7 %slice.9.mine_ref = bf16[8,256,512]{2,1,0:T(8,128)(2,1)S(1)} slice(bf16[8,392,512]{2,1,0:T(8,128)(2,1)} %bitcast.22), slice={[0:8], [0:256], [0:512]} | slice | bytes 4194304 | tf_op jit(solution)/shard_map/slice | solution.py:402
  61.8 0.3 collective-permute-start.7
  62.1 4.2 %shard_map.125 = (f32[512,256]{1,0:T(8,128)}, f32[8,16,128]{2,1,0:T(8,128)}) custom-call(s32[4]{0:T(128)} %pad_add_fusion.place_ref, f32[512,256]{1,0:T(8,128)} %get-tuple-element.75.part_ref, bf16[512,128]{1,0:T(8,128)(2,1)} %bitcast.44, f32[512,128]{1,0:T(8,128)} %get-tuple-element.72.aux_ref, bf16[8,392,512]{2,1,0:T(8,128)(2,1)} %bitcast.23), custom_call_target="tpu_custom_call" | custom-call | tf_op jit(solution)/shard_map/pallas_call | solution.py:53
  66.3 0.1 collective-permute-done.7.other_ref
  66.4 8.8 %shard_map.126 = (bf16[512,256]{1,0:T(8,128)(2,1)}, bf16[8,272,128]{2,1,0:T(8,128)(2,1)}) custom-call(s32[4]{0:T(128)} %pad_add_fusion.place_ref, bf16[512,8192]{1,0:T(8,128)(2,1)} %bitcast.21, bf16[8,256,512]{2,1,0:T(8,128)(2,1)} %copy-done, bf16[8,256,512]{2,1,0:T(8,128)(2,1)} %collective-permute-done.7.other_ref, ...), custom_call_target="tpu_custom_call" | custom-call | tf_op jit(solution)/shard_map/pallas_call | solution.py:182
  75.2 6.0 %all-to-all-start = ((bf16[8,272,128]{2,1,0:T(8,128)(2,1)}), bf16[8,272,128]{2,1,0:T(8,128)(2,1)S(1)}, u32[]{:S(2)}, u32[]{:S(2)}) async-start(bf16[8,272,128]{2,1,0:T(8,128)(2,1)} %get-tuple-element.82), calls=%async_computation | async-start | bytes 1114112 | tf_op jit(solution)/shard_map/all_to_all | solution.py:423
  81.3 1.9 %collective-permute-start.8 = (f32[128,256]{1,0:T(8,128)S(1)}, f32[128,256]{1,0:T(8,128)S(1)}, u32[]{:S(2)}, u32[]{:S(2)}) collective-permute-start(f32[128,256]{1,0:T(8,128)S(1)} %copy-done.21), channel_id=1, source_target_pairs={{0,16},{8,24},{16,32},{24,40},{32,48},{40,56},{48,0},{56,8},{64,80... | collective-permute-start | bytes 393224 | tf_op jit(solution)/shard_map/ppermute | solution.py:465
  83.2 1.6 %collective-permute-start.9 = (f32[128,256]{1,0:T(8,128)S(1)}, f32[128,256]{1,0:T(8,128)S(1)}, u32[]{:S(2)}, u32[]{:S(2)}) collective-permute-start(f32[128,256]{1,0:T(8,128)S(1)} %copy-done.20), channel_id=1, source_target_pairs={{0,32},{8,40},{16,48},{24,56},{32,0},{40,8},{48,16},{56,24},{64,96... | collective-permute-start | bytes 393224 | tf_op jit(solution)/shard_map/ppermute | solution.py:465
  84.8 1.7 %collective-permute-start.10 = (f32[128,256]{1,0:T(8,128)S(1)}, f32[128,256]{1,0:T(8,128)S(1)}, u32[]{:S(2)}, u32[]{:S(2)}) collective-permute-start(f32[128,256]{1,0:T(8,128)S(1)} %copy-done.19), channel_id=1, source_target_pairs={{0,48},{8,56},{16,0},{24,8},{32,16},{40,24},{48,32},{56,40},{64,11... | collective-permute-start | bytes 393224 | tf_op jit(solution)/shard_map/ppermute | solution.py:465
  86.5 0.3 collective-permute-start.11
  86.8 3.2 %collective-permute-start.12 = (f32[128,256]{1,0:T(8,128)S(1)}, f32[128,256]{1,0:T(8,128)S(1)}, u32[]{:S(2)}, u32[]{:S(2)}) collective-permute-start(f32[128,256]{1,0:T(8,128)S(1)} %copy-done.17), channel_id=1, source_target_pairs={{0,128},{8,136},{16,144},{24,152},{32,160},{40,168},{48,176},{56,1... | collective-permute-start | bytes 393224 | tf_op jit(solution)/shard_map/ppermute | solution.py:465
  90.0 0.0 collective-permute-done.8.refs_1_
  90.0 0.1 collective-permute-start.13
  90.1 0.7 collective-permute-done.9.refs_2_
  90.8 0.4 collective-permute-done.10.refs_3_
  91.2 1.1 collective-permute-done.11.refs_5_
  92.3 1.6 %collective-permute-done.12.refs_6_ = f32[128,256]{1,0:T(8,128)S(1)} collective-permute-done((f32[128,256]{1,0:T(8,128)S(1)}, f32[128,256]{1,0:T(8,128)S(1)}, u32[]{:S(2)}, u32[]{:S(2)}) %collective-permute-start.12) | collective-permute-done | bytes 131104 | tf_op jit(solution)/shard_map/ppermute | solution.py:465
  93.9 1.4 %collective-permute-done.13.refs_7_ = f32[128,256]{1,0:T(8,128)S(1)} collective-permute-done((f32[128,256]{1,0:T(8,128)S(1)}, f32[128,256]{1,0:T(8,128)S(1)}, u32[]{:S(2)}, u32[]{:S(2)}) %collective-permute-start.13) | collective-permute-done | bytes 131104 | tf_op jit(solution)/shard_map/ppermute | solution.py:465
  95.3 0.6 copy-done.15
  96.0 2.0 %shard_map.128 = f32[8,32,256]{2,1,0:T(8,128)} custom-call(f32[128,256]{1,0:T(8,128)} %get-tuple-element.83.refs_0_, f32[128,256]{1,0:T(8,128)} %copy-done.10, f32[128,256]{1,0:T(8,128)} %copy-done.11, f32[128,256]{1,0:T(8,128)} %copy-done.12, f32[128,256]{1,0:T(8,128)} %get-tuple-element.87.refs_4_, f32[128,256]{1,0:T(8,128)} %copy-done.13, ...), custom_call_target="tpu_custom_call" | custom-call | tf_op jit(solution)/shard_map/pallas_call | solution.py:53
  98.0 1.8 %all-to-all-done.adj_ref = bf16[8,272,128]{2,1,0:T(8,128)(2,1)S(1)} async-done(((bf16[8,272,128]{2,1,0:T(8,128)(2,1)}), bf16[8,272,128]{2,1,0:T(8,128)(2,1)S(1)}, u32[]{:S(2)}, u32[]{:S(2)}) %all-to-all-start) | async-done | bytes 557088 | tf_op jit(solution)/shard_map/all_to_all | solution.py:423
  99.8 0.1 collective-permute-start.14
  99.9 1.1 collective-permute-done.14
  101.0 2.0 %collective-permute-start.17 = (f32[2,128]{1,0:T(2,128)S(1)}, f32[2,128]{1,0:T(2,128)S(1)}, u32[]{:S(2)}, u32[]{:S(2)}) collective-permute-start(f32[2,128]{1,0:T(2,128)S(1)} %add.32), channel_id=1, source_target_pairs={{0,48},{8,56},{16,32},{24,40},{32,16},{40,24},{48,0},{56,8},{64,11... | collective-permute-start | bytes 3080 | tf_op jit(solution)/shard_map/ppermute | solution.py:469
  103.0 0.5 collective-permute-start.16
  103.5 2.3 %collective-permute-start.15 = (f32[2,128]{1,0:T(2,128)S(1)}, f32[2,128]{1,0:T(2,128)S(1)}, u32[]{:S(2)}, u32[]{:S(2)}) collective-permute-start(f32[2,128]{1,0:T(2,128)S(1)} %add.32), channel_id=1, source_target_pairs={{0,32},{8,40},{16,48},{24,56},{32,0},{40,8},{48,16},{56,24},{64,96... | collective-permute-start | bytes 3080 | tf_op jit(solution)/shard_map/ppermute | solution.py:469
  105.7 5.1 %all-to-all-start.1 = ((f32[8,32,256]{2,1,0:T(8,128)}), f32[8,32,256]{2,1,0:T(8,128)S(1)}, u32[]{:S(2)}, u32[]{:S(2)}) async-start(f32[8,32,256]{2,1,0:T(8,128)} %shard_map.128), calls=%async_computation.1 | async-start | bytes 524288 | tf_op jit(solution)/shard_map/all_to_all | solution.py:430
  110.8 0.0 collective-permute-done.17
  110.9 0.6 collective-permute-start.20
  111.5 3.6 %collective-permute-start.19 = (f32[2,128]{1,0:T(2,128)S(1)}, f32[2,128]{1,0:T(2,128)S(1)}, u32[]{:S(2)}, u32[]{:S(2)}) collective-permute-start(f32[2,128]{1,0:T(2,128)S(1)} %add_add_fusion.1), channel_id=1, source_target_pairs={{0,64},{8,72},{16,80},{24,88},{32,96},{40,104},{48,112},{56,120},{... | collective-permute-start | bytes 3080 | tf_op jit(solution)/shard_map/ppermute | solution.py:469
  115.1 4.9 %shard_map.127 = (f32[512,256]{1,0:T(8,128)}, f32[512,128]{1,0:T(8,128)}, f32[512,128]{1,0:T(8,128)}) custom-call(bf16[512,256]{1,0:T(8,128)(2,1)} %get-tuple-element.77.g_ref, bf16[512,256]{1,0:T(8,128)(2,1)} %bitcast.31, bf16[512,128]{1,0:T(8,128)(2,1)} %bitcast.36, bf16[512,128]{1,0:T(8,128)(2,1)} %bitcast.45, f32[2,128,128]{2,1,0:T(8,128)} %bitcast.41, ...), custom_call_target="tpu_custom_call" | custom-call | tf_op jit(solution)/shard_map/pallas_call | solution.py:53
  120.1 2.7 %shard_map.129 = (bf16[512,256]{1,0:T(8,128)(2,1)}, f32[512,128]{1,0:T(8,128)}) custom-call(s32[4]{0:T(128)} %pad_add_fusion.place_ref, f32[512,256]{1,0:T(8,128)} %get-tuple-element.80.gi_ref, f32[512,128]{1,0:T(8,128)} %get-tuple-element.81.ginj_ref, bf16[512,256]{1,0:T(8,128)(2,1)} %bitcast.32, bf16[512,128]{1,0:T(8,128)(2,1)} %bitcast.37, ...), custom_call_target="tpu_custom_call" | custom-call | tf_op jit(solution)/shard_map/pallas_call | solution.py:53
  122.7 0.0 collective-permute-done.18
  122.8 0.6 multiply_reduce_fusion
  123.4 0.0 all-to-all-done.1.in_ref
  123.4 0.7 copy-done.3
  124.1 1.6 %shard_map.130 = f32[32,256]{1,0:T(8,128)} custom-call(f32[8,32,256]{2,1,0:T(8,128)} %copy-done.3), custom_call_target="tpu_custom_call" | custom-call | tf_op jit(solution)/shard_map/pallas_call | solution.py:53
  (49 shorter events, 0.1 us)
Async XLA Ops:
  7.2 52.9 %all-gather.3.cloned.1.call-start = ((), (), s32[]{:S(2)}) async-start(), calls=%async_computation.2 | async-start | bytes 3612672 | tf_op jit(solution)/shard_map/all_gather | solution.py:376
  22.6 4.4 %collective-permute-start = (bf16[16,256,256]{2,1,0:T(8,128)(2,1)}, bf16[16,256,256]{2,1,0:T(8,128)(2,1)S(1)}, u32[]{:S(2)}, u32[]{:S(2)}) collective-permute-start(bf16[16,256,256]{2,1,0:T(8,128)(2,1)} %get-tuple-element.54), channel_id=1, source_target_pairs={{0,8},{8,0},{16,24},{24,16},{32,40},{40,32},{48,56},{56,48},{64,72... | collective-permute-start | bytes 6291464 | tf_op jit(solution)/shard_map/ppermute | solution.py:349
  26.9 1.3 %copy-start.1 = (bf16[16,256,256]{2,1,0:T(8,128)(2,1)}, bf16[16,256,256]{2,1,0:T(8,128)(2,1)S(1)}, u32[]{:S(2)}) copy-start(bf16[16,256,256]{2,1,0:T(8,128)(2,1)S(1)} %collective-permute-done) | copy-start | bytes 6291460
  33.6 9.6 %collective-permute-start.1 = (bf16[4,128,256]{2,1,0:T(8,128)(2,1)}, bf16[4,128,256]{2,1,0:T(8,128)(2,1)S(1)}, u32[]{:S(2)}, u32[]{:S(2)}) collective-permute-start(bf16[4,128,256]{2,1,0:T(8,128)(2,1)} %get-tuple-element.56), channel_id=1, source_target_pairs={{0,64},{8,72},{16,80},{24,88},{32,96},{40,104},{48,112},{56,120},{... | collective-permute-start | bytes 786440 | tf_op jit(solution)/shard_map/ppermute | solution.py:465
  35.1 14.8 %collective-permute-start.2 = (bf16[4,128,256]{2,1,0:T(8,128)(2,1)}, bf16[4,128,256]{2,1,0:T(8,128)(2,1)S(1)}, u32[]{:S(2)}, u32[]{:S(2)}) collective-permute-start(bf16[4,128,256]{2,1,0:T(8,128)(2,1)} %get-tuple-element.57), channel_id=1, source_target_pairs={{0,128},{8,136},{16,144},{24,152},{32,160},{40,168},{48,176},{56,1... | collective-permute-start | bytes 786440 | tf_op jit(solution)/shard_map/ppermute | solution.py:465
  37.9 12.5 %collective-permute-start.3 = (bf16[4,128,256]{2,1,0:T(8,128)(2,1)}, bf16[4,128,256]{2,1,0:T(8,128)(2,1)S(1)}, u32[]{:S(2)}, u32[]{:S(2)}) collective-permute-start(bf16[4,128,256]{2,1,0:T(8,128)(2,1)} %get-tuple-element.58), channel_id=1, source_target_pairs={{0,192},{8,200},{16,208},{24,216},{32,224},{40,232},{48,240},{56,2... | collective-permute-start | bytes 786440 | tf_op jit(solution)/shard_map/ppermute | solution.py:465
  38.3 12.2 %collective-permute-start.4 = (bf16[4,128,256]{2,1,0:T(8,128)(2,1)}, bf16[4,128,256]{2,1,0:T(8,128)(2,1)S(1)}, u32[]{:S(2)}, u32[]{:S(2)}) collective-permute-start(bf16[4,128,256]{2,1,0:T(8,128)(2,1)} %get-tuple-element.60), channel_id=1, source_target_pairs={{0,16},{8,24},{16,32},{24,40},{32,48},{40,56},{48,0},{56,8},{64,80... | collective-permute-start | bytes 786440 | tf_op jit(solution)/shard_map/ppermute | solution.py:465
  39.9 14.2 %collective-permute-start.5 = (bf16[4,128,256]{2,1,0:T(8,128)(2,1)}, bf16[4,128,256]{2,1,0:T(8,128)(2,1)S(1)}, u32[]{:S(2)}, u32[]{:S(2)}) collective-permute-start(bf16[4,128,256]{2,1,0:T(8,128)(2,1)} %get-tuple-element.61), channel_id=1, source_target_pairs={{0,32},{8,40},{16,48},{24,56},{32,0},{40,8},{48,16},{56,24},{64,96... | collective-permute-start | bytes 786440 | tf_op jit(solution)/shard_map/ppermute | solution.py:465
  43.2 10.9 %copy-start.4 = (bf16[4,128,256]{2,1,0:T(8,128)(2,1)}, bf16[4,128,256]{2,1,0:T(8,128)(2,1)S(1)}, u32[]{:S(2)}) copy-start(bf16[4,128,256]{2,1,0:T(8,128)(2,1)S(1)} %collective-permute-done.1.refs_1_) | copy-start | bytes 786436
  43.2 10.9 %collective-permute-start.6 = (bf16[4,128,256]{2,1,0:T(8,128)(2,1)}, bf16[4,128,256]{2,1,0:T(8,128)(2,1)S(1)}, u32[]{:S(2)}, u32[]{:S(2)}) collective-permute-start(bf16[4,128,256]{2,1,0:T(8,128)(2,1)} %get-tuple-element.62), channel_id=1, source_target_pairs={{0,48},{8,56},{16,0},{24,8},{32,16},{40,24},{48,32},{56,40},{64,11... | collective-permute-start | bytes 786440 | tf_op jit(solution)/shard_map/ppermute | solution.py:465
  49.8 4.3 %copy-start.5 = (bf16[4,128,256]{2,1,0:T(8,128)(2,1)}, bf16[4,128,256]{2,1,0:T(8,128)(2,1)S(1)}, u32[]{:S(2)}) copy-start(bf16[4,128,256]{2,1,0:T(8,128)(2,1)S(1)} %collective-permute-done.2.refs_2_) | copy-start | bytes 786436
  50.5 3.7 %copy-start.6 = (bf16[4,128,256]{2,1,0:T(8,128)(2,1)}, bf16[4,128,256]{2,1,0:T(8,128)(2,1)S(1)}, u32[]{:S(2)}) copy-start(bf16[4,128,256]{2,1,0:T(8,128)(2,1)S(1)} %collective-permute-done.3.refs_3_) | copy-start | bytes 786436
  50.5 3.7 %copy-start.7 = (bf16[4,128,256]{2,1,0:T(8,128)(2,1)}, bf16[4,128,256]{2,1,0:T(8,128)(2,1)S(1)}, u32[]{:S(2)}) copy-start(bf16[4,128,256]{2,1,0:T(8,128)(2,1)S(1)} %collective-permute-done.4.refs_5_) | copy-start | bytes 786436
  54.1 0.7 copy-start.8
  54.1 0.8 copy-start.9
  61.8 4.6 %copy-start = (bf16[8,256,512]{2,1,0:T(8,128)(2,1)}, bf16[8,256,512]{2,1,0:T(8,128)(2,1)S(1)}, u32[]{:S(2)}) copy-start(bf16[8,256,512]{2,1,0:T(8,128)(2,1)S(1)} %slice.9.mine_ref) | copy-start | bytes 6291460
  61.8 4.6 %collective-permute-start.7 = (bf16[8,256,512]{2,1,0:T(8,128)(2,1)S(1)}, bf16[8,256,512]{2,1,0:T(8,128)(2,1)}, u32[]{:S(2)}, u32[]{:S(2)}) collective-permute-start(bf16[8,256,512]{2,1,0:T(8,128)(2,1)S(1)} %slice.9.mine_ref), channel_id=1, source_target_pairs={{0,8},{8,0},{16,24},{24,16},{32,40},{40,32},{48,56},{56,48},{64,72... | collective-permute-start | bytes 6291464 | tf_op jit(solution)/shard_map/ppermute | solution.py:349
  66.4 14.9 %copy-start.21 = (f32[128,256]{1,0:T(8,128)S(1)}, f32[128,256]{1,0:T(8,128)}, u32[]{:S(2)}) copy-start(f32[128,256]{1,0:T(8,128)} %get-tuple-element.84) | copy-start | bytes 393220
  66.4 16.8 %copy-start.20 = (f32[128,256]{1,0:T(8,128)S(1)}, f32[128,256]{1,0:T(8,128)}, u32[]{:S(2)}) copy-start(f32[128,256]{1,0:T(8,128)} %get-tuple-element.85) | copy-start | bytes 393220
  66.4 18.4 %copy-start.19 = (f32[128,256]{1,0:T(8,128)S(1)}, f32[128,256]{1,0:T(8,128)}, u32[]{:S(2)}) copy-start(f32[128,256]{1,0:T(8,128)} %get-tuple-element.86) | copy-start | bytes 393220
  66.4 20.0 %copy-start.18 = (f32[128,256]{1,0:T(8,128)S(1)}, f32[128,256]{1,0:T(8,128)}, u32[]{:S(2)}) copy-start(f32[128,256]{1,0:T(8,128)} %get-tuple-element.88) | copy-start | bytes 393220
  66.4 20.3 %copy-start.17 = (f32[128,256]{1,0:T(8,128)S(1)}, f32[128,256]{1,0:T(8,128)}, u32[]{:S(2)}) copy-start(f32[128,256]{1,0:T(8,128)} %get-tuple-element.89) | copy-start | bytes 393220
  66.4 23.5 %copy-start.16 = (f32[128,256]{1,0:T(8,128)S(1)}, f32[128,256]{1,0:T(8,128)}, u32[]{:S(2)}) copy-start(f32[128,256]{1,0:T(8,128)} %get-tuple-element.90) | copy-start | bytes 393220
  75.2 24.5 %all-to-all-start = ((bf16[8,272,128]{2,1,0:T(8,128)(2,1)}), bf16[8,272,128]{2,1,0:T(8,128)(2,1)S(1)}, u32[]{:S(2)}, u32[]{:S(2)}) async-start(bf16[8,272,128]{2,1,0:T(8,128)(2,1)} %get-tuple-element.82), calls=%async_computation | async-start | bytes 1114112 | tf_op jit(solution)/shard_map/all_to_all | solution.py:423
  81.3 8.7 %collective-permute-start.8 = (f32[128,256]{1,0:T(8,128)S(1)}, f32[128,256]{1,0:T(8,128)S(1)}, u32[]{:S(2)}, u32[]{:S(2)}) collective-permute-start(f32[128,256]{1,0:T(8,128)S(1)} %copy-done.21), channel_id=1, source_target_pairs={{0,16},{8,24},{16,32},{24,40},{32,48},{40,56},{48,0},{56,8},{64,80... | collective-permute-start | bytes 393224 | tf_op jit(solution)/shard_map/ppermute | solution.py:465
  83.2 7.6 %collective-permute-start.9 = (f32[128,256]{1,0:T(8,128)S(1)}, f32[128,256]{1,0:T(8,128)S(1)}, u32[]{:S(2)}, u32[]{:S(2)}) collective-permute-start(f32[128,256]{1,0:T(8,128)S(1)} %copy-done.20), channel_id=1, source_target_pairs={{0,32},{8,40},{16,48},{24,56},{32,0},{40,8},{48,16},{56,24},{64,96... | collective-permute-start | bytes 393224 | tf_op jit(solution)/shard_map/ppermute | solution.py:465
  84.8 6.4 %collective-permute-start.10 = (f32[128,256]{1,0:T(8,128)S(1)}, f32[128,256]{1,0:T(8,128)S(1)}, u32[]{:S(2)}, u32[]{:S(2)}) collective-permute-start(f32[128,256]{1,0:T(8,128)S(1)} %copy-done.19), channel_id=1, source_target_pairs={{0,48},{8,56},{16,0},{24,8},{32,16},{40,24},{48,32},{56,40},{64,11... | collective-permute-start | bytes 393224 | tf_op jit(solution)/shard_map/ppermute | solution.py:465
  86.5 5.8 %collective-permute-start.11 = (f32[128,256]{1,0:T(8,128)S(1)}, f32[128,256]{1,0:T(8,128)S(1)}, u32[]{:S(2)}, u32[]{:S(2)}) collective-permute-start(f32[128,256]{1,0:T(8,128)S(1)} %copy-done.18), channel_id=1, source_target_pairs={{0,64},{8,72},{16,80},{24,88},{32,96},{40,104},{48,112},{56,120},{... | collective-permute-start | bytes 393224 | tf_op jit(solution)/shard_map/ppermute | solution.py:465
  86.8 7.2 %collective-permute-start.12 = (f32[128,256]{1,0:T(8,128)S(1)}, f32[128,256]{1,0:T(8,128)S(1)}, u32[]{:S(2)}, u32[]{:S(2)}) collective-permute-start(f32[128,256]{1,0:T(8,128)S(1)} %copy-done.17), channel_id=1, source_target_pairs={{0,128},{8,136},{16,144},{24,152},{32,160},{40,168},{48,176},{56,1... | collective-permute-start | bytes 393224 | tf_op jit(solution)/shard_map/ppermute | solution.py:465
  90.0 5.3 %copy-start.10 = (f32[128,256]{1,0:T(8,128)}, f32[128,256]{1,0:T(8,128)S(1)}, u32[]{:S(2)}) copy-start(f32[128,256]{1,0:T(8,128)S(1)} %collective-permute-done.8.refs_1_) | copy-start | bytes 393220
  90.0 5.3 %collective-permute-start.13 = (f32[128,256]{1,0:T(8,128)S(1)}, f32[128,256]{1,0:T(8,128)S(1)}, u32[]{:S(2)}, u32[]{:S(2)}) collective-permute-start(f32[128,256]{1,0:T(8,128)S(1)} %copy-done.16), channel_id=1, source_target_pairs={{0,192},{8,200},{16,208},{24,216},{32,224},{40,232},{48,240},{56,2... | collective-permute-start | bytes 393224 | tf_op jit(solution)/shard_map/ppermute | solution.py:465
  90.8 4.5 %copy-start.11 = (f32[128,256]{1,0:T(8,128)}, f32[128,256]{1,0:T(8,128)S(1)}, u32[]{:S(2)}) copy-start(f32[128,256]{1,0:T(8,128)S(1)} %collective-permute-done.9.refs_2_) | copy-start | bytes 393220
  91.2 4.1 %copy-start.12 = (f32[128,256]{1,0:T(8,128)}, f32[128,256]{1,0:T(8,128)S(1)}, u32[]{:S(2)}) copy-start(f32[128,256]{1,0:T(8,128)S(1)} %collective-permute-done.10.refs_3_) | copy-start | bytes 393220
  92.3 3.0 %copy-start.13 = (f32[128,256]{1,0:T(8,128)}, f32[128,256]{1,0:T(8,128)S(1)}, u32[]{:S(2)}) copy-start(f32[128,256]{1,0:T(8,128)S(1)} %collective-permute-done.11.refs_5_) | copy-start | bytes 393220
  93.9 1.4 %copy-start.14 = (f32[128,256]{1,0:T(8,128)}, f32[128,256]{1,0:T(8,128)S(1)}, u32[]{:S(2)}) copy-start(f32[128,256]{1,0:T(8,128)S(1)} %collective-permute-done.12.refs_6_) | copy-start | bytes 393220
  95.3 0.6 copy-start.15
  99.8 20.3 %copy-start.2 = (bf16[8,272,128]{2,1,0:T(8,128)(2,1)}, bf16[8,272,128]{2,1,0:T(8,128)(2,1)S(1)}, u32[]{:S(2)}) copy-start(bf16[8,272,128]{2,1,0:T(8,128)(2,1)S(1)} %all-to-all-done.adj_ref) | copy-start | bytes 1671172
  99.8 1.2 collective-permute-start.14
  101.0 9.8 %collective-permute-start.17 = (f32[2,128]{1,0:T(2,128)S(1)}, f32[2,128]{1,0:T(2,128)S(1)}, u32[]{:S(2)}, u32[]{:S(2)}) collective-permute-start(f32[2,128]{1,0:T(2,128)S(1)} %add.32), channel_id=1, source_target_pairs={{0,48},{8,56},{16,32},{24,40},{32,16},{40,24},{48,0},{56,8},{64,11... | collective-permute-start | bytes 3080 | tf_op jit(solution)/shard_map/ppermute | solution.py:469
  103.0 7.8 %collective-permute-start.16 = (f32[2,128]{1,0:T(2,128)S(1)}, f32[2,128]{1,0:T(2,128)S(1)}, u32[]{:S(2)}, u32[]{:S(2)}) collective-permute-start(f32[2,128]{1,0:T(2,128)S(1)} %add.32), channel_id=1, source_target_pairs={{0,16},{8,24},{16,0},{24,8},{32,48},{40,56},{48,32},{56,40},{64,80... | collective-permute-start | bytes 3080 | tf_op jit(solution)/shard_map/ppermute | solution.py:469
  103.5 7.4 %collective-permute-start.15 = (f32[2,128]{1,0:T(2,128)S(1)}, f32[2,128]{1,0:T(2,128)S(1)}, u32[]{:S(2)}, u32[]{:S(2)}) collective-permute-start(f32[2,128]{1,0:T(2,128)S(1)} %add.32), channel_id=1, source_target_pairs={{0,32},{8,40},{16,48},{24,56},{32,0},{40,8},{48,16},{56,24},{64,96... | collective-permute-start | bytes 3080 | tf_op jit(solution)/shard_map/ppermute | solution.py:469
  105.7 17.7 %all-to-all-start.1 = ((f32[8,32,256]{2,1,0:T(8,128)}), f32[8,32,256]{2,1,0:T(8,128)S(1)}, u32[]{:S(2)}, u32[]{:S(2)}) async-start(f32[8,32,256]{2,1,0:T(8,128)} %shard_map.128), calls=%async_computation.1 | async-start | bytes 524288 | tf_op jit(solution)/shard_map/all_to_all | solution.py:430
  110.9 11.9 %collective-permute-start.20 = (f32[2,128]{1,0:T(2,128)S(1)}, f32[2,128]{1,0:T(2,128)S(1)}, u32[]{:S(2)}, u32[]{:S(2)}) collective-permute-start(f32[2,128]{1,0:T(2,128)S(1)} %add_add_fusion.1), channel_id=1, source_target_pairs={{0,192},{8,200},{16,208},{24,216},{32,224},{40,232},{48,240},{56,2... | collective-permute-start | bytes 3080 | tf_op jit(solution)/shard_map/ppermute | solution.py:469
  111.5 11.2 %collective-permute-start.19 = (f32[2,128]{1,0:T(2,128)S(1)}, f32[2,128]{1,0:T(2,128)S(1)}, u32[]{:S(2)}, u32[]{:S(2)}) collective-permute-start(f32[2,128]{1,0:T(2,128)S(1)} %add_add_fusion.1), channel_id=1, source_target_pairs={{0,64},{8,72},{16,80},{24,88},{32,96},{40,104},{48,112},{56,120},{... | collective-permute-start | bytes 3080 | tf_op jit(solution)/shard_map/ppermute | solution.py:469
  115.1 7.6 %collective-permute-start.18 = (f32[2,128]{1,0:T(2,128)S(1)}, f32[2,128]{1,0:T(2,128)S(1)}, u32[]{:S(2)}, u32[]{:S(2)}) collective-permute-start(f32[2,128]{1,0:T(2,128)S(1)} %add_add_fusion.1), channel_id=1, source_target_pairs={{0,128},{8,136},{16,144},{24,152},{32,160},{40,168},{48,176},{56,1... | collective-permute-start | bytes 3080 | tf_op jit(solution)/shard_map/ppermute | solution.py:469
  123.4 0.7 copy-start.3
Sparse Core Ops, SparseCore 0:
  11.5 48.5 all-gather.2

commit v4 on v3

--- a/solution.py
+++ b/solution.py
@@ -14,6 +14,7 @@
 HP = 256
 N = 128
 SIDE = 4
+WEIGHT_STEPS = 2
 ROWS = 128
 PLANE = 16
 DEPTH = 8
@@ -41,7 +42,9 @@
     return high, (a - high.astype(F32)).astype(BF16)
 
 
-def call(kernel, outs, args, smem=(), hbm=(), scratch=(), flops=0, bytes_accessed=0):
+def call(
+    kernel, outs, args, smem=(), hbm=(), scratch=(), limit=VMEM_LIMIT, flops=0, bytes_accessed=0
+):
     def whole(dims):
         return pl.BlockSpec(dims, lambda _: (0,) * len(dims))
 
@@ -57,7 +60,7 @@
         in_specs=[spec(i, arg) for i, arg in enumerate(args)],
         out_specs=jax.tree.map(lambda out: whole(out.shape), outs),
         scratch_shapes=scratch,
-        compiler_params=pltpu.CompilerParams(vmem_limit_bytes=VMEM_LIMIT),
+        compiler_params=pltpu.CompilerParams(vmem_limit_bytes=limit),
         cost_estimate=pl.CostEstimate(
             flops=flops, bytes_accessed=bytes_accessed, transcendentals=0
         ),
@@ -86,8 +89,12 @@
     return rows, cols, count, 256.0 * nn(high, upper) + nn(low, upper)
 
 
-def payload_kernel(place_ref, rate_ref, half_ref, x_ref, inj_ref, code_ref, state_ref, pay_ref, chain_ref):
-    pay_ref[:HP, :] = half_ref[...]
+def payload_kernel(
+    rate_ref, weight_ref, x_ref, inj_ref, code_ref, state_ref, pay_ref, chain_ref, sem,
+):
+    core = lax.rem(lax.axis_index("dp"), 2)
+    half = weight_ref.at[:, pl.ds(pl.multiple_of(core * 512, 512), 512)]
+    copy = fetch(half, pay_ref.at[pl.ds(0, HP), :], sem)
     count = counts(code_ref[...])[3]
     inject_f = inj_ref[...].astype(F32)
     for h in range(2):
@@ -104,6 +111,7 @@
         for k, term in enumerate(split(chain_ref[h])):
             at = (2 * k + h) * 128
             pay_ref[HP : HP + N + 8, at : at + 128] = term
+    copy.wait()
 
 
 def forward_kernel(rate_ref, x_ref, inj_ref, rd_ref, code_ref, state_ref, out_t_ref, mix_ref):
@@ -158,7 +166,7 @@
             keep = rows[rs, :width] >= cols[rs, :width]
             spread = jnp.where(keep, spread, 0.0)
             wts = jnp.where(keep, jnp.exp(spread), 0.0)
-            wts_ref[h, rs, :width] = wts
+            wts_ref[h, rs, :width] = wts.astype(BF16)
             r_hi, r_lo = split(inter * wts * spread)
             part_ref[rs, hs] = weighted[rs] + nn(r_hi, x[:width]) + nn(r_lo, x[:width])
     aux_ref[...] = aux
@@ -170,15 +178,15 @@
     return copy
 
 
-def weight_kernel(place_ref, out_t_ref, cot_ref, send_ref, keep_ref):
-    core = place_ref[0]
-    for k in range(4):
+def weight_kernel(out_t_ref, cot_ref, send_ref, keep_ref):
+    core = lax.rem(lax.axis_index("dp"), 2)
+    for k in range(PLANE // WEIGHT_STEPS):
         for ref, side in ((send_ref, 1 - core), (keep_ref, core)):
             block = cot_ref[:, pl.ds(pl.multiple_of((2 * k + side) * 256, 256), 256)]
             ref[k] = nn(out_t_ref[...], block).astype(BF16)
 
 
-def gridded(kernel, steps, in_specs, out_specs, outs, args, scratch=()):
+def gridded(kernel, steps, in_specs, out_specs, outs, args, scratch=(), limit=VMEM_LIMIT):
     return pl.pallas_call(
         kernel,
         out_shape=outs,
@@ -189,7 +197,7 @@
             out_specs=out_specs,
             scratch_shapes=scratch,
         ),
-        compiler_params=pltpu.CompilerParams(vmem_limit_bytes=VMEM_LIMIT),
+        compiler_params=pltpu.CompilerParams(vmem_limit_bytes=limit),
         cost_estimate=pl.CostEstimate(flops=0, bytes_accessed=0, transcendentals=0),
     )(*args)
 
@@ -228,13 +236,6 @@
         total = total + ins[part * 4 + 2][...] + ins[part * 4 + 3][...]
         for k in range(4):
             out_ref[part * 4 + k] = total[k * 32 : k * 32 + 32, :]
-
-
-def depth_sum_kernel(in_ref, out_ref):
-    total = in_ref[0]
-    for k in range(1, DEPTH):
-        total = total + in_ref[k]
-    out_ref[...] = total
 
 
 def rate_vector_kernel(
@@ -261,7 +262,7 @@
     core = place_ref[0]
     step = pl.program_id(0)
     total = None
-    for k in range(2):
+    for k in range(4):
         first = cot_ref[:, pl.ds(pl.multiple_of((2 * k + core) * 512, 512), 512)]
         second = cot_ref[:, pl.ds(pl.multiple_of((2 * k + 1 - core) * 512, 512), 512)]
         terms = nt(first, mine_ref[k]) + nt(second, other_ref[k])
@@ -315,7 +316,7 @@
         for i in range(T // ROWS):
             rs = slice(i * ROWS, i * ROWS + ROWS)
             width = (i + 1) * ROWS
-            pairing = (nt(g[rs], x[:width]) * wts_ref[h, rs, :width]).astype(BF16)
+            pairing = (nt(g[rs], x[:width]) * wts_ref[h, rs, :width].astype(F32)).astype(BF16)
             through = nn(g[rs], state) * aux_ref[rs, 2 + h : 3 + h]
             read_part = nn(pairing, inject[:width]) + through
             if h == 0:
@@ -362,16 +363,10 @@
     me = lax.axis_index("dp")
     place = jnp.stack([core, lax.axis_index("ctx"), me // 8, me // 2 % SIDE]).astype(jnp.int32)
 
-    pay, chain = gridded(
-        payload_kernel, 1,
-        [
-            pl.BlockSpec(memory_space=pltpu.SMEM),
-            pl.BlockSpec((HP, 512), lambda i, place: (0, place[0])),
-            fixed((T, HP)), fixed((T, N)), fixed((2, T)), fixed((2, N, N)),
-        ],
-        [fixed((HP + N + 8, 512)), fixed((2, N + 8, 128))],
-        [shape((HP + N + 8, 512), BF16), shape((2, N + 8, 128))],
-        (place, decay_rate, out_weight, x, inject, code.T, state),
+    pay, chain = call(
+        payload_kernel, [shape((HP + N + 8, 512), BF16), shape((2, N + 8, 128))],
+        (decay_rate, out_weight, x, inject, code.T, state), smem=(0,), hbm=(1,),
+        scratch=[pltpu.SemaphoreType.DMA],
     )
     gathered = lax.all_gather(pay, "ctx", axis=0)
     x, _ = lax.optimization_barrier((x, chain))
@@ -380,21 +375,29 @@
         (decay_rate, x, inject, read, code.T, state), smem=(0,),
     )
     half_terms = shape((PLANE, 256, 256), BF16)
-    part_spec = pl.BlockSpec((4, 256, 256), lambda i, place: (i, 0, 0))
-    sent, kept = gridded(
-        weight_kernel, 4,
-        [fixed((HP, T)), pl.BlockSpec((T, 2048), lambda i, place: (0, i))],
-        [part_spec, part_spec], [half_terms, half_terms], (place, out_t, cot),
-    )
+    width = D // WEIGHT_STEPS
+    part_spec = pl.BlockSpec((PLANE // WEIGHT_STEPS, 256, 256), lambda i: (i, 0, 0))
+    sent, kept = pl.pallas_call(
+        weight_kernel,
+        grid=(WEIGHT_STEPS,),
+        out_shape=[half_terms, half_terms],
+        in_specs=[
+            pl.BlockSpec((HP, T), lambda i: (0, 0)),
+            pl.BlockSpec((T, width), lambda i: (0, i)),
+        ],
+        out_specs=[part_spec, part_spec],
+        compiler_params=pltpu.CompilerParams(vmem_limit_bytes=VMEM_LIMIT),
+        cost_estimate=pl.CostEstimate(flops=0, bytes_accessed=0, transcendentals=0),
+    )(out_t, cot)
     parts = core_sum(place, kept, swap_cores(sent))
     first = exchanged(parts[:SIDE], 8)
     second = exchanged(parts[SIDE:], 2)
-    parts = call(line_sum_kernel, [shape((128, 256))] * 8, (place, *first, *second), smem=(0,))
+    parts = call(line_sum_kernel, [shape((128, 256))] * 8, (place, *first, *second), smem=(0,), limit=16 << 20)
 
     read_later, _ = lax.optimization_barrier((read, kept))
     wts, part, from_start, aux = call(
         prepare_kernel,
-        [shape((2, T, T)), shape((T, HP)), shape((2, T, N), BF16), shape((T, 128))],
+        [shape((2, T, T), BF16), shape((T, HP)), shape((2, T, N), BF16), shape((T, 128))],
         (decay_rate, x, inject, read_later, code.T, state), smem=(0,),
     )
 
@@ -406,11 +409,11 @@
         (place, part, read, aux, gathered), smem=(0,), hbm=(4,),
         scratch=[pltpu.VMEM((DEPTH, N + 8, 512), BF16), pltpu.SemaphoreType.DMA],
     )
-    one = pl.BlockSpec((2, HP, 512), lambda i, place: (i, 0, 0))
+    one = pl.BlockSpec((4, HP, 512), lambda i, place: (i, 0, 0))
     grad, pay = gridded(
-        output_grad_kernel, 4,
+        output_grad_kernel, 2,
         [
-            pl.BlockSpec((T, 2048), lambda i, place: (0, i)), one, one, fixed((2, T, N)),
+            pl.BlockSpec((T, 4096), lambda i, place: (0, i)), one, one, fixed((2, T, N)),
             fixed((T, HP)),
         ],
         [fixed((T, HP)), fixed((DEPTH, HP + 16, 128))],
@@ -425,7 +428,8 @@
         backward_kernel, [shape((T, HP)), shape((T, N)), shape((T, N))],
         (grad, x, inject, read, state, mix, wts, aux),
     )
-    blocks = call(plane_sum_kernel, shape((DEPTH, 32, 256)), (*first, *second))
+    first[1:], _ = lax.optimization_barrier((first[1:], gi))
+    blocks = call(plane_sum_kernel, shape((DEPTH, 32, 256)), (*first, *second), limit=16 << 20)
     blocks, pay = lax.optimization_barrier((blocks, pay))
     blocks = lax.all_to_all(blocks, "ctx", 0, 0, tiled=True)
     rate = jnp.sum(pay[:, HP:, :].astype(F32).reshape(DEPTH, 2, 8, 128), axis=(0, 2))
@@ -434,7 +438,7 @@
         finish_kernel, [shape((T, HP), BF16), shape((T, N))],
         (place, gi, ginj, x, inject, aux, pay, decay), smem=(0,),
     )
-    grad_weight = call(depth_sum_kernel, shape((32, 256)), (blocks,))
+    grad_weight = jnp.sum(blocks, axis=0)
     tokens = T * lax.axis_size("dp") * lax.axis_size("ctx")
     return grad_input[None], grad_inject[None], grad_read[None], grad_weight, rate[:, 0] / tokens
 
@@ -450,7 +454,7 @@
     part = (SIDE, 128, 256)
     return gridded(
         core_sum_kernel, SIDE, [by_x, by_x, by_y, by_y], [fixed(part)] * 8,
-        [shape(part, BF16)] * 8, (place, kept, recv, kept, recv),
+        [shape(part, BF16)] * 8, (place, kept, recv, kept, recv), limit=16 << 20,
     )
 
 

time: 135 us -> 126 us (0.933)
  Pallas kernels: 50.7 us -> 39.2 us
  waiting for transfers between devices: 19.6 us -> 27.5 us
  starting transfers between devices: 41.4 us -> 39 us
  local copies, waits for them, and re-layouts: 5.23 us -> 3.4 us
    pallas_call x4 -> x2, Pallas kernels: 25.5 us -> 10 us  [gridded(): pl.pallas_call(kernel, out_shape=outs, grid_spec=pltpu.PrefetchScalarGrid...]
    all_gather x1, waiting for transfers between devices: 2.43 us -> 9.93 us  [local(): gathered = lax.all_gather(pay, 'ctx', axis=0)]
    pallas_call x0 -> x1, Pallas kernels: none -> 6.19 us  [local(): pl.pallas_call(weight_kernel, grid=(WEIGHT_STEPS,), out_shape=[half_terms...]
    ppermute x12, waiting for transfers between devices: 9.83 us -> 4.57 us  [exchanged(): lax.ppermute(parts[d], 'dp', pairs(d))]
    all_to_all x1, waiting for transfers between devices: 0.01 us -> 3.87 us  [local(): blocks = lax.all_to_all(blocks, 'ctx', 0, 0, tiled=True)]
    pallas_call x8, Pallas kernels: 25.3 us -> 22.9 us  [call(): pl.pallas_call(kernel, grid=(1,), out_shape=outs, in_specs=[spec(i, arg)...]
    unnamed x44 -> x8, local copies, waits for them, and re-layouts: 3.5 us -> 1.67 us
    all_to_all x1, starting transfers between devices: 6.05 us -> 4.33 us  [local(): pay = lax.all_to_all(pay, 'ctx', 0, 0, tiled=True)]
  transfers between devices with their start and end apart: 24 -> 24, of which waited for: 13 -> 10; matrix products, arithmetic and copies ran while one was open for 0% -> 1% of each run, Pallas kernels for 28% -> 23%
where the time goes in v4:
time: 126 us; the launch traced here: 125 us
  Pallas kernels  39.2 us (31%)
  starting transfers between devices  39 us (31%)
  waiting for transfers between devices  27.5 us (22%)
  between operations  14.2 us (11%)
  local copies, waits for them, and re-layouts  3.4 us (3%)
  other arithmetic  1.38 us (1%)
    pallas_call x8, Pallas kernels, call(): pl.pallas_call(kernel, grid=(1,), out_shape=outs, in_specs=[spec(i, arg)...  22.9 us
    ppermute x12, starting transfers between devices, exchanged(): lax.ppermute(parts[d], 'dp', pairs(d))  21.8 us
    pallas_call x2, Pallas kernels, gridded(): pl.pallas_call(kernel, out_shape=outs, grid_spec=pltpu.PrefetchScalarGrid...  10 us
    all_gather x1, waiting for transfers between devices, local(): gathered = lax.all_gather(pay, 'ctx', axis=0)  9.93 us
    ppermute x7, starting transfers between devices, flipped(): return lax.ppermute(value, 'dp', [(i, i ^ bits) for i in range(2 * PLANE)])  8.43 us
    pallas_call x1, Pallas kernels, local(): pl.pallas_call(weight_kernel, grid=(WEIGHT_STEPS,), out_shape=[half_terms...  6.19 us
    ppermute x12, waiting for transfers between devices, exchanged(): lax.ppermute(parts[d], 'dp', pairs(d))  4.57 us
    ppermute x2, waiting for transfers between devices, swap_cores(): return lax.ppermute(value, 'dp', [(i, i ^ 1) for i in range(2 * PLANE)])  4.35 us
  transfers between devices with their start and end apart: 24, of which 10 were waited for; matrix products, arithmetic and copies ran while one was open for 1% of the time, Pallas kernels for 23%

profile of v4, /device:TPU:2, one launch (start us, length us, event | category | flops | bytes accessed | tf_op | source)
XLA Modules:
  0.0 124.7 jit_solution(14640859940554241912)
XLA Ops:
  7.2 0.0 all-gather.3.cloned.1.call-start
  7.2 2.8 %shard_map.119 = (bf16[392,512]{1,0:T(8,128)(2,1)}, f32[2,136,128]{2,1,0:T(8,128)}) custom-call(f32[2]{0:T(128)} %rate_ref.5, bf16[256,1024]{1,0:T(8,128)(2,1)} %weight_ref.1, bf16[512,256]{1,0:T(8,128)(2,1)} %bitcast.28, bf16[512,128]{1,0:T(8,128)(2,1)} %bitcast.33, s32[2,512]{1,0:T(2,128)} %bitcast.46, f32[2,128,128]{2,1,0:T(8,128)} %bitcast.42), custom_call_target="tpu_custom_call" | custom-call | tf_op jit(solution)/shard_map/pallas_call | solution.py:56
  10.1 0.0 all-gather.3.cloned.1.call-update
  10.1 3.3 %shard_map.120 = (bf16[256,512]{1,0:T(8,128)(2,1)}, bf16[2,512,512]{2,1,0:T(8,128)(2,1)}) custom-call(f32[2]{0:T(128)} %rate_ref.5, bf16[512,256]{1,0:T(8,128)(2,1)} %bitcast.29, bf16[512,128]{1,0:T(8,128)(2,1)} %bitcast.34, bf16[512,128]{1,0:T(8,128)(2,1)} %bitcast.38, s32[2,512]{1,0:T(2,128)} %bitcast.47, f32[2,128,128]{2,1,0:T(8,128)} %bitcast.43), custom_call_target="tpu_custom_call" | custom-call | tf_op jit(solution)/shard_map/pallas_call | solution.py:56
  13.4 6.2 %shard_map.121 = (bf16[16,256,256]{2,1,0:T(8,128)(2,1)}, bf16[16,256,256]{2,1,0:T(8,128)(2,1)}) custom-call(bf16[256,512]{1,0:T(8,128)(2,1)} %get-tuple-element.55.out_t_ref, bf16[512,8192]{1,0:T(8,128)(2,1)} %bitcast.24), custom_call_target="tpu_custom_call" | custom-call | tf_op jit(solution)/shard_map/pallas_call | solution.py:380
  19.6 0.0 collective-permute-start
  19.6 0.1 pad_add_fusion.place_ref
  19.7 4.3 %collective-permute-done = bf16[16,256,256]{2,1,0:T(8,128)(2,1)S(1)} collective-permute-done((bf16[16,256,256]{2,1,0:T(8,128)(2,1)}, bf16[16,256,256]{2,1,0:T(8,128)(2,1)S(1)}, u32[]{:S(2)}, u32[]{:S(2)}) %collective-permute-start) | collective-permute-done | bytes 2097184 | tf_op jit(solution)/shard_map/ppermute | solution.py:350
  24.0 1.7 %copy-done = bf16[16,256,256]{2,1,0:T(8,128)(2,1)S(1)} copy-done((bf16[16,256,256]{2,1,0:T(8,128)(2,1)S(1)}, bf16[16,256,256]{2,1,0:T(8,128)(2,1)}, u32[]{:S(2)}) %copy-start) | copy-done | bytes 2097176
  25.6 2.0 %shard_map.122 = (bf16[4,128,256]{2,1,0:T(8,128)(2,1)S(1)}, bf16[4,128,256]{2,1,0:T(8,128)(2,1)S(1)}, bf16[4,128,256]{2,1,0:T(8,128)(2,1)S(1)}, bf16[4,128,256]{...) custom-call(s32[4]{0:T(128)S(1)} %pad_add_fusion.place_ref, ...), custom_call_target="tpu_custom_call" | custom-call | tf_op jit(solution)/shard_map/pallas_call | solution.py:190
  27.7 1.6 %collective-permute-start.1 = (bf16[4,128,256]{2,1,0:T(8,128)(2,1)S(1)}, bf16[4,128,256]{2,1,0:T(8,128)(2,1)S(1)}, u32[]{:S(2)}, u32[]{:S(2)}) collective-permute-start(bf16[4,128,256]{2,1,0:T(8,128)(2,1)S(1)} %get-tuple-element.59), channel_id=1, source_target_pairs={{0,64},{8,72},{16,80},{24,88},{32,96},{40,104},{48,112},{56,120},{... | collective-permute-start | bytes 786440 | tf_op jit(solution)/shard_map/ppermute | solution.py:469
  29.3 2.8 %collective-permute-start.2 = (bf16[4,128,256]{2,1,0:T(8,128)(2,1)S(1)}, bf16[4,128,256]{2,1,0:T(8,128)(2,1)S(1)}, u32[]{:S(2)}, u32[]{:S(2)}) collective-permute-start(bf16[4,128,256]{2,1,0:T(8,128)(2,1)S(1)} %get-tuple-element.60), channel_id=1, source_target_pairs={{0,128},{8,136},{16,144},{24,152},{32,160},{40,168},{48,176},{56,1... | collective-permute-start | bytes 786440 | tf_op jit(solution)/shard_map/ppermute | solution.py:469
  32.1 0.5 collective-permute-start.3
  32.5 1.6 %collective-permute-start.4 = (bf16[4,128,256]{2,1,0:T(8,128)(2,1)S(1)}, bf16[4,128,256]{2,1,0:T(8,128)(2,1)S(1)}, u32[]{:S(2)}, u32[]{:S(2)}) collective-permute-start(bf16[4,128,256]{2,1,0:T(8,128)(2,1)S(1)} %get-tuple-element.63), channel_id=1, source_target_pairs={{0,16},{8,24},{16,32},{24,40},{32,48},{40,56},{48,0},{56,8},{64,80... | collective-permute-start | bytes 786440 | tf_op jit(solution)/shard_map/ppermute | solution.py:469
  34.1 2.9 %collective-permute-start.5 = (bf16[4,128,256]{2,1,0:T(8,128)(2,1)S(1)}, bf16[4,128,256]{2,1,0:T(8,128)(2,1)S(1)}, u32[]{:S(2)}, u32[]{:S(2)}) collective-permute-start(bf16[4,128,256]{2,1,0:T(8,128)(2,1)S(1)} %get-tuple-element.64), channel_id=1, source_target_pairs={{0,32},{8,40},{16,48},{24,56},{32,0},{40,8},{48,16},{56,24},{64,96... | collective-permute-start | bytes 786440 | tf_op jit(solution)/shard_map/ppermute | solution.py:469
  37.0 0.1 collective-permute-done.1.refs_1_
  37.1 2.8 %collective-permute-start.6 = (bf16[4,128,256]{2,1,0:T(8,128)(2,1)S(1)}, bf16[4,128,256]{2,1,0:T(8,128)(2,1)S(1)}, u32[]{:S(2)}, u32[]{:S(2)}) collective-permute-start(bf16[4,128,256]{2,1,0:T(8,128)(2,1)S(1)} %get-tuple-element.65), channel_id=1, source_target_pairs={{0,48},{8,56},{16,0},{24,8},{32,16},{40,24},{48,32},{56,40},{64,11... | collective-permute-start | bytes 786440 | tf_op jit(solution)/shard_map/ppermute | solution.py:469
  39.9 3.7 %shard_map.124 = (bf16[2,512,512]{2,1,0:T(8,128)(2,1)}, f32[512,256]{1,0:T(8,128)}, bf16[2,512,128]{2,1,0:T(8,128)(2,1)}, f32[512,128]{1,0:T(8,128)}) custom-call(f32[2]{0:T(128)} %rate_ref.5, bf16[512,256]{1,0:T(8,128)(2,1)} %bitcast.30, bf16[512,128]{1,0:T(8,128)(2,1)} %bitcast.35, bf16[512,128]{1,0:T(8,128)(2,1)} %bitcast.39, s32[2,512]{1,0:T(2,128)} %bitcast.48, ...), custom_call_target="tpu_custom_call" | custom-call | tf_op jit(solution)/shard_map/pallas_call | solution.py:56
  43.6 0.0 collective-permute-done.2.refs_2_
  43.6 0.8 collective-permute-done.3.refs_3_
  44.5 0.0 collective-permute-done.4.refs_5_
  44.5 3.6 %collective-permute-done.5.refs_6_ = bf16[4,128,256]{2,1,0:T(8,128)(2,1)S(1)} collective-permute-done((bf16[4,128,256]{2,1,0:T(8,128)(2,1)S(1)}, bf16[4,128,256]{2,1,0:T(8,128)(2,1)S(1)}, u32[]{:S(2)}, u32[]{:S(2)}) %collective-permute-start.5) | collective-permute-done | bytes 262176 | tf_op jit(solution)/shard_map/ppermute | solution.py:469
  48.1 0.0 collective-permute-done.6.refs_7_
  48.1 0.8 shard_map.123
  48.9 9.9 %all-gather.3.cloned.1.call-done = bf16[3136,512]{1,0:T(8,128)(2,1)} async-done(((bf16[392,512]{1,0:T(8,128)(2,1)}), bf16[3136,512]{1,0:T(8,128)(2,1)}) %all-gather.3.cloned.1.call-update) | async-done | bytes 3211280 | tf_op jit(solution)/shard_map/all_gather | solution.py:371
  58.8 1.7 %slice.9.mine_ref = bf16[8,256,512]{2,1,0:T(8,128)(2,1)S(1)} slice(bf16[8,392,512]{2,1,0:T(8,128)(2,1)} %bitcast.26), slice={[0:8], [0:256], [0:512]} | slice | bytes 4194304 | tf_op jit(solution)/shard_map/slice | solution.py:405
  60.5 0.3 collective-permute-start.7
  60.8 4.2 %shard_map.125 = (f32[512,256]{1,0:T(8,128)}, f32[8,16,128]{2,1,0:T(8,128)}) custom-call(s32[4]{0:T(128)} %copy-done.1, f32[512,256]{1,0:T(8,128)} %get-tuple-element.78.part_ref, bf16[512,128]{1,0:T(8,128)(2,1)} %bitcast.40, f32[512,128]{1,0:T(8,128)} %get-tuple-element.75.aux_ref, bf16[8,392,512]{2,1,0:T(8,128)(2,1)} %bitcast.27), custom_call_target="tpu_custom_call" | custom-call | tf_op jit(solution)/shard_map/pallas_call | solution.py:56
  65.0 0.1 collective-permute-done.7.other_ref
  65.1 8.0 %shard_map.126 = (bf16[512,256]{1,0:T(8,128)(2,1)}, bf16[8,272,128]{2,1,0:T(8,128)(2,1)}) custom-call(s32[4]{0:T(128)} %copy-done.1, bf16[512,8192]{1,0:T(8,128)(2,1)} %bitcast.25, bf16[8,256,512]{2,1,0:T(8,128)(2,1)} %copy-done.2, bf16[8,256,512]{2,1,0:T(8,128)(2,1)} %collective-permute-done.7.other_ref, bf16[2,512,128]{2,1,0:T(8,128)(2,1)} %get-tuple-element.77.fr_ref, ...), custom_call_target="tpu_custom_call" | custom-call | tf_op jit(solution)/shard_map/pallas_call | solution.py:190
  73.1 4.3 %all-to-all-start = ((bf16[8,272,128]{2,1,0:T(8,128)(2,1)}), bf16[8,272,128]{2,1,0:T(8,128)(2,1)S(1)}, u32[]{:S(2)}, u32[]{:S(2)}) async-start(bf16[8,272,128]{2,1,0:T(8,128)(2,1)} %get-tuple-element.85), calls=%async_computation | async-start | bytes 1114112 | tf_op jit(solution)/shard_map/all_to_all | solution.py:426
  77.4 2.7 %collective-permute-start.10 = (f32[128,256]{1,0:T(8,128)S(1)}, f32[128,256]{1,0:T(8,128)S(1)}, u32[]{:S(2)}, u32[]{:S(2)}) collective-permute-start(f32[128,256]{1,0:T(8,128)S(1)} %get-tuple-element.89), channel_id=1, source_target_pairs={{0,48},{8,56},{16,0},{24,8},{32,16},{40,24},{48,32},{56,40},{64,11... | collective-permute-start | bytes 393224 | tf_op jit(solution)/shard_map/ppermute | solution.py:469
  80.2 0.0 collective-permute-start.8
  80.2 2.3 %collective-permute-start.9 = (f32[128,256]{1,0:T(8,128)S(1)}, f32[128,256]{1,0:T(8,128)S(1)}, u32[]{:S(2)}, u32[]{:S(2)}) collective-permute-start(f32[128,256]{1,0:T(8,128)S(1)} %get-tuple-element.88), channel_id=1, source_target_pairs={{0,32},{8,40},{16,48},{24,56},{32,0},{40,8},{48,16},{56,24},{64,96... | collective-permute-start | bytes 393224 | tf_op jit(solution)/shard_map/ppermute | solution.py:469
  82.5 1.5 %collective-permute-start.11 = (f32[128,256]{1,0:T(8,128)S(1)}, f32[128,256]{1,0:T(8,128)S(1)}, u32[]{:S(2)}, u32[]{:S(2)}) collective-permute-start(f32[128,256]{1,0:T(8,128)S(1)} %get-tuple-element.94), channel_id=1, source_target_pairs={{0,64},{8,72},{16,80},{24,88},{32,96},{40,104},{48,112},{56,120},{... | collective-permute-start | bytes 393224 | tf_op jit(solution)/shard_map/ppermute | solution.py:469
  83.9 1.2 collective-permute-start.12
  85.1 0.0 collective-permute-done.10.refs_3_
  85.1 2.1 %collective-permute-start.13 = (f32[128,256]{1,0:T(8,128)S(1)}, f32[128,256]{1,0:T(8,128)S(1)}, u32[]{:S(2)}, u32[]{:S(2)}) collective-permute-start(f32[128,256]{1,0:T(8,128)S(1)} %get-tuple-element.96), channel_id=1, source_target_pairs={{0,192},{8,200},{16,208},{24,216},{32,224},{40,232},{48,240},{56,2... | collective-permute-start | bytes 393224 | tf_op jit(solution)/shard_map/ppermute | solution.py:469
  87.2 4.6 %shard_map.127 = (f32[512,256]{1,0:T(8,128)}, f32[512,128]{1,0:T(8,128)}, f32[512,128]{1,0:T(8,128)}) custom-call(bf16[512,256]{1,0:T(8,128)(2,1)} %get-tuple-element.80.g_ref, bf16[512,256]{1,0:T(8,128)(2,1)} %bitcast.31, bf16[512,128]{1,0:T(8,128)(2,1)} %bitcast.36, bf16[512,128]{1,0:T(8,128)(2,1)} %bitcast.41, f32[2,128,128]{2,1,0:T(8,128)} %bitcast.45, ...), custom_call_target="tpu_custom_call" | custom-call | tf_op jit(solution)/shard_map/pallas_call | solution.py:56
  91.8 0.0 collective-permute-done.8.refs_1_
  91.8 0.0 collective-permute-done.9.refs_2_
  91.8 0.0 collective-permute-done.11.refs_5_
  91.8 0.0 collective-permute-done.12.refs_6_
  91.8 0.0 collective-permute-done.13.refs_7_
  91.8 0.7 shard_map.128
  92.6 3.4 %all-to-all-done.adj_ref = bf16[8,272,128]{2,1,0:T(8,128)(2,1)S(1)} async-done(((bf16[8,272,128]{2,1,0:T(8,128)(2,1)}), bf16[8,272,128]{2,1,0:T(8,128)(2,1)S(1)}, u32[]{:S(2)}, u32[]{:S(2)}) %all-to-all-start) | async-done | bytes 557088 | tf_op jit(solution)/shard_map/all_to_all | solution.py:426
  96.0 0.1 collective-permute-start.14
  96.1 1.1 collective-permute-done.14
  97.2 3.0 %collective-permute-start.15 = (f32[2,128]{1,0:T(2,128)S(1)}, f32[2,128]{1,0:T(2,128)S(1)}, u32[]{:S(2)}, u32[]{:S(2)}) collective-permute-start(f32[2,128]{1,0:T(2,128)S(1)} %add.32), channel_id=1, source_target_pairs={{0,32},{8,40},{16,48},{24,56},{32,0},{40,8},{48,16},{56,24},{64,96... | collective-permute-start | bytes 3080 | tf_op jit(solution)/shard_map/ppermute | solution.py:473
  100.2 0.6 collective-permute-start.16
  100.8 0.6 collective-permute-start.17
  101.4 4.2 %all-to-all-start.1 = ((f32[8,32,256]{2,1,0:T(8,128)}), f32[8,32,256]{2,1,0:T(8,128)S(1)}, u32[]{:S(2)}, u32[]{:S(2)}) async-start(f32[8,32,256]{2,1,0:T(8,128)} %shard_map.128), calls=%async_computation.1 | async-start | bytes 524288 | tf_op jit(solution)/shard_map/all_to_all | solution.py:434
  105.5 0.0 collective-permute-done.15
  105.5 0.0 collective-permute-done.16
  105.5 0.0 collective-permute-done.17
  105.6 2.1 %collective-permute-start.18 = (f32[2,128]{1,0:T(2,128)S(1)}, f32[2,128]{1,0:T(2,128)S(1)}, u32[]{:S(2)}, u32[]{:S(2)}) collective-permute-start(f32[2,128]{1,0:T(2,128)S(1)} %add_add_fusion.1), channel_id=1, source_target_pairs={{0,128},{8,136},{16,144},{24,152},{32,160},{40,168},{48,176},{56,1... | collective-permute-start | bytes 3080 | tf_op jit(solution)/shard_map/ppermute | solution.py:473
  107.6 1.5 %collective-permute-start.19 = (f32[2,128]{1,0:T(2,128)S(1)}, f32[2,128]{1,0:T(2,128)S(1)}, u32[]{:S(2)}, u32[]{:S(2)}) collective-permute-start(f32[2,128]{1,0:T(2,128)S(1)} %add_add_fusion.1), channel_id=1, source_target_pairs={{0,64},{8,72},{16,80},{24,88},{32,96},{40,104},{48,112},{56,120},{... | collective-permute-start | bytes 3080 | tf_op jit(solution)/shard_map/ppermute | solution.py:473
  109.1 0.6 collective-permute-start.20
  109.7 2.7 %shard_map.129 = (bf16[512,256]{1,0:T(8,128)(2,1)}, f32[512,128]{1,0:T(8,128)}) custom-call(s32[4]{0:T(128)} %copy-done.1, f32[512,256]{1,0:T(8,128)} %get-tuple-element.83.gi_ref, f32[512,128]{1,0:T(8,128)} %get-tuple-element.84.ginj_ref, bf16[512,256]{1,0:T(8,128)(2,1)} %bitcast.32, bf16[512,128]{1,0:T(8,128)(2,1)} %bitcast.37, ...), custom_call_target="tpu_custom_call" | custom-call | tf_op jit(solution)/shard_map/pallas_call | solution.py:56
  112.4 0.0 collective-permute-done.18
  112.4 0.3 collective-permute-done.20
  112.7 0.6 multiply_reduce_fusion
  113.3 3.9 %all-to-all-done.1 = f32[8,32,256]{2,1,0:T(8,128)S(1)} async-done(((f32[8,32,256]{2,1,0:T(8,128)}), f32[8,32,256]{2,1,0:T(8,128)S(1)}, u32[]{:S(2)}, u32[]{:S(2)}) %all-to-all-start.1) | async-done | bytes 262176 | tf_op jit(solution)/shard_map/all_to_all | solution.py:434
  117.2 0.6 reduce_sum.21
  (13 shorter events, 0.1 us)
Async XLA Ops:
  7.2 51.6 %all-gather.3.cloned.1.call-start = ((), (), s32[]{:S(2)}) async-start(), calls=%async_computation.2 | async-start | bytes 3612672 | tf_op jit(solution)/shard_map/all_gather | solution.py:371
  19.6 4.4 %collective-permute-start = (bf16[16,256,256]{2,1,0:T(8,128)(2,1)}, bf16[16,256,256]{2,1,0:T(8,128)(2,1)S(1)}, u32[]{:S(2)}, u32[]{:S(2)}) collective-permute-start(bf16[16,256,256]{2,1,0:T(8,128)(2,1)} %get-tuple-element.57), channel_id=1, source_target_pairs={{0,8},{8,0},{16,24},{24,16},{32,40},{40,32},{48,56},{56,48},{64,72... | collective-permute-start | bytes 6291464 | tf_op jit(solution)/shard_map/ppermute | solution.py:350
  19.7 28.4 %copy-start.1 = (s32[4]{0:T(128)}, s32[4]{0:T(128)S(1)}, u32[]{:S(2)}) copy-start(s32[4]{0:T(128)S(1)} %pad_add_fusion.place_ref) | copy-start | bytes 52
  24.0 1.7 %copy-start = (bf16[16,256,256]{2,1,0:T(8,128)(2,1)S(1)}, bf16[16,256,256]{2,1,0:T(8,128)(2,1)}, u32[]{:S(2)}) copy-start(bf16[16,256,256]{2,1,0:T(8,128)(2,1)} %get-tuple-element.56) | copy-start | bytes 6291460
  27.7 9.4 %collective-permute-start.1 = (bf16[4,128,256]{2,1,0:T(8,128)(2,1)S(1)}, bf16[4,128,256]{2,1,0:T(8,128)(2,1)S(1)}, u32[]{:S(2)}, u32[]{:S(2)}) collective-permute-start(bf16[4,128,256]{2,1,0:T(8,128)(2,1)S(1)} %get-tuple-element.59), channel_id=1, source_target_pairs={{0,64},{8,72},{16,80},{24,88},{32,96},{40,104},{48,112},{56,120},{... | collective-permute-start | bytes 786440 | tf_op jit(solution)/shard_map/ppermute | solution.py:469
  29.3 14.4 %collective-permute-start.2 = (bf16[4,128,256]{2,1,0:T(8,128)(2,1)S(1)}, bf16[4,128,256]{2,1,0:T(8,128)(2,1)S(1)}, u32[]{:S(2)}, u32[]{:S(2)}) collective-permute-start(bf16[4,128,256]{2,1,0:T(8,128)(2,1)S(1)} %get-tuple-element.60), channel_id=1, source_target_pairs={{0,128},{8,136},{16,144},{24,152},{32,160},{40,168},{48,176},{56,1... | collective-permute-start | bytes 786440 | tf_op jit(solution)/shard_map/ppermute | solution.py:469
  32.1 12.4 %collective-permute-start.3 = (bf16[4,128,256]{2,1,0:T(8,128)(2,1)S(1)}, bf16[4,128,256]{2,1,0:T(8,128)(2,1)S(1)}, u32[]{:S(2)}, u32[]{:S(2)}) collective-permute-start(bf16[4,128,256]{2,1,0:T(8,128)(2,1)S(1)} %get-tuple-element.61), channel_id=1, source_target_pairs={{0,192},{8,200},{16,208},{24,216},{32,224},{40,232},{48,240},{56,2... | collective-permute-start | bytes 786440 | tf_op jit(solution)/shard_map/ppermute | solution.py:469
  32.5 11.9 %collective-permute-start.4 = (bf16[4,128,256]{2,1,0:T(8,128)(2,1)S(1)}, bf16[4,128,256]{2,1,0:T(8,128)(2,1)S(1)}, u32[]{:S(2)}, u32[]{:S(2)}) collective-permute-start(bf16[4,128,256]{2,1,0:T(8,128)(2,1)S(1)} %get-tuple-element.63), channel_id=1, source_target_pairs={{0,16},{8,24},{16,32},{24,40},{32,48},{40,56},{48,0},{56,8},{64,80... | collective-permute-start | bytes 786440 | tf_op jit(solution)/shard_map/ppermute | solution.py:469
  34.1 14.0 %collective-permute-start.5 = (bf16[4,128,256]{2,1,0:T(8,128)(2,1)S(1)}, bf16[4,128,256]{2,1,0:T(8,128)(2,1)S(1)}, u32[]{:S(2)}, u32[]{:S(2)}) collective-permute-start(bf16[4,128,256]{2,1,0:T(8,128)(2,1)S(1)} %get-tuple-element.64), channel_id=1, source_target_pairs={{0,32},{8,40},{16,48},{24,56},{32,0},{40,8},{48,16},{56,24},{64,96... | collective-permute-start | bytes 786440 | tf_op jit(solution)/shard_map/ppermute | solution.py:469
  37.1 11.0 %collective-permute-start.6 = (bf16[4,128,256]{2,1,0:T(8,128)(2,1)S(1)}, bf16[4,128,256]{2,1,0:T(8,128)(2,1)S(1)}, u32[]{:S(2)}, u32[]{:S(2)}) collective-permute-start(bf16[4,128,256]{2,1,0:T(8,128)(2,1)S(1)} %get-tuple-element.65), channel_id=1, source_target_pairs={{0,48},{8,56},{16,0},{24,8},{32,16},{40,24},{48,32},{56,40},{64,11... | collective-permute-start | bytes 786440 | tf_op jit(solution)/shard_map/ppermute | solution.py:469
  60.5 4.6 %copy-start.2 = (bf16[8,256,512]{2,1,0:T(8,128)(2,1)}, bf16[8,256,512]{2,1,0:T(8,128)(2,1)S(1)}, u32[]{:S(2)}) copy-start(bf16[8,256,512]{2,1,0:T(8,128)(2,1)S(1)} %slice.9.mine_ref) | copy-start | bytes 6291460
  60.5 4.6 %collective-permute-start.7 = (bf16[8,256,512]{2,1,0:T(8,128)(2,1)S(1)}, bf16[8,256,512]{2,1,0:T(8,128)(2,1)}, u32[]{:S(2)}, u32[]{:S(2)}) collective-permute-start(bf16[8,256,512]{2,1,0:T(8,128)(2,1)S(1)} %slice.9.mine_ref), channel_id=1, source_target_pairs={{0,8},{8,0},{16,24},{24,16},{32,40},{40,32},{48,56},{56,48},{64,72... | collective-permute-start | bytes 6291464 | tf_op jit(solution)/shard_map/ppermute | solution.py:350
  73.1 22.8 %all-to-all-start = ((bf16[8,272,128]{2,1,0:T(8,128)(2,1)}), bf16[8,272,128]{2,1,0:T(8,128)(2,1)S(1)}, u32[]{:S(2)}, u32[]{:S(2)}) async-start(bf16[8,272,128]{2,1,0:T(8,128)(2,1)} %get-tuple-element.85), calls=%async_computation | async-start | bytes 1114112 | tf_op jit(solution)/shard_map/all_to_all | solution.py:426
  77.4 7.7 %collective-permute-start.10 = (f32[128,256]{1,0:T(8,128)S(1)}, f32[128,256]{1,0:T(8,128)S(1)}, u32[]{:S(2)}, u32[]{:S(2)}) collective-permute-start(f32[128,256]{1,0:T(8,128)S(1)} %get-tuple-element.89), channel_id=1, source_target_pairs={{0,48},{8,56},{16,0},{24,8},{32,16},{40,24},{48,32},{56,40},{64,11... | collective-permute-start | bytes 393224 | tf_op jit(solution)/shard_map/ppermute | solution.py:469
  80.2 11.6 %collective-permute-start.8 = (f32[128,256]{1,0:T(8,128)S(1)}, f32[128,256]{1,0:T(8,128)S(1)}, u32[]{:S(2)}, u32[]{:S(2)}) collective-permute-start(f32[128,256]{1,0:T(8,128)S(1)} %get-tuple-element.87), channel_id=1, source_target_pairs={{0,16},{8,24},{16,32},{24,40},{32,48},{40,56},{48,0},{56,8},{64,80... | collective-permute-start | bytes 393224 | tf_op jit(solution)/shard_map/ppermute | solution.py:469
  80.2 11.6 %collective-permute-start.9 = (f32[128,256]{1,0:T(8,128)S(1)}, f32[128,256]{1,0:T(8,128)S(1)}, u32[]{:S(2)}, u32[]{:S(2)}) collective-permute-start(f32[128,256]{1,0:T(8,128)S(1)} %get-tuple-element.88), channel_id=1, source_target_pairs={{0,32},{8,40},{16,48},{24,56},{32,0},{40,8},{48,16},{56,24},{64,96... | collective-permute-start | bytes 393224 | tf_op jit(solution)/shard_map/ppermute | solution.py:469
  82.5 9.3 %collective-permute-start.11 = (f32[128,256]{1,0:T(8,128)S(1)}, f32[128,256]{1,0:T(8,128)S(1)}, u32[]{:S(2)}, u32[]{:S(2)}) collective-permute-start(f32[128,256]{1,0:T(8,128)S(1)} %get-tuple-element.94), channel_id=1, source_target_pairs={{0,64},{8,72},{16,80},{24,88},{32,96},{40,104},{48,112},{56,120},{... | collective-permute-start | bytes 393224 | tf_op jit(solution)/shard_map/ppermute | solution.py:469
  83.9 7.9 %collective-permute-start.12 = (f32[128,256]{1,0:T(8,128)S(1)}, f32[128,256]{1,0:T(8,128)S(1)}, u32[]{:S(2)}, u32[]{:S(2)}) collective-permute-start(f32[128,256]{1,0:T(8,128)S(1)} %get-tuple-element.95), channel_id=1, source_target_pairs={{0,128},{8,136},{16,144},{24,152},{32,160},{40,168},{48,176},{56,1... | collective-permute-start | bytes 393224 | tf_op jit(solution)/shard_map/ppermute | solution.py:469
  85.1 6.7 %collective-permute-start.13 = (f32[128,256]{1,0:T(8,128)S(1)}, f32[128,256]{1,0:T(8,128)S(1)}, u32[]{:S(2)}, u32[]{:S(2)}) collective-permute-start(f32[128,256]{1,0:T(8,128)S(1)} %get-tuple-element.96), channel_id=1, source_target_pairs={{0,192},{8,200},{16,208},{24,216},{32,224},{40,232},{48,240},{56,2... | collective-permute-start | bytes 393224 | tf_op jit(solution)/shard_map/ppermute | solution.py:469
  95.9 13.8 %copy-start.3 = (bf16[8,272,128]{2,1,0:T(8,128)(2,1)}, bf16[8,272,128]{2,1,0:T(8,128)(2,1)S(1)}, u32[]{:S(2)}) copy-start(bf16[8,272,128]{2,1,0:T(8,128)(2,1)S(1)} %all-to-all-done.adj_ref) | copy-start | bytes 1671172
  96.0 1.2 collective-permute-start.14
  97.2 8.3 %collective-permute-start.15 = (f32[2,128]{1,0:T(2,128)S(1)}, f32[2,128]{1,0:T(2,128)S(1)}, u32[]{:S(2)}, u32[]{:S(2)}) collective-permute-start(f32[2,128]{1,0:T(2,128)S(1)} %add.32), channel_id=1, source_target_pairs={{0,32},{8,40},{16,48},{24,56},{32,0},{40,8},{48,16},{56,24},{64,96... | collective-permute-start | bytes 3080 | tf_op jit(solution)/shard_map/ppermute | solution.py:473
  100.2 5.3 %collective-permute-start.16 = (f32[2,128]{1,0:T(2,128)S(1)}, f32[2,128]{1,0:T(2,128)S(1)}, u32[]{:S(2)}, u32[]{:S(2)}) collective-permute-start(f32[2,128]{1,0:T(2,128)S(1)} %add.32), channel_id=1, source_target_pairs={{0,16},{8,24},{16,0},{24,8},{32,48},{40,56},{48,32},{56,40},{64,80... | collective-permute-start | bytes 3080 | tf_op jit(solution)/shard_map/ppermute | solution.py:473
  100.8 4.8 %collective-permute-start.17 = (f32[2,128]{1,0:T(2,128)S(1)}, f32[2,128]{1,0:T(2,128)S(1)}, u32[]{:S(2)}, u32[]{:S(2)}) collective-permute-start(f32[2,128]{1,0:T(2,128)S(1)} %add.32), channel_id=1, source_target_pairs={{0,48},{8,56},{16,32},{24,40},{32,16},{40,24},{48,0},{56,8},{64,11... | collective-permute-start | bytes 3080 | tf_op jit(solution)/shard_map/ppermute | solution.py:473
  101.4 15.8 %all-to-all-start.1 = ((f32[8,32,256]{2,1,0:T(8,128)}), f32[8,32,256]{2,1,0:T(8,128)S(1)}, u32[]{:S(2)}, u32[]{:S(2)}) async-start(f32[8,32,256]{2,1,0:T(8,128)} %shard_map.128), calls=%async_computation.1 | async-start | bytes 524288 | tf_op jit(solution)/shard_map/all_to_all | solution.py:434
  105.6 6.8 %collective-permute-start.18 = (f32[2,128]{1,0:T(2,128)S(1)}, f32[2,128]{1,0:T(2,128)S(1)}, u32[]{:S(2)}, u32[]{:S(2)}) collective-permute-start(f32[2,128]{1,0:T(2,128)S(1)} %add_add_fusion.1), channel_id=1, source_target_pairs={{0,128},{8,136},{16,144},{24,152},{32,160},{40,168},{48,176},{56,1... | collective-permute-start | bytes 3080 | tf_op jit(solution)/shard_map/ppermute | solution.py:473
  107.6 4.7 %collective-permute-start.19 = (f32[2,128]{1,0:T(2,128)S(1)}, f32[2,128]{1,0:T(2,128)S(1)}, u32[]{:S(2)}, u32[]{:S(2)}) collective-permute-start(f32[2,128]{1,0:T(2,128)S(1)} %add_add_fusion.1), channel_id=1, source_target_pairs={{0,64},{8,72},{16,80},{24,88},{32,96},{40,104},{48,112},{56,120},{... | collective-permute-start | bytes 3080 | tf_op jit(solution)/shard_map/ppermute | solution.py:473
  109.1 3.6 %collective-permute-start.20 = (f32[2,128]{1,0:T(2,128)S(1)}, f32[2,128]{1,0:T(2,128)S(1)}, u32[]{:S(2)}, u32[]{:S(2)}) collective-permute-start(f32[2,128]{1,0:T(2,128)S(1)} %add_add_fusion.1), channel_id=1, source_target_pairs={{0,192},{8,200},{16,208},{24,216},{32,224},{40,232},{48,240},{56,2... | collective-permute-start | bytes 3080 | tf_op jit(solution)/shard_map/ppermute | solution.py:473
Sparse Core Ops, SparseCore 0:
  10.2 48.5 all-gather.2

commit v5 on v4

--- a/solution.py
+++ b/solution.py
@@ -436,7 +436,7 @@
     rate = plane_total(rate)
     grad_input, grad_inject = call(
         finish_kernel, [shape((T, HP), BF16), shape((T, N))],
-        (place, gi, ginj, x, inject, aux, pay, decay), smem=(0,),
+        (place, gi, ginj, x, inject, aux, pay, decay), smem=(0,), limit=16 << 20,
     )
     grad_weight = jnp.sum(blocks, axis=0)
     tokens = T * lax.axis_size("dp") * lax.axis_size("ctx")

time: 126 us -> 126 us (level)
    unnamed x8 -> x20, local copies, waits for them, and re-layouts: 1.67 us -> 2.64 us
where the time goes in v5:
time: 126 us; the launch traced here: 125 us
  starting transfers between devices  39 us (31%)
  Pallas kernels  38.9 us (31%)
  waiting for transfers between devices  26.8 us (21%)
  between operations  14.2 us (11%)
  local copies, waits for them, and re-layouts  4.37 us (3%)
  other arithmetic  1.38 us (1%)
    pallas_call x8, Pallas kernels, call(): pl.pallas_call(kernel, grid=(1,), out_shape=outs, in_specs=[spec(i, arg)...  22 us
    ppermute x12, starting transfers between devices, exchanged(): lax.ppermute(parts[d], 'dp', pairs(d))  21.7 us
    pallas_call x2, Pallas kernels, gridded(): pl.pallas_call(kernel, out_shape=outs, grid_spec=pltpu.PrefetchScalarGrid...  10.7 us
    all_gather x1, waiting for transfers between devices, local(): gathered = lax.all_gather(pay, 'ctx', axis=0)  9.34 us
    ppermute x7, starting transfers between devices, flipped(): return lax.ppermute(value, 'dp', [(i, i ^ bits) for i in range(2 * PLANE)])  8.44 us
    pallas_call x1, Pallas kernels, local(): pl.pallas_call(weight_kernel, grid=(WEIGHT_STEPS,), out_shape=[half_terms...  6.2 us
    ppermute x12, waiting for transfers between devices, exchanged(): lax.ppermute(parts[d], 'dp', pairs(d))  4.57 us
    ppermute x2, waiting for transfers between devices, swap_cores(): return lax.ppermute(value, 'dp', [(i, i ^ 1) for i in range(2 * PLANE)])  4.34 us
  transfers between devices with their start and end apart: 24, of which 10 were waited for; matrix products, arithmetic and copies ran while one was open for 1% of the time, Pallas kernels for 23%

profile of v5, /device:TPU:2, one launch (start us, length us, event | category | flops | bytes accessed | tf_op | source)
XLA Modules:
  0.0 124.7 jit_solution(7111107328032658525)
XLA Ops:
  7.2 0.0 all-gather.3.cloned.1.call-start
  7.2 2.8 %shard_map.119 = (bf16[392,512]{1,0:T(8,128)(2,1)}, f32[2,136,128]{2,1,0:T(8,128)}) custom-call(f32[2]{0:T(128)} %rate_ref.5, bf16[256,1024]{1,0:T(8,128)(2,1)} %weight_ref.1, bf16[512,256]{1,0:T(8,128)(2,1)} %bitcast.24, bf16[512,128]{1,0:T(8,128)(2,1)} %bitcast.29, s32[2,512]{1,0:T(2,128)} %bitcast.46, f32[2,128,128]{2,1,0:T(8,128)} %bitcast.42), custom_call_target="tpu_custom_call" | custom-call | tf_op jit(solution)/shard_map/pallas_call | solution.py:56
  10.1 0.0 all-gather.3.cloned.1.call-update
  10.1 3.3 %shard_map.120 = (bf16[256,512]{1,0:T(8,128)(2,1)}, bf16[2,512,512]{2,1,0:T(8,128)(2,1)}) custom-call(f32[2]{0:T(128)} %rate_ref.5, bf16[512,256]{1,0:T(8,128)(2,1)} %bitcast.25, bf16[512,128]{1,0:T(8,128)(2,1)} %bitcast.30, bf16[512,128]{1,0:T(8,128)(2,1)} %bitcast.38, s32[2,512]{1,0:T(2,128)} %bitcast.47, f32[2,128,128]{2,1,0:T(8,128)} %bitcast.43), custom_call_target="tpu_custom_call" | custom-call | tf_op jit(solution)/shard_map/pallas_call | solution.py:56
  13.4 6.2 %shard_map.121 = (bf16[16,256,256]{2,1,0:T(8,128)(2,1)}, bf16[16,256,256]{2,1,0:T(8,128)(2,1)}) custom-call(bf16[256,512]{1,0:T(8,128)(2,1)} %get-tuple-element.55.out_t_ref, bf16[512,8192]{1,0:T(8,128)(2,1)} %bitcast.34), custom_call_target="tpu_custom_call" | custom-call | tf_op jit(solution)/shard_map/pallas_call | solution.py:380
  19.6 0.0 collective-permute-start
  19.6 0.1 pad_add_fusion.place_ref
  19.7 4.3 %collective-permute-done = bf16[16,256,256]{2,1,0:T(8,128)(2,1)S(1)} collective-permute-done((bf16[16,256,256]{2,1,0:T(8,128)(2,1)}, bf16[16,256,256]{2,1,0:T(8,128)(2,1)S(1)}, u32[]{:S(2)}, u32[]{:S(2)}) %collective-permute-start) | collective-permute-done | bytes 2097184 | tf_op jit(solution)/shard_map/ppermute | solution.py:350
  24.0 1.7 %copy-done = bf16[16,256,256]{2,1,0:T(8,128)(2,1)S(1)} copy-done((bf16[16,256,256]{2,1,0:T(8,128)(2,1)S(1)}, bf16[16,256,256]{2,1,0:T(8,128)(2,1)}, u32[]{:S(2)}) %copy-start) | copy-done | bytes 2097176
  25.6 2.7 %shard_map.122 = (bf16[4,128,256]{2,1,0:T(8,128)(2,1)S(1)}, bf16[4,128,256]{2,1,0:T(8,128)(2,1)S(1)}, bf16[4,128,256]{2,1,0:T(8,128)(2,1)}, bf16[4,128,256]{2,1,...) custom-call(s32[4]{0:T(128)S(1)} %pad_add_fusion.place_ref, ...), custom_call_target="tpu_custom_call" | custom-call | tf_op jit(solution)/shard_map/pallas_call | solution.py:190
  28.4 1.5 %collective-permute-start.1 = (bf16[4,128,256]{2,1,0:T(8,128)(2,1)S(1)}, bf16[4,128,256]{2,1,0:T(8,128)(2,1)S(1)}, u32[]{:S(2)}, u32[]{:S(2)}) collective-permute-start(bf16[4,128,256]{2,1,0:T(8,128)(2,1)S(1)} %get-tuple-element.59), channel_id=1, source_target_pairs={{0,64},{8,72},{16,80},{24,88},{32,96},{40,104},{48,112},{56,120},{... | collective-permute-start | bytes 786440 | tf_op jit(solution)/shard_map/ppermute | solution.py:469
  29.9 2.8 %collective-permute-start.2 = (bf16[4,128,256]{2,1,0:T(8,128)(2,1)}, bf16[4,128,256]{2,1,0:T(8,128)(2,1)S(1)}, u32[]{:S(2)}, u32[]{:S(2)}) collective-permute-start(bf16[4,128,256]{2,1,0:T(8,128)(2,1)} %get-tuple-element.60), channel_id=1, source_target_pairs={{0,128},{8,136},{16,144},{24,152},{32,160},{40,168},{48,176},{56,1... | collective-permute-start | bytes 786440 | tf_op jit(solution)/shard_map/ppermute | solution.py:469
  32.6 0.5 collective-permute-start.3
  33.1 1.6 %collective-permute-start.4 = (bf16[4,128,256]{2,1,0:T(8,128)(2,1)S(1)}, bf16[4,128,256]{2,1,0:T(8,128)(2,1)S(1)}, u32[]{:S(2)}, u32[]{:S(2)}) collective-permute-start(bf16[4,128,256]{2,1,0:T(8,128)(2,1)S(1)} %get-tuple-element.63), channel_id=1, source_target_pairs={{0,16},{8,24},{16,32},{24,40},{32,48},{40,56},{48,0},{56,8},{64,80... | collective-permute-start | bytes 786440 | tf_op jit(solution)/shard_map/ppermute | solution.py:469
  34.7 2.9 %collective-permute-start.5 = (bf16[4,128,256]{2,1,0:T(8,128)(2,1)S(1)}, bf16[4,128,256]{2,1,0:T(8,128)(2,1)S(1)}, u32[]{:S(2)}, u32[]{:S(2)}) collective-permute-start(bf16[4,128,256]{2,1,0:T(8,128)(2,1)S(1)} %get-tuple-element.64), channel_id=1, source_target_pairs={{0,32},{8,40},{16,48},{24,56},{32,0},{40,8},{48,16},{56,24},{64,96... | collective-permute-start | bytes 786440 | tf_op jit(solution)/shard_map/ppermute | solution.py:469
  37.5 0.1 collective-permute-done.1.refs_1_
  37.7 2.8 %collective-permute-start.6 = (bf16[4,128,256]{2,1,0:T(8,128)(2,1)S(1)}, bf16[4,128,256]{2,1,0:T(8,128)(2,1)S(1)}, u32[]{:S(2)}, u32[]{:S(2)}) collective-permute-start(bf16[4,128,256]{2,1,0:T(8,128)(2,1)S(1)} %get-tuple-element.65), channel_id=1, source_target_pairs={{0,48},{8,56},{16,0},{24,8},{32,16},{40,24},{48,32},{56,40},{64,11... | collective-permute-start | bytes 786440 | tf_op jit(solution)/shard_map/ppermute | solution.py:469
  40.5 3.7 %shard_map.124 = (bf16[2,512,512]{2,1,0:T(8,128)(2,1)}, f32[512,256]{1,0:T(8,128)}, bf16[2,512,128]{2,1,0:T(8,128)(2,1)}, f32[512,128]{1,0:T(8,128)}) custom-call(f32[2]{0:T(128)} %rate_ref.5, bf16[512,256]{1,0:T(8,128)(2,1)} %bitcast.26, bf16[512,128]{1,0:T(8,128)(2,1)} %bitcast.31, bf16[512,128]{1,0:T(8,128)(2,1)} %bitcast.39, s32[2,512]{1,0:T(2,128)} %bitcast.48, ...), custom_call_target="tpu_custom_call" | custom-call | tf_op jit(solution)/shard_map/pallas_call | solution.py:56
  44.2 0.0 collective-permute-done.2.refs_2_
  44.2 1.1 collective-permute-done.3.refs_3_
  45.3 0.0 collective-permute-done.4.refs_5_
  45.3 3.4 %collective-permute-done.5.refs_6_ = bf16[4,128,256]{2,1,0:T(8,128)(2,1)S(1)} collective-permute-done((bf16[4,128,256]{2,1,0:T(8,128)(2,1)S(1)}, bf16[4,128,256]{2,1,0:T(8,128)(2,1)S(1)}, u32[]{:S(2)}, u32[]{:S(2)}) %collective-permute-start.5) | collective-permute-done | bytes 262176 | tf_op jit(solution)/shard_map/ppermute | solution.py:469
  48.6 0.0 collective-permute-done.6.refs_7_
  48.6 0.8 shard_map.123
  49.4 9.3 %all-gather.3.cloned.1.call-done = bf16[3136,512]{1,0:T(8,128)(2,1)} async-done(((bf16[392,512]{1,0:T(8,128)(2,1)}), bf16[3136,512]{1,0:T(8,128)(2,1)}) %all-gather.3.cloned.1.call-update) | async-done | bytes 3211280 | tf_op jit(solution)/shard_map/all_gather | solution.py:371
  58.8 1.7 %slice.9.mine_ref = bf16[8,256,512]{2,1,0:T(8,128)(2,1)S(1)} slice(bf16[8,392,512]{2,1,0:T(8,128)(2,1)} %bitcast.36), slice={[0:8], [0:256], [0:512]} | slice | bytes 4194304 | tf_op jit(solution)/shard_map/slice | solution.py:405
  60.5 0.3 collective-permute-start.7
  60.8 4.2 %shard_map.125 = (f32[512,256]{1,0:T(8,128)}, f32[8,16,128]{2,1,0:T(8,128)}) custom-call(s32[4]{0:T(128)} %copy-done.7, f32[512,256]{1,0:T(8,128)} %get-tuple-element.78.part_ref, bf16[512,128]{1,0:T(8,128)(2,1)} %bitcast.40, f32[512,128]{1,0:T(8,128)} %get-tuple-element.75.aux_ref, bf16[8,392,512]{2,1,0:T(8,128)(2,1)} %bitcast.37), custom_call_target="tpu_custom_call" | custom-call | tf_op jit(solution)/shard_map/pallas_call | solution.py:56
  65.0 0.1 collective-permute-done.7.other_ref
  65.1 8.0 %shard_map.126 = (bf16[512,256]{1,0:T(8,128)(2,1)}, bf16[8,272,128]{2,1,0:T(8,128)(2,1)}) custom-call(s32[4]{0:T(128)} %copy-done.7, bf16[512,8192]{1,0:T(8,128)(2,1)} %bitcast.35, bf16[8,256,512]{2,1,0:T(8,128)(2,1)} %copy-done.9, bf16[8,256,512]{2,1,0:T(8,128)(2,1)} %collective-permute-done.7.other_ref, bf16[2,512,128]{2,1,0:T(8,128)(2,1)} %get-tuple-element.77.fr_ref, ...), custom_call_target="tpu_custom_call" | custom-call | tf_op jit(solution)/shard_map/pallas_call | solution.py:190
  73.1 4.3 %all-to-all-start = ((bf16[8,272,128]{2,1,0:T(8,128)(2,1)}), bf16[8,272,128]{2,1,0:T(8,128)(2,1)S(1)}, u32[]{:S(2)}, u32[]{:S(2)}) async-start(bf16[8,272,128]{2,1,0:T(8,128)(2,1)} %get-tuple-element.85), calls=%async_computation | async-start | bytes 1114112 | tf_op jit(solution)/shard_map/all_to_all | solution.py:426
  77.4 2.7 %collective-permute-start.10 = (f32[128,256]{1,0:T(8,128)S(1)}, f32[128,256]{1,0:T(8,128)S(1)}, u32[]{:S(2)}, u32[]{:S(2)}) collective-permute-start(f32[128,256]{1,0:T(8,128)S(1)} %get-tuple-element.89), channel_id=1, source_target_pairs={{0,48},{8,56},{16,0},{24,8},{32,16},{40,24},{48,32},{56,40},{64,11... | collective-permute-start | bytes 393224 | tf_op jit(solution)/shard_map/ppermute | solution.py:469
  80.2 0.0 collective-permute-start.8
  80.2 2.3 %collective-permute-start.9 = (f32[128,256]{1,0:T(8,128)S(1)}, f32[128,256]{1,0:T(8,128)S(1)}, u32[]{:S(2)}, u32[]{:S(2)}) collective-permute-start(f32[128,256]{1,0:T(8,128)S(1)} %get-tuple-element.88), channel_id=1, source_target_pairs={{0,32},{8,40},{16,48},{24,56},{32,0},{40,8},{48,16},{56,24},{64,96... | collective-permute-start | bytes 393224 | tf_op jit(solution)/shard_map/ppermute | solution.py:469
  82.5 1.5 %collective-permute-start.11 = (f32[128,256]{1,0:T(8,128)S(1)}, f32[128,256]{1,0:T(8,128)S(1)}, u32[]{:S(2)}, u32[]{:S(2)}) collective-permute-start(f32[128,256]{1,0:T(8,128)S(1)} %get-tuple-element.94), channel_id=1, source_target_pairs={{0,64},{8,72},{16,80},{24,88},{32,96},{40,104},{48,112},{56,120},{... | collective-permute-start | bytes 393224 | tf_op jit(solution)/shard_map/ppermute | solution.py:469
  83.9 1.2 collective-permute-start.12
  85.1 0.0 collective-permute-done.10.refs_3_
  85.1 2.1 %collective-permute-start.13 = (f32[128,256]{1,0:T(8,128)S(1)}, f32[128,256]{1,0:T(8,128)S(1)}, u32[]{:S(2)}, u32[]{:S(2)}) collective-permute-start(f32[128,256]{1,0:T(8,128)S(1)} %get-tuple-element.96), channel_id=1, source_target_pairs={{0,192},{8,200},{16,208},{24,216},{32,224},{40,232},{48,240},{56,2... | collective-permute-start | bytes 393224 | tf_op jit(solution)/shard_map/ppermute | solution.py:469
  87.2 0.0 copy-start.8
  87.2 4.6 %shard_map.127 = (f32[512,256]{1,0:T(8,128)}, f32[512,128]{1,0:T(8,128)}, f32[512,128]{1,0:T(8,128)}) custom-call(bf16[512,256]{1,0:T(8,128)(2,1)} %get-tuple-element.80.g_ref, bf16[512,256]{1,0:T(8,128)(2,1)} %bitcast.27, bf16[512,128]{1,0:T(8,128)(2,1)} %bitcast.32, bf16[512,128]{1,0:T(8,128)(2,1)} %bitcast.41, f32[2,128,128]{2,1,0:T(8,128)} %bitcast.45, ...), custom_call_target="tpu_custom_call" | custom-call | tf_op jit(solution)/shard_map/pallas_call | solution.py:56
  91.9 0.0 collective-permute-done.8.refs_1_
  91.9 0.0 collective-permute-done.9.refs_2_
  91.9 0.0 collective-permute-done.11.refs_5_
  91.9 0.7 shard_map.128
  92.6 3.3 %all-to-all-done.adj_ref = bf16[8,272,128]{2,1,0:T(8,128)(2,1)S(1)} async-done(((bf16[8,272,128]{2,1,0:T(8,128)(2,1)}), bf16[8,272,128]{2,1,0:T(8,128)(2,1)S(1)}, u32[]{:S(2)}, u32[]{:S(2)}) %all-to-all-start) | async-done | bytes 557088 | tf_op jit(solution)/shard_map/all_to_all | solution.py:426
  96.0 0.1 collective-permute-start.14
  96.1 1.1 collective-permute-done.14
  97.2 3.0 %collective-permute-start.15 = (f32[2,128]{1,0:T(2,128)S(1)}, f32[2,128]{1,0:T(2,128)S(1)}, u32[]{:S(2)}, u32[]{:S(2)}) collective-permute-start(f32[2,128]{1,0:T(2,128)S(1)} %add.32), channel_id=1, source_target_pairs={{0,32},{8,40},{16,48},{24,56},{32,0},{40,8},{48,16},{56,24},{64,96... | collective-permute-start | bytes 3080 | tf_op jit(solution)/shard_map/ppermute | solution.py:473
  100.2 0.6 collective-permute-start.16
  100.8 0.6 collective-permute-start.17
  101.4 4.2 %all-to-all-start.1 = ((f32[8,32,256]{2,1,0:T(8,128)}), f32[8,32,256]{2,1,0:T(8,128)S(1)}, u32[]{:S(2)}, u32[]{:S(2)}) async-start(f32[8,32,256]{2,1,0:T(8,128)} %shard_map.128), calls=%async_computation.1 | async-start | bytes 524288 | tf_op jit(solution)/shard_map/all_to_all | solution.py:434
  105.6 0.0 collective-permute-done.15
  105.6 0.0 collective-permute-done.17
  105.6 2.0 %collective-permute-start.18 = (f32[2,128]{1,0:T(2,128)S(1)}, f32[2,128]{1,0:T(2,128)S(1)}, u32[]{:S(2)}, u32[]{:S(2)}) collective-permute-start(f32[2,128]{1,0:T(2,128)S(1)} %add_add_fusion.1), channel_id=1, source_target_pairs={{0,128},{8,136},{16,144},{24,152},{32,160},{40,168},{48,176},{56,1... | collective-permute-start | bytes 3080 | tf_op jit(solution)/shard_map/ppermute | solution.py:473
  107.7 1.5 %collective-permute-start.19 = (f32[2,128]{1,0:T(2,128)S(1)}, f32[2,128]{1,0:T(2,128)S(1)}, u32[]{:S(2)}, u32[]{:S(2)}) collective-permute-start(f32[2,128]{1,0:T(2,128)S(1)} %add_add_fusion.1), channel_id=1, source_target_pairs={{0,64},{8,72},{16,80},{24,88},{32,96},{40,104},{48,112},{56,120},{... | collective-permute-start | bytes 3080 | tf_op jit(solution)/shard_map/ppermute | solution.py:473
  109.1 0.7 collective-permute-start.20
  109.8 0.0 copy-start.5
  109.9 0.9 copy-done.5
  110.8 1.7 %shard_map.129 = (bf16[512,256]{1,0:T(8,128)(2,1)}, f32[512,128]{1,0:T(8,128)}) custom-call(s32[4]{0:T(128)S(1)} %copy-done.8, f32[512,256]{1,0:T(8,128)S(1)} %copy-done.4, f32[512,128]{1,0:T(8,128)S(1)} %copy-done.5, bf16[512,256]{1,0:T(8,128)(2,1)S(1)} %bitcast.28, bf16[512,128]{1,0:T(8,128)(2,1)S(1)} %bitcast.33, f32[512,128]{1,0:T(8,128)S(1)} %copy-done.3, ...), custom_call_target="tpu_custom_call" | custom-call | tf_op jit(solution)/shard_map/pallas_call | solution.py:56
  112.5 0.0 collective-permute-done.19
  112.5 0.2 collective-permute-done.20
  112.7 0.6 multiply_reduce_fusion
  113.3 3.9 %all-to-all-done.1 = f32[8,32,256]{2,1,0:T(8,128)S(1)} async-done(((f32[8,32,256]{2,1,0:T(8,128)}), f32[8,32,256]{2,1,0:T(8,128)S(1)}, u32[]{:S(2)}, u32[]{:S(2)}) %all-to-all-start.1) | async-done | bytes 262176 | tf_op jit(solution)/shard_map/all_to_all | solution.py:434
  117.3 0.6 reduce_sum.21
  (25 shorter events, 0.1 us)
Async XLA Ops:
  7.2 51.6 %all-gather.3.cloned.1.call-start = ((), (), s32[]{:S(2)}) async-start(), calls=%async_computation.2 | async-start | bytes 3612672 | tf_op jit(solution)/shard_map/all_gather | solution.py:371
  19.6 4.4 %collective-permute-start = (bf16[16,256,256]{2,1,0:T(8,128)(2,1)}, bf16[16,256,256]{2,1,0:T(8,128)(2,1)S(1)}, u32[]{:S(2)}, u32[]{:S(2)}) collective-permute-start(bf16[16,256,256]{2,1,0:T(8,128)(2,1)} %get-tuple-element.57), channel_id=1, source_target_pairs={{0,8},{8,0},{16,24},{24,16},{32,40},{40,32},{48,56},{56,48},{64,72... | collective-permute-start | bytes 6291464 | tf_op jit(solution)/shard_map/ppermute | solution.py:350
  19.7 29.0 %copy-start.7 = (s32[4]{0:T(128)}, s32[4]{0:T(128)S(1)}, u32[]{:S(2)}) copy-start(s32[4]{0:T(128)S(1)} %pad_add_fusion.place_ref) | copy-start | bytes 52
  24.0 1.7 %copy-start = (bf16[16,256,256]{2,1,0:T(8,128)(2,1)S(1)}, bf16[16,256,256]{2,1,0:T(8,128)(2,1)}, u32[]{:S(2)}) copy-start(bf16[16,256,256]{2,1,0:T(8,128)(2,1)} %get-tuple-element.56) | copy-start | bytes 6291460
  28.4 9.3 %collective-permute-start.1 = (bf16[4,128,256]{2,1,0:T(8,128)(2,1)S(1)}, bf16[4,128,256]{2,1,0:T(8,128)(2,1)S(1)}, u32[]{:S(2)}, u32[]{:S(2)}) collective-permute-start(bf16[4,128,256]{2,1,0:T(8,128)(2,1)S(1)} %get-tuple-element.59), channel_id=1, source_target_pairs={{0,64},{8,72},{16,80},{24,88},{32,96},{40,104},{48,112},{56,120},{... | collective-permute-start | bytes 786440 | tf_op jit(solution)/shard_map/ppermute | solution.py:469
  29.9 14.4 %collective-permute-start.2 = (bf16[4,128,256]{2,1,0:T(8,128)(2,1)}, bf16[4,128,256]{2,1,0:T(8,128)(2,1)S(1)}, u32[]{:S(2)}, u32[]{:S(2)}) collective-permute-start(bf16[4,128,256]{2,1,0:T(8,128)(2,1)} %get-tuple-element.60), channel_id=1, source_target_pairs={{0,128},{8,136},{16,144},{24,152},{32,160},{40,168},{48,176},{56,1... | collective-permute-start | bytes 786440 | tf_op jit(solution)/shard_map/ppermute | solution.py:469
  32.6 12.6 %collective-permute-start.3 = (bf16[4,128,256]{2,1,0:T(8,128)(2,1)S(1)}, bf16[4,128,256]{2,1,0:T(8,128)(2,1)S(1)}, u32[]{:S(2)}, u32[]{:S(2)}) collective-permute-start(bf16[4,128,256]{2,1,0:T(8,128)(2,1)S(1)} %get-tuple-element.61), channel_id=1, source_target_pairs={{0,192},{8,200},{16,208},{24,216},{32,224},{40,232},{48,240},{56,2... | collective-permute-start | bytes 786440 | tf_op jit(solution)/shard_map/ppermute | solution.py:469
  33.1 12.2 %collective-permute-start.4 = (bf16[4,128,256]{2,1,0:T(8,128)(2,1)S(1)}, bf16[4,128,256]{2,1,0:T(8,128)(2,1)S(1)}, u32[]{:S(2)}, u32[]{:S(2)}) collective-permute-start(bf16[4,128,256]{2,1,0:T(8,128)(2,1)S(1)} %get-tuple-element.63), channel_id=1, source_target_pairs={{0,16},{8,24},{16,32},{24,40},{32,48},{40,56},{48,0},{56,8},{64,80... | collective-permute-start | bytes 786440 | tf_op jit(solution)/shard_map/ppermute | solution.py:469
  34.7 14.0 %collective-permute-start.5 = (bf16[4,128,256]{2,1,0:T(8,128)(2,1)S(1)}, bf16[4,128,256]{2,1,0:T(8,128)(2,1)S(1)}, u32[]{:S(2)}, u32[]{:S(2)}) collective-permute-start(bf16[4,128,256]{2,1,0:T(8,128)(2,1)S(1)} %get-tuple-element.64), channel_id=1, source_target_pairs={{0,32},{8,40},{16,48},{24,56},{32,0},{40,8},{48,16},{56,24},{64,96... | collective-permute-start | bytes 786440 | tf_op jit(solution)/shard_map/ppermute | solution.py:469
  37.7 11.0 %collective-permute-start.6 = (bf16[4,128,256]{2,1,0:T(8,128)(2,1)S(1)}, bf16[4,128,256]{2,1,0:T(8,128)(2,1)S(1)}, u32[]{:S(2)}, u32[]{:S(2)}) collective-permute-start(bf16[4,128,256]{2,1,0:T(8,128)(2,1)S(1)} %get-tuple-element.65), channel_id=1, source_target_pairs={{0,48},{8,56},{16,0},{24,8},{32,16},{40,24},{48,32},{56,40},{64,11... | collective-permute-start | bytes 786440 | tf_op jit(solution)/shard_map/ppermute | solution.py:469
  60.5 4.6 %copy-start.9 = (bf16[8,256,512]{2,1,0:T(8,128)(2,1)}, bf16[8,256,512]{2,1,0:T(8,128)(2,1)S(1)}, u32[]{:S(2)}) copy-start(bf16[8,256,512]{2,1,0:T(8,128)(2,1)S(1)} %slice.9.mine_ref) | copy-start | bytes 6291460
  60.5 4.6 %collective-permute-start.7 = (bf16[8,256,512]{2,1,0:T(8,128)(2,1)S(1)}, bf16[8,256,512]{2,1,0:T(8,128)(2,1)}, u32[]{:S(2)}, u32[]{:S(2)}) collective-permute-start(bf16[8,256,512]{2,1,0:T(8,128)(2,1)S(1)} %slice.9.mine_ref), channel_id=1, source_target_pairs={{0,8},{8,0},{16,24},{24,16},{32,40},{40,32},{48,56},{56,48},{64,72... | collective-permute-start | bytes 6291464 | tf_op jit(solution)/shard_map/ppermute | solution.py:350
  73.1 22.8 %all-to-all-start = ((bf16[8,272,128]{2,1,0:T(8,128)(2,1)}), bf16[8,272,128]{2,1,0:T(8,128)(2,1)S(1)}, u32[]{:S(2)}, u32[]{:S(2)}) async-start(bf16[8,272,128]{2,1,0:T(8,128)(2,1)} %get-tuple-element.85), calls=%async_computation | async-start | bytes 1114112 | tf_op jit(solution)/shard_map/all_to_all | solution.py:426
  77.4 7.7 %collective-permute-start.10 = (f32[128,256]{1,0:T(8,128)S(1)}, f32[128,256]{1,0:T(8,128)S(1)}, u32[]{:S(2)}, u32[]{:S(2)}) collective-permute-start(f32[128,256]{1,0:T(8,128)S(1)} %get-tuple-element.89), channel_id=1, source_target_pairs={{0,48},{8,56},{16,0},{24,8},{32,16},{40,24},{48,32},{56,40},{64,11... | collective-permute-start | bytes 393224 | tf_op jit(solution)/shard_map/ppermute | solution.py:469
  80.2 11.7 %collective-permute-start.8 = (f32[128,256]{1,0:T(8,128)S(1)}, f32[128,256]{1,0:T(8,128)S(1)}, u32[]{:S(2)}, u32[]{:S(2)}) collective-permute-start(f32[128,256]{1,0:T(8,128)S(1)} %get-tuple-element.87), channel_id=1, source_target_pairs={{0,16},{8,24},{16,32},{24,40},{32,48},{40,56},{48,0},{56,8},{64,80... | collective-permute-start | bytes 393224 | tf_op jit(solution)/shard_map/ppermute | solution.py:469
  80.2 11.7 %collective-permute-start.9 = (f32[128,256]{1,0:T(8,128)S(1)}, f32[128,256]{1,0:T(8,128)S(1)}, u32[]{:S(2)}, u32[]{:S(2)}) collective-permute-start(f32[128,256]{1,0:T(8,128)S(1)} %get-tuple-element.88), channel_id=1, source_target_pairs={{0,32},{8,40},{16,48},{24,56},{32,0},{40,8},{48,16},{56,24},{64,96... | collective-permute-start | bytes 393224 | tf_op jit(solution)/shard_map/ppermute | solution.py:469
  82.5 9.4 %collective-permute-start.11 = (f32[128,256]{1,0:T(8,128)S(1)}, f32[128,256]{1,0:T(8,128)S(1)}, u32[]{:S(2)}, u32[]{:S(2)}) collective-permute-start(f32[128,256]{1,0:T(8,128)S(1)} %get-tuple-element.94), channel_id=1, source_target_pairs={{0,64},{8,72},{16,80},{24,88},{32,96},{40,104},{48,112},{56,120},{... | collective-permute-start | bytes 393224 | tf_op jit(solution)/shard_map/ppermute | solution.py:469
  83.9 7.9 %collective-permute-start.12 = (f32[128,256]{1,0:T(8,128)S(1)}, f32[128,256]{1,0:T(8,128)S(1)}, u32[]{:S(2)}, u32[]{:S(2)}) collective-permute-start(f32[128,256]{1,0:T(8,128)S(1)} %get-tuple-element.95), channel_id=1, source_target_pairs={{0,128},{8,136},{16,144},{24,152},{32,160},{40,168},{48,176},{56,1... | collective-permute-start | bytes 393224 | tf_op jit(solution)/shard_map/ppermute | solution.py:469
  85.1 6.8 %collective-permute-start.13 = (f32[128,256]{1,0:T(8,128)S(1)}, f32[128,256]{1,0:T(8,128)S(1)}, u32[]{:S(2)}, u32[]{:S(2)}) collective-permute-start(f32[128,256]{1,0:T(8,128)S(1)} %get-tuple-element.96), channel_id=1, source_target_pairs={{0,192},{8,200},{16,208},{24,216},{32,224},{40,232},{48,240},{56,2... | collective-permute-start | bytes 393224 | tf_op jit(solution)/shard_map/ppermute | solution.py:469
  87.2 22.6 %copy-start.1 = (bf16[1,512,256]{2,1,0:T(8,128)(2,1)S(1)}, bf16[1,512,256]{2,1,0:T(8,128)(2,1)}, u32[]{:S(2)}) copy-start(bf16[1,512,256]{2,1,0:T(8,128)(2,1)} %param.10) | copy-start | bytes 786436
  87.2 22.6 %copy-start.2 = (bf16[1,512,128]{2,1,0:T(8,128)(2,1)S(1)}, bf16[1,512,128]{2,1,0:T(8,128)(2,1)}, u32[]{:S(2)}) copy-start(bf16[1,512,128]{2,1,0:T(8,128)(2,1)} %param.11) | copy-start | bytes 393220
  87.2 22.6 %copy-start.3 = (f32[512,128]{1,0:T(8,128)S(1)}, f32[512,128]{1,0:T(8,128)}, u32[]{:S(2)}) copy-start(f32[512,128]{1,0:T(8,128)} %get-tuple-element.75.aux_ref) | copy-start | bytes 786436
  87.2 22.6 %copy-start.6 = (f32[8,16,128]{2,1,0:T(8,128)S(1)}, f32[8,16,128]{2,1,0:T(8,128)}, u32[]{:S(2)}) copy-start(f32[8,16,128]{2,1,0:T(8,128)} %get-tuple-element.98.decay_ref) | copy-start | bytes 196612
  87.2 22.6 %copy-start.8 = (s32[4]{0:T(128)S(1)}, s32[4]{0:T(128)}, u32[]{:S(2)}) copy-start(s32[4]{0:T(128)} %copy-done.7) | copy-start | bytes 52
  91.8 18.0 %copy-start.4 = (f32[512,256]{1,0:T(8,128)S(1)}, f32[512,256]{1,0:T(8,128)}, u32[]{:S(2)}) copy-start(f32[512,256]{1,0:T(8,128)} %get-tuple-element.83.gi_ref) | copy-start | bytes 1572868
  96.0 1.2 collective-permute-start.14
  97.2 8.4 %collective-permute-start.15 = (f32[2,128]{1,0:T(2,128)S(1)}, f32[2,128]{1,0:T(2,128)S(1)}, u32[]{:S(2)}, u32[]{:S(2)}) collective-permute-start(f32[2,128]{1,0:T(2,128)S(1)} %add.32), channel_id=1, source_target_pairs={{0,32},{8,40},{16,48},{24,56},{32,0},{40,8},{48,16},{56,24},{64,96... | collective-permute-start | bytes 3080 | tf_op jit(solution)/shard_map/ppermute | solution.py:473
  100.2 5.4 %collective-permute-start.16 = (f32[2,128]{1,0:T(2,128)S(1)}, f32[2,128]{1,0:T(2,128)S(1)}, u32[]{:S(2)}, u32[]{:S(2)}) collective-permute-start(f32[2,128]{1,0:T(2,128)S(1)} %add.32), channel_id=1, source_target_pairs={{0,16},{8,24},{16,0},{24,8},{32,48},{40,56},{48,32},{56,40},{64,80... | collective-permute-start | bytes 3080 | tf_op jit(solution)/shard_map/ppermute | solution.py:473
  100.8 4.8 %collective-permute-start.17 = (f32[2,128]{1,0:T(2,128)S(1)}, f32[2,128]{1,0:T(2,128)S(1)}, u32[]{:S(2)}, u32[]{:S(2)}) collective-permute-start(f32[2,128]{1,0:T(2,128)S(1)} %add.32), channel_id=1, source_target_pairs={{0,48},{8,56},{16,32},{24,40},{32,16},{40,24},{48,0},{56,8},{64,11... | collective-permute-start | bytes 3080 | tf_op jit(solution)/shard_map/ppermute | solution.py:473
  101.4 15.9 %all-to-all-start.1 = ((f32[8,32,256]{2,1,0:T(8,128)}), f32[8,32,256]{2,1,0:T(8,128)S(1)}, u32[]{:S(2)}, u32[]{:S(2)}) async-start(f32[8,32,256]{2,1,0:T(8,128)} %shard_map.128), calls=%async_computation.1 | async-start | bytes 524288 | tf_op jit(solution)/shard_map/all_to_all | solution.py:434
  105.6 6.9 %collective-permute-start.18 = (f32[2,128]{1,0:T(2,128)S(1)}, f32[2,128]{1,0:T(2,128)S(1)}, u32[]{:S(2)}, u32[]{:S(2)}) collective-permute-start(f32[2,128]{1,0:T(2,128)S(1)} %add_add_fusion.1), channel_id=1, source_target_pairs={{0,128},{8,136},{16,144},{24,152},{32,160},{40,168},{48,176},{56,1... | collective-permute-start | bytes 3080 | tf_op jit(solution)/shard_map/ppermute | solution.py:473
  107.7 4.8 %collective-permute-start.19 = (f32[2,128]{1,0:T(2,128)S(1)}, f32[2,128]{1,0:T(2,128)S(1)}, u32[]{:S(2)}, u32[]{:S(2)}) collective-permute-start(f32[2,128]{1,0:T(2,128)S(1)} %add_add_fusion.1), channel_id=1, source_target_pairs={{0,64},{8,72},{16,80},{24,88},{32,96},{40,104},{48,112},{56,120},{... | collective-permute-start | bytes 3080 | tf_op jit(solution)/shard_map/ppermute | solution.py:473
  109.1 3.6 %collective-permute-start.20 = (f32[2,128]{1,0:T(2,128)S(1)}, f32[2,128]{1,0:T(2,128)S(1)}, u32[]{:S(2)}, u32[]{:S(2)}) collective-permute-start(f32[2,128]{1,0:T(2,128)S(1)} %add_add_fusion.1), channel_id=1, source_target_pairs={{0,192},{8,200},{16,208},{24,216},{32,224},{40,232},{48,240},{56,2... | collective-permute-start | bytes 3080 | tf_op jit(solution)/shard_map/ppermute | solution.py:473
  109.8 1.0 copy-start.5
Sparse Core Ops, SparseCore 0:
  10.2 48.5 all-gather.2
